TPU v7x, 32 devices: a whole 2x2x4 slice. The times are simulated.
32 devices in a mesh: comp: 4 (over y, core), gx: 2 (over x), gy: 4 (over z).
Axes of the slice: x: 2, y: 2, z: 4, core: 2. Of those that a mesh axis runs over, the one named last changes fastest.
Arguments:
- field: float32 [4, 256, 64, 256], P('comp', 'gx', 'gy'), may hold values from -6 to 6
- third_level: int32 [4], replicated, may hold values from 2 to 6
- coefficients: int32 [4], replicated, may hold values from -3 to 3, as said below
- rates: float32 [2, 4], replicated, may hold values from 0.01 to 0.4, as said below
- reaction: float32 [1], replicated, may hold values from 0.1 to 0.3
Outputs:
- result: float32 [4, 256, 64, 256], P('comp', 'gx', 'gy')
Inputs may be any that keep to these rules, and one draw needn't show every extreme that they name: The fourth dimension of grid g has level 8 minus third_level[g]. `coefficients`: every weight is a nonzero integer; some are positive and some negative. `rates`: courant numbers of the first two dimensions lie from 0.3 to 0.4, all other entries from 0.01 to 0.02.
All inputs are finite; a program needn't handle non-finite values.
Results may differ from a plain program's by a relative error of at most 0.0003.
Values sent between devices are 32-bit elements; how exact they have to be, the bound alone decides.
No kernel may reach another device: no remote copies, remote signals or barrier semaphores. Data moves between devices by JAX's collectives and lax.ppermute only.
A program may use at most 128 MiB of HBM per device.

v0:
```python
import jax
import jax.numpy as jnp
from jax import lax
from jax.experimental import pallas as pl
from jax.experimental.pallas import tpu as pltpu
from jax.sharding import PartitionSpec as P


SECTIONS = 4
LEVEL_SUM = 8
TOP = LEVEL_SUM - 2
FINE = 2**TOP
LANES = 128
F32 = jnp.float32
BF16 = jnp.bfloat16
SMEM = pl.BlockSpec(memory_space=pltpu.SMEM)
VMEM = pl.BlockSpec(memory_space=pltpu.VMEM)
ANY = pl.BlockSpec(memory_space=pl.ANY)


def points(level):
    return 1 if level == 0 else 2 ** (level - 1)


def ring(count, step):
    return [(i, (i + step) % count) for i in range(count)]


def split(values):
    head = values.astype(BF16)
    tail = (values - head.astype(F32)).astype(BF16)
    return head, tail


def dot(left, right):
    return jnp.dot(left, right, preferred_element_type=F32)


def staircase(ones, others):
    betas = []
    for k3 in range(TOP + 1):
        beta = jnp.int32(-1)
        for one in ones:
            for other in others:
                third = jnp.minimum(one, other)
                fourth = LEVEL_SUM - jnp.maximum(one, other)
                beta = jnp.maximum(beta, jnp.where(third >= k3, fourth, -1))
        betas.append(beta)
    return betas


def stair_counts(betas):
    return [
        jnp.where(beta >= 0, points(k3) * jnp.left_shift(jnp.int32(1), jnp.maximum(beta, 0)), 0)
        for k3, beta in enumerate(betas)
    ]


def slot_places(row, betas):
    total = jnp.int32(0)
    k3 = jnp.full_like(row, -1)
    start = jnp.zeros_like(row)
    beta_row = jnp.zeros_like(row)
    for k, (beta, count) in enumerate(zip(betas, stair_counts(betas))):
        past = row >= total
        k3 = jnp.where(past, k, k3)
        start = jnp.where(past, total, start)
        beta_row = jnp.where(past, jnp.maximum(beta, 0), beta_row)
        total = total + count
    used = row < total
    inside = row - start
    fourth = jnp.bitwise_and(inside, jnp.left_shift(jnp.ones_like(row), beta_row) - 1)
    rank = jnp.right_shift(inside, beta_row)
    place3 = jnp.where(k3 == 0, 0, jnp.left_shift(2 * rank + 1, jnp.maximum(TOP - k3, 0)))
    place4 = jnp.left_shift(fourth, jnp.maximum(TOP - beta_row, 0))
    return place3, place4, used


def cell_places(index, level_a):
    level_b = LEVEL_SUM - level_a
    third = jnp.right_shift(index, level_b)
    fourth = jnp.bitwise_and(index, jnp.left_shift(jnp.int32(1), level_b) - 1)
    return jnp.left_shift(third, TOP - level_a), jnp.left_shift(fourth, TOP - level_b)


def held(place3, place4, level_a):
    low3 = jnp.left_shift(jnp.int32(1), TOP - level_a) - 1
    low4 = jnp.left_shift(jnp.int32(1), TOP - (LEVEL_SUM - level_a)) - 1
    return jnp.logical_and(jnp.bitwise_and(place3, low3) == 0, jnp.bitwise_and(place4, low4) == 0)


def surplus_weight(cell, slot):
    half = jnp.bitwise_and(slot, -slot)
    side = jnp.where(slot == 0, 0.0, -0.5)
    weight = jnp.where(cell == slot, 1.0, 0.0)
    weight = weight + jnp.where(cell == slot - half, side, 0.0)
    return weight + jnp.where(cell == jnp.bitwise_and(slot + half, FINE - 1), side, 0.0)


def hat_weight(cell, slot):
    half = jnp.bitwise_and(slot, -slot)
    reach = jnp.maximum(half - jnp.abs(cell - slot), 0).astype(F32)
    return jnp.where(slot == 0, 1.0, reach / jnp.maximum(half, 1).astype(F32))


def linear_weight(cell, node, low_a, low_b):
    coarse = jnp.left_shift(jnp.int32(1), TOP - jnp.minimum(low_a, low_b))
    gap = jnp.bitwise_and(cell - node, FINE - 1)
    gap = jnp.minimum(gap, FINE - gap)
    reach = jnp.maximum(coarse - gap, 0).astype(F32)
    scale = jnp.float32(1.0)
    for k in range(TOP):
        scale = scale * jnp.where(TOP - jnp.minimum(low_a, low_b) > k, 0.5, 1.0)
    return jnp.where(jnp.bitwise_and(node, coarse - 1) == 0, reach * scale, 0.0)


def grid_numbers(rates, level_a):
    level_b = LEVEL_SUM - level_a
    third = jnp.float32(1.0)
    fourth = jnp.float32(1.0)
    for k in range(TOP):
        third = third * jnp.where(TOP - level_a > k, 0.5, 1.0)
        fourth = fourth * jnp.where(TOP - level_b > k, 0.5, 1.0)
    dif = [rates[0], rates[1], rates[2] * (third * third), rates[3] * (fourth * fourth)]
    cou = [rates[4], rates[5], rates[6] * third, rates[7] * fourth]
    return dif, cou


def setup_kernel(flat, chips, place, levels, weights, rates, *outs):
    head_out, tail_out, partner_out = outs[:3]
    mine = place[0]
    other = mine + 1 - 2 * jnp.bitwise_and(mine, 1)
    chip = jnp.right_shift(mine, 1)
    level = levels[mine]
    level_other = levels[other]
    weight = weights[mine].astype(F32)
    weight_other = weights[other].astype(F32)
    rows = lax.broadcasted_iota(jnp.int32, (flat, flat), 0)
    columns = lax.broadcasted_iota(jnp.int32, (flat, flat), 1)
    dif, cou = grid_numbers(rates, level)
    width = jnp.left_shift(jnp.int32(1), LEVEL_SUM - level)
    row4 = jnp.bitwise_and(rows, width - 1)
    column4 = jnp.bitwise_and(columns, width - 1)
    same3 = (rows - row4) == (columns - column4)
    step = jnp.where(jnp.bitwise_and(columns + width, flat - 1) == rows, dif[2], 0.0)
    step = step + jnp.where(jnp.bitwise_and(columns - width, flat - 1) == rows, dif[2] + cou[2], 0.0)
    up4 = jnp.logical_and(same3, jnp.bitwise_and(column4 + 1, width - 1) == row4)
    down4 = jnp.logical_and(same3, jnp.bitwise_and(column4 - 1, width - 1) == row4)
    step = step + jnp.where(up4, dif[3], 0.0)
    step = step + jnp.where(down4, dif[3] + cou[3], 0.0)
    head, tail = split(step)
    head_out[...] = head
    tail_out[...] = tail

    node3, node4 = cell_places(rows, level_other)
    cell3, cell4 = cell_places(columns, level)
    linear = linear_weight(cell3, node3, level, level_other)
    linear = linear * linear_weight(cell4, node4, LEVEL_SUM - level, LEVEL_SUM - level_other)
    partner_out[...] = (linear * weight_other).astype(BF16)

    slots = 2 * flat
    for shift in range(1, chips):
        own_out, other_out, back_out = outs[3 * shift : 3 * shift + 3]
        target = lax.rem(chip + shift, jnp.int32(chips))
        source = lax.rem(chip + chips - shift, jnp.int32(chips))
        betas = staircase((level, level_other), (levels[2 * target], levels[2 * target + 1]))
        row = lax.broadcasted_iota(jnp.int32, (1, slots), 1)
        cell = lax.broadcasted_iota(jnp.int32, (flat, 1), 0)
        place3, place4, used = slot_places(row, betas)
        for out, grid_level, grid_weight in (
            (own_out, level, weight),
            (other_out, level_other, weight_other),
        ):
            kept = jnp.where(
                jnp.logical_and(used, held(place3, place4, grid_level)), grid_weight, 0.0
            )
            cell3, cell4 = cell_places(cell, grid_level)
            value = surplus_weight(cell3, place3) * surplus_weight(cell4, place4) * kept
            out[...] = value.astype(BF16)
        betas = staircase((level, level_other), (levels[2 * source], levels[2 * source + 1]))
        row = lax.broadcasted_iota(jnp.int32, (slots, 1), 0)
        cell = lax.broadcasted_iota(jnp.int32, (1, flat), 1)
        place3, place4, used = slot_places(row, betas)
        kept = jnp.where(jnp.logical_and(used, held(place3, place4, level)), 1.0, 0.0)
        cell3, cell4 = cell_places(cell, level)
        value = hat_weight(cell3, place3) * hat_weight(cell4, place4) * kept
        back_out[...] = value.astype(BF16)


def setup_tables(flat, chips, place, levels, weights, rates):
    shapes = [jax.ShapeDtypeStruct((flat, flat), BF16)] * 3
    for _ in range(1, chips):
        shapes += [jax.ShapeDtypeStruct((flat, 2 * flat), BF16)] * 2
        shapes += [jax.ShapeDtypeStruct((2 * flat, flat), BF16)]
    return pl.pallas_call(
        lambda *refs: setup_kernel(flat, chips, *refs),
        out_shape=shapes,
        in_specs=[SMEM] * 4,
        out_specs=[VMEM] * len(shapes),
        name="tables",
    )(place, levels, weights, rates.reshape(-1))


def stencil_kernel(plan, keep, place, levels, rates, reaction, field, *refs):
    sides = refs[: plan["sides"]]
    head_ref, tail_ref, out, first, second, sem = refs[plan["sides"] :]
    halo = SECTIONS
    own = field.shape[1]
    tall = own + 2 * halo
    flat = field.shape[2]
    copies = []
    for source, start, target, count in plan["own"]:
        if source is None:
            copies.append(
                pltpu.make_async_copy(
                    field.at[pl.ds(start, count)],
                    first.at[pl.ds(target, count), pl.ds(0, own)],
                    sem.at[len(copies)],
                )
            )
            copies[-1].start()
    for source, start, target, count in plan["own"]:
        if source is not None:
            first[target : target + count, :own] = sides[source][start : start + count]
    for low, high, start, target, count in plan["edge"]:
        first[target : target + count, own : own + halo] = sides[high][start : start + count]
        first[target : target + count, own + halo :] = sides[low][start : start + count]
    level = levels[place[0]]
    dif, cou = grid_numbers(rates, level)
    centre_weight = 1.0 - 2.0 * (dif[0] + dif[1] + dif[2] + dif[3])
    centre_weight = centre_weight - (cou[0] + cou[1] + cou[2] + cou[3])
    rate = reaction[0]
    for copy in copies:
        copy.wait()

    def block(source, at, depth, step):
        centre = source[pl.ds(at, step)]
        above = source[pl.ds(at + 1, step), :depth]
        below = source[pl.ds(at - 1, step), :depth]
        ahead = jnp.roll(centre, -1, axis=1)[:, :depth]
        behind = jnp.roll(centre, 1, axis=1)[:, :depth]
        centre = centre[:, :depth]
        flatter = centre.reshape(step * depth, flat)
        head, tail = split(flatter)
        inner = dot(head, head_ref[...]) + dot(tail, head_ref[...]) + dot(head, tail_ref[...])
        value = centre * (centre_weight + rate / (1.0 + centre * centre))
        value = value + dif[0] * above + (dif[0] + cou[0]) * below
        value = value + dif[1] * ahead + (dif[1] + cou[1]) * behind
        return value + inner.reshape(step, depth, flat)

    step = plan["step"]
    source, target = first, second
    for section in range(1, SECTIONS):
        blocks = -(-(plan["rows"] - 2 * section) // step)

        def body(i, carry, source=source, target=target, section=section):
            at = section + i * step
            target[pl.ds(at, step)] = block(source, at, tall, step)
            return carry

        lax.fori_loop(0, blocks, body, 0)
        source, target = target, source
    done = 0
    step = plan["last"]
    for start, count in keep:

        def last(i, carry, start=start, done=done):
            out[pl.ds(done + i * step, step)] = block(source, start + i * step, own, step)
            return carry

        lax.fori_loop(0, count // step, last, 0)
        done = done + count


def stencil(plan, keep, place, levels, rates, reaction, field, sides, head, tail):
    halo = SECTIONS
    rows = plan["rows"] + 2 * plan["step"]
    tall = field.shape[1] + 2 * halo
    scratch = pltpu.VMEM((rows, tall, field.shape[2]), F32)
    count = sum(n for _, n in keep)
    return pl.pallas_call(
        lambda *refs: stencil_kernel(plan, keep, *refs),
        out_shape=jax.ShapeDtypeStruct((count,) + field.shape[1:], F32),
        in_specs=[SMEM] * 4 + [ANY] + [VMEM] * (len(sides) + 2),
        out_specs=VMEM,
        scratch_shapes=[
            scratch,
            scratch,
            pltpu.SemaphoreType.DMA((len(plan["own"]),)),
        ],
        name="sections",
    )(place, levels, rates.reshape(-1), reaction, field, *sides, head, tail)


def pack(cap, core, values, others, tables):
    count, own, flat = values.shape
    half = count // 2

    def kernel(core, mine, other, *refs):
        parts = len(tables)
        head, tail = split(mine[...].reshape(half * own, flat))
        other_head, other_tail = split(other[...].reshape(half * own, flat))
        for shift in range(parts):
            own_table = refs[2 * shift][...]
            other_table = refs[2 * shift + 1][...]
            out = refs[2 * parts + shift]
            out[...] = (
                dot(head, own_table)
                + dot(tail, own_table)
                + dot(other_head, other_table)
                + dot(other_tail, other_table)
            )

    block = pl.BlockSpec((half, own, flat), lambda i, core: (core[0], 0, 0))
    table = pl.BlockSpec((flat, cap), lambda i, core: (0, 0))
    out = pl.BlockSpec((half * own, cap), lambda i, core: (0, 0))
    return pl.pallas_call(
        kernel,
        out_shape=[jax.ShapeDtypeStruct((half * own, cap), F32)] * len(tables),
        grid_spec=pltpu.PrefetchScalarGridSpec(
            num_scalar_prefetch=1,
            grid=(1,),
            in_specs=[block, block] + [table] * (2 * len(tables)),
            out_specs=[out] * len(tables),
        ),
        name="pack",
    )(core, values, others, *[t for pair in tables for t in pair])


def finish(cap, at, core, weight, values, others, partner, near, far, backs, carry, shape):
    count, own, flat = values.shape
    half = count // 2
    parts = len(backs)
    quarters = shape[0] // half

    def kernel(core, weight, mine, other, partner, *refs):
        out = refs[-1]
        centre = mine[...].reshape(half * own, flat)
        head, tail = split(other[...].reshape(half * own, flat))
        total = weight[0] * centre + dot(head, partner[...]) + dot(tail, partner[...])

        def ended(received):
            value = total
            for shift in range(parts):
                head, tail = split(received[shift][...])
                back = refs[2 * parts + shift][...]
                value = value + dot(head, back) + dot(tail, back)
            out[...] = value.reshape(half, own, flat)

        @pl.when(pl.program_id(0) == 0)
        def _():
            ended(refs[:parts])

        @pl.when(pl.program_id(0) == 1)
        def _():
            ended(refs[parts : 2 * parts])

    def which(i, core):
        return lax.rem(core[0] + i, 2)

    block = pl.BlockSpec((half, own, flat), lambda i, core: (which(i, core), 0, 0))
    whole = pl.BlockSpec((flat, flat), lambda i, core: (0, 0))
    message = pl.BlockSpec((half * own, cap), lambda i, core: (0, 0))
    back = pl.BlockSpec((cap, flat), lambda i, core: (0, 0))
    out = pl.BlockSpec(
        (half, own, flat), lambda i, core: (lax.rem(at + which(i, core), quarters), 0, 0)
    )
    operands = [core, weight, values, others, partner, *near, *far, *backs]
    specs = [SMEM, block, block, whole] + [message] * (2 * parts) + [back] * parts
    aliases = {}
    if carry is not None:
        aliases = {len(operands): 0}
        operands.append(carry)
        specs.append(ANY)
    return pl.pallas_call(
        kernel,
        out_shape=jax.ShapeDtypeStruct(shape, F32),
        grid_spec=pltpu.PrefetchScalarGridSpec(
            num_scalar_prefetch=1, grid=(2,), in_specs=specs, out_specs=out
        ),
        input_output_aliases=aliases,
        name="finish",
    )(*operands)


def slots_needed(third_level, chips):
    levels = third_level.reshape(chips, 2)
    most = jnp.int32(0)
    for shift in range(1, chips):
        shifted = jnp.roll(levels, -shift, axis=0)
        betas = staircase(
            (levels[:, 0], levels[:, 1]), (shifted[:, 0], shifted[:, 1])
        )
        most = jnp.maximum(most, jnp.max(sum(stair_counts(betas))))
    return most


def local(sizes, field, third_level, coefficients, rates, reaction):
    block = field[0]
    long, own, flat = block.shape
    halo = SECTIONS
    chips = sizes["comp"] // 2
    mine = lax.axis_index("comp")
    place = mine.reshape(1).astype(jnp.int32)
    core = jnp.bitwise_and(place, 1)
    weight = lax.dynamic_index_in_dim(coefficients, mine, 0, True).astype(F32)
    swap = [(i, i ^ 1) for i in range(sizes["comp"])]
    forward = {axis: ring(sizes[axis], 1) for axis in ("gx", "gy")}
    backward = {axis: ring(sizes[axis], -1) for axis in ("gx", "gy")}

    quarter = long // 4
    left = quarter - halo
    right = long - left
    low_one = lax.ppermute(block[left:right, own - halo :], "gy", forward["gy"])
    high_one = lax.ppermute(block[left:right, :halo], "gy", backward["gy"])
    before = lax.ppermute(block[long - halo :], "gx", forward["gx"])
    after = lax.ppermute(block[:halo], "gx", backward["gx"])

    def outer(rows):
        return jnp.concatenate([before[:, rows], block[:left, rows], block[right:, rows], after[:, rows]])

    top, bottom = outer(slice(own - halo, own)), outer(slice(0, halo))
    low_two = lax.ppermute(top, "gy", forward["gy"])
    high_two = lax.ppermute(bottom, "gy", backward["gy"])
    branch = lax.div(slots_needed(third_level, chips) - 1, jnp.int32(LANES))

    tables = setup_tables(flat, chips, place, third_level, coefficients, rates)
    head, tail, partner = tables[:3]
    pairs = [(tables[3 * r], tables[3 * r + 1]) for r in range(1, chips)]
    backs = [tables[3 * r + 2] for r in range(1, chips)]

    middle = right - left
    plan_one = {
        "rows": middle,
        "step": -(-middle // 4),
        "last": quarter // 2,
        "sides": 2,
        "own": [(None, left, 0, middle)],
        "edge": [(0, 1, 0, 0, middle)],
    }
    piece = quarter + 2 * halo
    plan_two = {
        "rows": 2 * piece,
        "step": piece // 2,
        "last": quarter // 2,
        "sides": 6,
        "own": [
            (None, long - quarter - halo, 0, quarter + halo),
            (5, 0, quarter + halo, halo),
            (4, 0, piece, halo),
            (None, 0, piece + halo, quarter + halo),
        ],
        "edge": [
            (0, 1, middle - 2 * halo, 0, 2 * halo),
            (2, 3, halo + left, 2 * halo, left + halo),
            (2, 3, 0, piece, halo + left),
            (0, 1, 0, piece + halo + left, 2 * halo),
        ],
    }
    keep_one = [(halo, 2 * quarter)]
    keep_two = [(halo, quarter), (piece + halo, quarter)]

    ready = lax.optimization_barrier((place, branch, top, bottom, partner))[0]
    scalars = (third_level, rates, reaction, block)
    one = stencil(plan_one, keep_one, ready, *scalars, [low_one, high_one], head, tail)
    one_other = lax.ppermute(one, "comp", swap)

    def hop(cap, values, others):
        sent = pack(cap, core, values, others, pairs)
        shifts = [
            [(2 * h + c, 2 * ((h + r) % chips) + c) for h in range(chips) for c in range(2)]
            for r in range(1, chips)
        ]
        received = []
        for message, pairs_of in zip(sent, shifts):
            received.append(lax.ppermute(message, "comp", pairs_of))
        return sent[0], received

    def tail_of(cap):
        def run(one, one_other, low_two, high_two, before, after):
            sent, near_one = hop(cap, one, one_other)
            ready = lax.optimization_barrier((place, sent))[0]
            sides = [low_one, high_one, low_two, high_two, before, after]
            two = stencil(plan_two, keep_two, ready, *scalars, sides, head, tail)
            two_other = lax.ppermute(two, "comp", swap)
            _, near_two = hop(cap, two, two_other)
            far_one = [lax.ppermute(m, "comp", swap) for m in near_one]
            shape = block.shape
            result = finish(
                cap, 1, core, weight, one, one_other, partner, near_one, far_one, backs, None, shape
            )
            far_two = [lax.ppermute(m, "comp", swap) for m in near_two]
            return finish(
                cap, 3, core, weight, two, two_other, partner, near_two, far_two, backs, result, shape
            )

        return run

    caps = list(range(LANES, 2 * flat + 1, LANES))
    return lax.switch(
        branch, [tail_of(cap) for cap in caps], one, one_other, low_two, high_two, before, after
    )[None]


def solution(mesh):
    sizes = dict(mesh.shape)
    step = jax.shard_map(
        lambda *args: local(sizes, *args),
        mesh=mesh,
        in_specs=(P("comp", "gx", "gy", None), P(), P(), P(), P()),
        out_specs=P("comp", "gx", "gy", None),
        check_vma=False,
    )

    def run(field, third_level, coefficients, rates, reaction):
        placed = step
        return placed(field, third_level, coefficients, rates, reaction)

    return run
```

profile of v0, /device:TPU:0, one launch (start us, length us, event | category | flops | bytes accessed | tf_op | source)
XLA Modules:
  0.0 108.7 jit_solution(7008263972612978122)
XLA Ops:
  0.0 1.7 %slice_bitcast_fusion.1 = (f32[4,16,256]{2,1,0:T(8,128)}, f32[4,16,256]{2,1,0:T(8,128)S(1)}) fusion(f32[1,128,16,256]{3,2,1,0:T(8,128)} %param.9), kind=kLoop, calls=%fused_computation.3 | loop fusion | bytes 262144 | tf_op jit(solution)/shard_map/slice | solution.py:416
  1.7 3.0 %collective-permute-start.20 = (f32[4,16,256]{2,1,0:T(8,128)}, f32[4,16,256]{2,1,0:T(8,128)S(1)}, u32[]{:S(2)}, u32[]{:S(2)}) collective-permute-start(f32[4,16,256]{2,1,0:T(8,128)} %get-tuple-element.288), channel_id=1, source_target_pairs={{0,4},{4,0},{1,5},{5,1},{2,6},{6,2},{3,7},{7,3},{8,12},{12,8},{9,1... | collective-permute-start | bytes 196616 | tf_op jit(solution)/shard_map/ppermute | solution.py:416
  4.7 2.2 %fusion.35 = (f32[72,4,256]{2,1,0:T(4,128)}, f32[72,4,256]{2,1,0:T(4,128)}) fusion(f32[128,16,256]{2,1,0:T(8,128)} %bitcast.14), kind=kLoop, calls=%fused_computation.81 | loop fusion | bytes 1179648 | tf_op jit(solution)/shard_map/slice | solution.py:415
  6.8 4.1 %collective-permute-start.23 = (f32[72,4,256]{2,1,0:T(4,128)}, f32[72,4,256]{2,1,0:T(4,128)S(1)}, u32[]{:S(2)}, u32[]{:S(2)}) collective-permute-start(f32[72,4,256]{2,1,0:T(4,128)} %get-tuple-element.282), channel_id=1, source_target_pairs={{0,3},{1,0},{2,1},{3,2},{4,7},{5,4},{6,5},{7,6},{8,11},{9,8},{10,9... | collective-permute-start | bytes 884744 | tf_op jit(solution)/shard_map/ppermute | solution.py:415
  12.5 2.1 %fusion.36 = (f32[28,4,256]{2,1,0:T(4,128)}, f32[28,4,256]{2,1,0:T(4,128)}, f32[28,4,256]{2,1,0:T(4,128)S(1)}, f32[28,4,256]{2,1,0:T(4,128)S(1)}) fusion(f32[128,16,256]{2,1,0:T(8,128)} %bitcast.15), kind=kLoop, calls=%fused_computation.82 | loop fusion | bytes 917504 | tf_op jit(solution)/shard_map/slice | solution.py:420
  17.3 2.7 %tables.1 = (bf16[256,256]{1,0:T(8,128)(2,1)}, bf16[256,256]{1,0:T(8,128)(2,1)}, bf16[256,256]{1,0:T(8,128)(2,1)S(1)}, bf16[256,512]{1,0:T(8,128)(2,1)}, bf16[25...) custom-call(s32[1]{0:T(128)} %bitcast.6.refs_0_, s32[4]{0:T(128)S(1)} %copy-done.34, s32[4]{0:T(128)} %refs_2_.1, ...), custom_call_target="tpu_custom_call" | custom-call | tf_op jit(solution)/shard_map/tables/pallas_call | solution.py:195
  20.1 1.7 %pad_maximum_fusion.1 = f32[64,4,256]{2,1,0:T(4,128)} fusion(f32[4,4,256]{2,1,0:T(4,128)S(1)} %get-tuple-element.292, f32[28,4,256]{2,1,0:T(4,128)} %get-tuple-element.285, f32[28,4,256]{2,1,0:T(4,128)} %get-tuple-element.284, f32[4,4,256]{2,1,0:T(4,128)S(1)} %get-tuple-element.290), kind=kLoop, calls=%fused_computation.1 | loop fusion | flops 196608 | bytes 524288 | tf_op jit(solution)/shard_map/concatenate | solution.py:420
  22.6 1.5 %collective-permute-done.22.refs_5_ = f32[72,4,256]{2,1,0:T(4,128)S(1)} collective-permute-done((f32[72,4,256]{2,1,0:T(4,128)}, f32[72,4,256]{2,1,0:T(4,128)S(1)}, u32[]{:S(2)}, u32[]{:S(2)}) %collective-permute-start.22) | collective-permute-done | bytes 294944 | tf_op jit(solution)/shard_map/ppermute | solution.py:414
  24.8 8.1 %sections.9 = f32[64,16,256]{2,1,0:T(8,128)S(1)} custom-call(s32[1]{0:T(128)} %bitcast.6.refs_0_, s32[4]{0:T(128)S(1)} %copy-done.34, f32[8]{0:T(128)} %reshape.170.refs_3_.refs_2_, f32[1]{0:T(128)S(6)} %copy.22.refs_3_, f32[128,16,256]{2,1,0:T(8,128)S(1)} %bitcast.20, f32[72,4,256]{2,1,0:T(4,128)} %copy-done.14, f32[72,4,256]{2,1,0:T(4,128)} %copy-done.9, ...), custom_call_target="tpu_custom_call" | custom-call | tf_op jit(solution)/shard_map/sections/pallas_call | solution.py:281
  33.0 1.7 %collective-permute-start.25 = (f32[64,4,256]{2,1,0:T(4,128)}, f32[64,4,256]{2,1,0:T(4,128)}, u32[]{:S(2)}, u32[]{:S(2)}) collective-permute-start(f32[64,4,256]{2,1,0:T(4,128)} %pad_maximum_fusion), channel_id=1, source_target_pairs={{0,1},{1,2},{2,3},{3,0},{4,5},{5,6},{6,7},{7,4},{8,9},{9,10},{10,1... | collective-permute-start | bytes 786440 | tf_op jit(solution)/shard_map/ppermute | solution.py:423
  34.6 2.2 %collective-permute-start.26 = (f32[64,4,256]{2,1,0:T(4,128)}, f32[64,4,256]{2,1,0:T(4,128)}, u32[]{:S(2)}, u32[]{:S(2)}) collective-permute-start(f32[64,4,256]{2,1,0:T(4,128)} %pad_maximum_fusion.1), channel_id=1, source_target_pairs={{0,3},{1,0},{2,1},{3,2},{4,7},{5,4},{6,5},{7,6},{8,11},{9,8},{10,9... | collective-permute-start | bytes 786440 | tf_op jit(solution)/shard_map/ppermute | solution.py:424
  38.1 6.3 %collective-permute-done.25 = f32[64,4,256]{2,1,0:T(4,128)} collective-permute-done((f32[64,4,256]{2,1,0:T(4,128)}, f32[64,4,256]{2,1,0:T(4,128)}, u32[]{:S(2)}, u32[]{:S(2)}) %collective-permute-start.25) | collective-permute-done | bytes 262176 | tf_op jit(solution)/shard_map/ppermute | solution.py:423
  44.4 4.6 %collective-permute-done.26 = f32[64,4,256]{2,1,0:T(4,128)} collective-permute-done((f32[64,4,256]{2,1,0:T(4,128)}, f32[64,4,256]{2,1,0:T(4,128)}, u32[]{:S(2)}, u32[]{:S(2)}) %collective-permute-start.26) | collective-permute-done | bytes 262176 | tf_op jit(solution)/shard_map/ppermute | solution.py:424
  49.0 59.8 %conditional.1 = (f32[1,128,16,256]{3,2,1,0:T(8,128)}) conditional(s32[]{:T(128)} %clamp.3, (s32[1]{0:T(128)}, f32[64,16,256]{2,1,0:T(8,128)S(1)}, f32[64,16,256]{2,1,0:T(8,128)S(1)}, bf16[256,512]{1,0:T(8,128)(2,1)}, bf16[256,512]{1,0:T(8,128)(2,1)}, /*index=5*/f32[2,4]{1,0:T(2,128)S(1)}, s32[4]{0:T(128)S(1)}, ...), branch_computations={%region_1.2_spmd, %region_2.3_spmd, %region_3.4_spmd, %region_4.5_... | conditional | flops 1 | bytes 29229508 | solution.py:500
  49.6 2.6 %pack.12 = f32[512,384]{1,0:T(8,128)} custom-call(s32[1]{0:T(128)S(6)} %and.12.core, f32[64,16,256]{2,1,0:T(8,128)S(1)} %get-tuple-element.227.mine, f32[64,16,256]{2,1,0:T(8,128)S(1)} %get-tuple-element.228.other, bf16[256,512]{1,0:T(8,128)(2,1)} %get-tuple-element.229.refs_0_, bf16[256,512]{1,0:T(8,128)(2,1)} %get-tuple-element.230.refs_1_), custom_call_target="tpu_custom_call" | custom-call | tf_op jit(solution)/shard_map/cond/branch_2_fun/pack/pallas_call | solution.py:317
  52.2 11.3 %sections.7.mine = f32[64,16,256]{2,1,0:T(8,128)} custom-call(s32[1]{0:T(128)} %get-tuple-element.231.refs_0_, s32[4]{0:T(128)S(1)} %get-tuple-element.232.refs_1_, f32[8]{0:T(128)} %reshape.163.refs_2_, f32[1]{0:T(128)} %get-tuple-element.234.refs_3_, f32[128,16,256]{2,1,0:T(8,128)} %get-tuple-element.235.refs_4_, ...), custom_call_target="tpu_custom_call" | custom-call | tf_op jit(solution)/shard_map/cond/branch_2_fun/sections/pallas_call | solution.py:281
  63.6 1.6 %collective-permute-start.13 = (f32[512,384]{1,0:T(8,128)}, f32[512,384]{1,0:T(8,128)}, u32[]{:S(2)}, u32[]{:S(2)}) collective-permute-start(f32[512,384]{1,0:T(8,128)} %pack.12), channel_id=1, source_target_pairs={{0,16},{8,24},{16,0},{24,8},{1,17},{9,25},{17,1},{25,9},{2,18},{10... | collective-permute-start | bytes 2359304 | tf_op jit(solution)/shard_map/cond/branch_2_fun/ppermute | solution.py:476
  65.2 1.4 %collective-permute-done.10.other = f32[64,16,256]{2,1,0:T(8,128)} collective-permute-done((f32[64,16,256]{2,1,0:T(8,128)}, f32[64,16,256]{2,1,0:T(8,128)}, u32[]{:S(2)}, u32[]{:S(2)}) %collective-permute-start.10) | collective-permute-done | bytes 1048608 | tf_op jit(solution)/shard_map/cond/branch_2_fun/ppermute | solution.py:485
  66.6 2.8 %pack.13 = f32[512,384]{1,0:T(8,128)} custom-call(s32[1]{0:T(128)S(6)} %and.12.core, f32[64,16,256]{2,1,0:T(8,128)} %sections.7.mine, f32[64,16,256]{2,1,0:T(8,128)} %collective-permute-done.10.other, bf16[256,512]{1,0:T(8,128)(2,1)S(1)} %copy-done.3, bf16[256,512]{1,0:T(8,128)(2,1)S(1)} %copy-done.7), custom_call_target="tpu_custom_call" | custom-call | tf_op jit(solution)/shard_map/cond/branch_2_fun/pack/pallas_call | solution.py:317
  69.4 1.5 %collective-permute-start.11 = (f32[512,384]{1,0:T(8,128)}, f32[512,384]{1,0:T(8,128)S(1)}, u32[]{:S(2)}, u32[]{:S(2)}) collective-permute-start(f32[512,384]{1,0:T(8,128)} %pack.13), channel_id=1, source_target_pairs={{0,16},{8,24},{16,0},{24,8},{1,17},{9,25},{17,1},{25,9},{2,18},{10... | collective-permute-start | bytes 2359304 | tf_op jit(solution)/shard_map/cond/branch_2_fun/ppermute | solution.py:476
  71.0 13.5 %collective-permute-done.13.refs_0_ = f32[512,384]{1,0:T(8,128)} collective-permute-done((f32[512,384]{1,0:T(8,128)}, f32[512,384]{1,0:T(8,128)}, u32[]{:S(2)}, u32[]{:S(2)}) %collective-permute-start.13) | collective-permute-done | bytes 786464 | tf_op jit(solution)/shard_map/cond/branch_2_fun/ppermute | solution.py:476
  84.4 16.2 %collective-permute-done.11.refs_0_ = f32[512,384]{1,0:T(8,128)S(1)} collective-permute-done((f32[512,384]{1,0:T(8,128)}, f32[512,384]{1,0:T(8,128)S(1)}, u32[]{:S(2)}, u32[]{:S(2)}) %collective-permute-start.11) | collective-permute-done | bytes 786464 | tf_op jit(solution)/shard_map/cond/branch_2_fun/ppermute | solution.py:476
  100.7 4.0 %finish.12.refs_3_ = f32[128,16,256]{2,1,0:T(8,128)} custom-call(s32[1]{0:T(128)S(6)} %and.12.core, f32[1]{0:T(128)} %get-tuple-element.226.weight, f32[64,16,256]{2,1,0:T(8,128)S(1)} %get-tuple-element.227.mine, f32[64,16,256]{2,1,0:T(8,128)S(1)} %get-tuple-element.228.other, bf16[256,256]{1,0:T(8,128)(2,1)S(1)} %get-tuple-element.244.partner, ...), custom_call_target="tpu_custom_call" | custom-call | tf_op jit(solution)/shard_map/cond/branch_2_fun/finish/pallas_call | solution.py:375
  104.6 4.1 %finish.13 = f32[128,16,256]{2,1,0:T(8,128)} custom-call(s32[1]{0:T(128)S(6)} %and.12.core, f32[1]{0:T(128)} %get-tuple-element.226.weight, f32[64,16,256]{2,1,0:T(8,128)} %sections.7.mine, f32[64,16,256]{2,1,0:T(8,128)} %collective-permute-done.10.other, bf16[256,256]{1,0:T(8,128)(2,1)S(1)} %get-tuple-element.244.partner, ...), custom_call_target="tpu_custom_call", output_to_operand_aliasing={{}: (8, {})} | custom-call | tf_op jit(solution)/shard_map/cond/branch_2_fun/finish/pallas_call | solution.py:375
  (50 shorter events, 5.8 us)
Async XLA Ops:
  0.0 24.8 %copy-start = (f32[1,128,16,256]{3,2,1,0:T(8,128)S(1)}, f32[1,128,16,256]{3,2,1,0:T(8,128)}, u32[]{:S(2)}) copy-start(f32[1,128,16,256]{3,2,1,0:T(8,128)} %param.9) | copy-start | bytes 6291460
  0.0 17.3 %copy-start.34 = (s32[4]{0:T(128)S(1)}, s32[4]{0:T(128)}, u32[]{:S(2)}) copy-start(s32[4]{0:T(128)} %refs_1_.3) | copy-start | bytes 52
  0.0 16.6 %copy-start.36 = (f32[2,4]{1,0:T(2,128)S(1)}, f32[2,4]{1,0:T(2,128)}, u32[]{:S(2)}) copy-start(f32[2,4]{1,0:T(2,128)} %param.12) | copy-start | bytes 100
  1.7 18.4 %collective-permute-start.20 = (f32[4,16,256]{2,1,0:T(8,128)}, f32[4,16,256]{2,1,0:T(8,128)S(1)}, u32[]{:S(2)}, u32[]{:S(2)}) collective-permute-start(f32[4,16,256]{2,1,0:T(8,128)} %get-tuple-element.288), channel_id=1, source_target_pairs={{0,4},{4,0},{1,5},{5,1},{2,6},{6,2},{3,7},{7,3},{8,12},{12,8},{9,1... | collective-permute-start | bytes 196616 | tf_op jit(solution)/shard_map/ppermute | solution.py:416
  4.6 15.4 %collective-permute-start.21 = (f32[4,16,256]{2,1,0:T(8,128)S(1)}, f32[4,16,256]{2,1,0:T(8,128)S(1)}, u32[]{:S(2)}, u32[]{:S(2)}) collective-permute-start(f32[4,16,256]{2,1,0:T(8,128)S(1)} %get-tuple-element.289), channel_id=1, source_target_pairs={{0,4},{4,0},{1,5},{5,1},{2,6},{6,2},{3,7},{7,3},{8,12},{12,8},{9,1... | collective-permute-start | bytes 196616 | tf_op jit(solution)/shard_map/ppermute | solution.py:417
  6.8 15.7 %collective-permute-start.23 = (f32[72,4,256]{2,1,0:T(4,128)}, f32[72,4,256]{2,1,0:T(4,128)S(1)}, u32[]{:S(2)}, u32[]{:S(2)}) collective-permute-start(f32[72,4,256]{2,1,0:T(4,128)} %get-tuple-element.282), channel_id=1, source_target_pairs={{0,3},{1,0},{2,1},{3,2},{4,7},{5,4},{6,5},{7,6},{8,11},{9,8},{10,9... | collective-permute-start | bytes 884744 | tf_op jit(solution)/shard_map/ppermute | solution.py:415
  10.9 13.1 %collective-permute-start.22 = (f32[72,4,256]{2,1,0:T(4,128)}, f32[72,4,256]{2,1,0:T(4,128)S(1)}, u32[]{:S(2)}, u32[]{:S(2)}) collective-permute-start(f32[72,4,256]{2,1,0:T(4,128)} %get-tuple-element.283), channel_id=1, source_target_pairs={{0,1},{1,2},{2,3},{3,0},{4,5},{5,6},{6,7},{7,4},{8,9},{9,10},{10,1... | collective-permute-start | bytes 884744 | tf_op jit(solution)/shard_map/ppermute | solution.py:414
  20.0 4.1 %copy-start.19 = (f32[4,16,256]{2,1,0:T(8,128)}, f32[4,16,256]{2,1,0:T(8,128)S(1)}, u32[]{:S(2)}) copy-start(f32[4,16,256]{2,1,0:T(8,128)S(1)} %collective-permute-done.20) | copy-start | bytes 196612
  20.1 4.0 %copy-start.24 = (f32[4,16,256]{2,1,0:T(8,128)}, f32[4,16,256]{2,1,0:T(8,128)S(1)}, u32[]{:S(2)}) copy-start(f32[4,16,256]{2,1,0:T(8,128)S(1)} %collective-permute-done.21) | copy-start | bytes 196612
  22.6 14.3 %copy-start.35 = (s32[4]{0:T(128)S(1)}, s32[4]{0:T(128)}, u32[]{:S(2)}) copy-start(s32[4]{0:T(128)} %refs_2_.1) | copy-start | bytes 52
  32.9 16.1 %collective-permute-start.24 = (f32[64,16,256]{2,1,0:T(8,128)S(1)}, f32[64,16,256]{2,1,0:T(8,128)S(1)}, u32[]{:S(2)}, u32[]{:S(2)}) collective-permute-start(f32[64,16,256]{2,1,0:T(8,128)S(1)} %sections.9), channel_id=1, source_target_pairs={{0,8},{8,0},{16,24},{24,16},{1,9},{9,1},{17,25},{25,17},{2,10},{10... | collective-permute-start | bytes 3145736 | tf_op jit(solution)/shard_map/ppermute | solution.py:466
  33.0 11.4 %collective-permute-start.25 = (f32[64,4,256]{2,1,0:T(4,128)}, f32[64,4,256]{2,1,0:T(4,128)}, u32[]{:S(2)}, u32[]{:S(2)}) collective-permute-start(f32[64,4,256]{2,1,0:T(4,128)} %pad_maximum_fusion), channel_id=1, source_target_pairs={{0,1},{1,2},{2,3},{3,0},{4,5},{5,6},{6,7},{7,4},{8,9},{9,10},{10,1... | collective-permute-start | bytes 786440 | tf_op jit(solution)/shard_map/ppermute | solution.py:423
  34.6 14.3 %collective-permute-start.26 = (f32[64,4,256]{2,1,0:T(4,128)}, f32[64,4,256]{2,1,0:T(4,128)}, u32[]{:S(2)}, u32[]{:S(2)}) collective-permute-start(f32[64,4,256]{2,1,0:T(4,128)} %pad_maximum_fusion.1), channel_id=1, source_target_pairs={{0,3},{1,0},{2,1},{3,2},{4,7},{5,4},{6,5},{7,6},{8,11},{9,8},{10,9... | collective-permute-start | bytes 786440 | tf_op jit(solution)/shard_map/ppermute | solution.py:424
  49.0 3.2 %copy-start.12 = (f32[72,4,256]{2,1,0:T(4,128)S(1)}, f32[72,4,256]{2,1,0:T(4,128)}, u32[]{:S(2)}) copy-start(f32[72,4,256]{2,1,0:T(4,128)} %get-tuple-element.237.refs_6_) | copy-start | bytes 884740 | tf_op jit(solution)/shard_map/cond
  49.0 3.2 %copy-start.17 = (bf16[256,256]{1,0:T(8,128)(2,1)S(1)}, bf16[256,256]{1,0:T(8,128)(2,1)}, u32[]{:S(2)}) copy-start(bf16[256,256]{1,0:T(8,128)(2,1)} %get-tuple-element.242.refs_11_) | copy-start | bytes 393220 | tf_op jit(solution)/shard_map/cond
  49.0 3.2 %copy-start.22 = (f32[4,16,256]{2,1,0:T(8,128)S(1)}, f32[4,16,256]{2,1,0:T(8,128)}, u32[]{:S(2)}) copy-start(f32[4,16,256]{2,1,0:T(8,128)} %get-tuple-element.240.refs_9_) | copy-start | bytes 196612 | tf_op jit(solution)/shard_map/cond
  52.2 14.4 %copy-start.3 = (bf16[256,512]{1,0:T(8,128)(2,1)S(1)}, bf16[256,512]{1,0:T(8,128)(2,1)}, u32[]{:S(2)}) copy-start(bf16[256,512]{1,0:T(8,128)(2,1)} %get-tuple-element.229.refs_0_) | copy-start | bytes 786436 | tf_op jit(solution)/shard_map/cond
  52.2 14.4 %copy-start.7 = (bf16[256,512]{1,0:T(8,128)(2,1)S(1)}, bf16[256,512]{1,0:T(8,128)(2,1)}, u32[]{:S(2)}) copy-start(bf16[256,512]{1,0:T(8,128)(2,1)} %get-tuple-element.230.refs_1_) | copy-start | bytes 786436 | tf_op jit(solution)/shard_map/cond
  63.6 3.1 %collective-permute-start.10 = (f32[64,16,256]{2,1,0:T(8,128)}, f32[64,16,256]{2,1,0:T(8,128)}, u32[]{:S(2)}, u32[]{:S(2)}) collective-permute-start(f32[64,16,256]{2,1,0:T(8,128)} %sections.7.mine), channel_id=1, source_target_pairs={{0,8},{8,0},{16,24},{24,16},{1,9},{9,1},{17,25},{25,17},{2,10},{10... | collective-permute-start | bytes 3145736 | tf_op jit(solution)/shard_map/cond/branch_2_fun/ppermute | solution.py:485
  63.6 20.8 %collective-permute-start.13 = (f32[512,384]{1,0:T(8,128)}, f32[512,384]{1,0:T(8,128)}, u32[]{:S(2)}, u32[]{:S(2)}) collective-permute-start(f32[512,384]{1,0:T(8,128)} %pack.12), channel_id=1, source_target_pairs={{0,16},{8,24},{16,0},{24,8},{1,17},{9,25},{17,1},{25,9},{2,18},{10... | collective-permute-start | bytes 2359304 | tf_op jit(solution)/shard_map/cond/branch_2_fun/ppermute | solution.py:476
  69.4 31.2 %collective-permute-start.11 = (f32[512,384]{1,0:T(8,128)}, f32[512,384]{1,0:T(8,128)S(1)}, u32[]{:S(2)}, u32[]{:S(2)}) collective-permute-start(f32[512,384]{1,0:T(8,128)} %pack.13), channel_id=1, source_target_pairs={{0,16},{8,24},{16,0},{24,8},{1,17},{9,25},{17,1},{25,9},{2,18},{10... | collective-permute-start | bytes 2359304 | tf_op jit(solution)/shard_map/cond/branch_2_fun/ppermute | solution.py:476
  84.4 16.2 %collective-permute-start.14 = (f32[512,384]{1,0:T(8,128)}, f32[512,384]{1,0:T(8,128)}, u32[]{:S(2)}, u32[]{:S(2)}) collective-permute-start(f32[512,384]{1,0:T(8,128)} %collective-permute-done.13.refs_0_), channel_id=1, source_target_pairs={{0,8},{8,0},{16,24},{24,16},{1,9},{9,1},{17,25},{25,17},{2,10},{10... | collective-permute-start | bytes 2359304 | tf_op jit(solution)/shard_map/cond/branch_2_fun/ppermute | solution.py:487
  100.6 4.0 %copy-start.26 = (f32[512,384]{1,0:T(8,128)}, f32[512,384]{1,0:T(8,128)S(1)}, u32[]{:S(2)}) copy-start(f32[512,384]{1,0:T(8,128)S(1)} %collective-permute-done.11.refs_0_) | copy-start | bytes 2359300 | tf_op jit(solution)/shard_map/cond
  100.6 4.0 %collective-permute-start.12 = (f32[512,384]{1,0:T(8,128)S(1)}, f32[512,384]{1,0:T(8,128)}, u32[]{:S(2)}, u32[]{:S(2)}) collective-permute-start(f32[512,384]{1,0:T(8,128)S(1)} %collective-permute-done.11.refs_0_), channel_id=1, source_target_pairs={{0,8},{8,0},{16,24},{24,16},{1,9},{9,1},{17,25},{25,17},{2,10},{10... | collective-permute-start | bytes 2359304 | tf_op jit(solution)/shard_map/cond/branch_2_fun/ppermute | solution.py:492
  (2 other events, 2.2 us)
where the time goes:
time: 109 us
  waiting for transfers between devices  43.5 us (40%)
  Pallas kernels  35.6 us (33%)
  starting transfers between devices  14.2 us (13%)
  local copies, waits for them, and re-layouts  10 us (9%)
  other arithmetic  3.27 us (3%)
  between operations  2.04 us (2%)
    ppermute x2, waiting for transfers between devices, hop(): received.append(lax.ppermute(message, 'comp', pairs_of))  29.7 us
    pallas_call x2, Pallas kernels, stencil(): pl.pallas_call(lambda *refs: stencil_kernel(plan, keep, *refs), out_shape...  19.4 us
    pallas_call x2, Pallas kernels, finish(): pl.pallas_call(kernel, out_shape=jax.ShapeDtypeStruct(shape, F32), grid_s...  8.05 us
    ppermute x1, waiting for transfers between devices, local(): low_two = lax.ppermute(top, 'gy', forward['gy'])  6.27 us
    pallas_call x2, Pallas kernels, pack(): pl.pallas_call(kernel, out_shape=[jax.ShapeDtypeStruct((half * own, cap),...  5.44 us
    ppermute x1, waiting for transfers between devices, local(): high_two = lax.ppermute(bottom, 'gy', backward['gy'])  4.6 us
    ppermute x1, starting transfers between devices, local(): high_one = lax.ppermute(block[left:right, :halo], 'gy', backward['gy'])  4.11 us
    ppermute x2, starting transfers between devices, hop(): received.append(lax.ppermute(message, 'comp', pairs_of))  3.1 us
  transfers between devices with their start and end apart: 12, of which 6 were waited for; matrix products, arithmetic and copies ran while one was open for 9% of the time, Pallas kernels for 9%

commit v1 on v0

v1 whole, which is shorter than its diff:
```python
import jax
import jax.numpy as jnp
from jax import lax
from jax.experimental import pallas as pl
from jax.experimental.pallas import tpu as pltpu
from jax.sharding import PartitionSpec as P


SECTIONS = 4
LEVEL_SUM = 8
TOP = LEVEL_SUM - 2
FINE = 2**TOP
LANES = 128
F32 = jnp.float32
BF16 = jnp.bfloat16
SMEM = pl.BlockSpec(memory_space=pltpu.SMEM)
VMEM = pl.BlockSpec(memory_space=pltpu.VMEM)
ANY = pl.BlockSpec(memory_space=pl.ANY)
ROOM = pltpu.CompilerParams(vmem_limit_bytes=24 * 2**20)


def points(level):
    return 1 if level == 0 else 2 ** (level - 1)


def ring(count, step):
    return [(i, (i + step) % count) for i in range(count)]


def split(values):
    head = values.astype(BF16)
    tail = (values - head.astype(F32)).astype(BF16)
    return head, tail


def dot(left, right):
    return jnp.dot(left, right, preferred_element_type=F32)


def staircase(ones, others):
    betas = []
    for k3 in range(TOP + 1):
        beta = jnp.int32(-1)
        for one in ones:
            for other in others:
                third = jnp.minimum(one, other)
                fourth = LEVEL_SUM - jnp.maximum(one, other)
                beta = jnp.maximum(beta, jnp.where(third >= k3, fourth, -1))
        betas.append(beta)
    return betas


def stair_counts(betas):
    return [
        jnp.where(beta >= 0, points(k3) * jnp.left_shift(jnp.int32(1), jnp.maximum(beta, 0)), 0)
        for k3, beta in enumerate(betas)
    ]


def slot_places(row, betas):
    total = jnp.int32(0)
    k3 = jnp.full_like(row, -1)
    start = jnp.zeros_like(row)
    beta_row = jnp.zeros_like(row)
    for k, (beta, count) in enumerate(zip(betas, stair_counts(betas))):
        past = row >= total
        k3 = jnp.where(past, k, k3)
        start = jnp.where(past, total, start)
        beta_row = jnp.where(past, jnp.maximum(beta, 0), beta_row)
        total = total + count
    used = row < total
    inside = row - start
    fourth = jnp.bitwise_and(inside, jnp.left_shift(jnp.ones_like(row), beta_row) - 1)
    rank = jnp.right_shift(inside, beta_row)
    place3 = jnp.where(k3 == 0, 0, jnp.left_shift(2 * rank + 1, jnp.maximum(TOP - k3, 0)))
    place4 = jnp.left_shift(fourth, jnp.maximum(TOP - beta_row, 0))
    return place3, place4, used


def cell_places(index, level_a):
    level_b = LEVEL_SUM - level_a
    third = jnp.right_shift(index, level_b)
    fourth = jnp.bitwise_and(index, jnp.left_shift(jnp.int32(1), level_b) - 1)
    return jnp.left_shift(third, TOP - level_a), jnp.left_shift(fourth, TOP - level_b)


def held(place3, place4, level_a):
    low3 = jnp.left_shift(jnp.int32(1), TOP - level_a) - 1
    low4 = jnp.left_shift(jnp.int32(1), TOP - (LEVEL_SUM - level_a)) - 1
    return jnp.logical_and(jnp.bitwise_and(place3, low3) == 0, jnp.bitwise_and(place4, low4) == 0)


def surplus_weight(cell, slot):
    half = jnp.bitwise_and(slot, -slot)
    side = jnp.where(slot == 0, 0.0, -0.5)
    weight = jnp.where(cell == slot, 1.0, 0.0)
    weight = weight + jnp.where(cell == slot - half, side, 0.0)
    return weight + jnp.where(cell == jnp.bitwise_and(slot + half, FINE - 1), side, 0.0)


def hat_weight(cell, slot):
    half = jnp.bitwise_and(slot, -slot)
    reach = jnp.maximum(half - jnp.abs(cell - slot), 0).astype(F32)
    return jnp.where(slot == 0, 1.0, reach / jnp.maximum(half, 1).astype(F32))


def linear_weight(cell, node, low_a, low_b):
    coarse = jnp.left_shift(jnp.int32(1), TOP - jnp.minimum(low_a, low_b))
    gap = jnp.bitwise_and(cell - node, FINE - 1)
    gap = jnp.minimum(gap, FINE - gap)
    reach = jnp.maximum(coarse - gap, 0).astype(F32)
    scale = jnp.float32(1.0)
    for k in range(TOP):
        scale = scale * jnp.where(TOP - jnp.minimum(low_a, low_b) > k, 0.5, 1.0)
    return jnp.where(jnp.bitwise_and(node, coarse - 1) == 0, reach * scale, 0.0)


def grid_numbers(rates, level_a):
    level_b = LEVEL_SUM - level_a
    third = jnp.float32(1.0)
    fourth = jnp.float32(1.0)
    for k in range(TOP):
        third = third * jnp.where(TOP - level_a > k, 0.5, 1.0)
        fourth = fourth * jnp.where(TOP - level_b > k, 0.5, 1.0)
    dif = [rates[0], rates[1], rates[2] * (third * third), rates[3] * (fourth * fourth)]
    cou = [rates[4], rates[5], rates[6] * third, rates[7] * fourth]
    return dif, cou


def setup_kernel(flat, chips, place, levels, weights, rates, *outs):
    head_out, tail_out, partner_out = outs[:3]
    mine = place[0]
    other = mine + 1 - 2 * jnp.bitwise_and(mine, 1)
    chip = jnp.right_shift(mine, 1)
    level = levels[mine]
    level_other = levels[other]
    weight = weights[mine].astype(F32)
    weight_other = weights[other].astype(F32)
    rows = lax.broadcasted_iota(jnp.int32, (flat, flat), 0)
    columns = lax.broadcasted_iota(jnp.int32, (flat, flat), 1)
    dif, cou = grid_numbers(rates, level)
    width = jnp.left_shift(jnp.int32(1), LEVEL_SUM - level)
    row4 = jnp.bitwise_and(rows, width - 1)
    column4 = jnp.bitwise_and(columns, width - 1)
    same3 = (rows - row4) == (columns - column4)
    step = jnp.where(jnp.bitwise_and(columns + width, flat - 1) == rows, dif[2], 0.0)
    step = step + jnp.where(jnp.bitwise_and(columns - width, flat - 1) == rows, dif[2] + cou[2], 0.0)
    up4 = jnp.logical_and(same3, jnp.bitwise_and(column4 + 1, width - 1) == row4)
    down4 = jnp.logical_and(same3, jnp.bitwise_and(column4 - 1, width - 1) == row4)
    step = step + jnp.where(up4, dif[3], 0.0)
    step = step + jnp.where(down4, dif[3] + cou[3], 0.0)
    head, tail = split(step)
    head_out[...] = head
    tail_out[...] = tail

    node3, node4 = cell_places(rows, level_other)
    cell3, cell4 = cell_places(columns, level)
    linear = linear_weight(cell3, node3, level, level_other)
    linear = linear * linear_weight(cell4, node4, LEVEL_SUM - level, LEVEL_SUM - level_other)
    partner_out[...] = (linear * weight_other).astype(BF16)

    slots = 2 * flat
    for shift in range(1, chips):
        own_out, other_out, back_out = outs[3 * shift : 3 * shift + 3]
        target = lax.rem(chip + shift, jnp.int32(chips))
        source = lax.rem(chip + chips - shift, jnp.int32(chips))
        betas = staircase((level, level_other), (levels[2 * target], levels[2 * target + 1]))
        row = lax.broadcasted_iota(jnp.int32, (1, slots), 1)
        cell = lax.broadcasted_iota(jnp.int32, (flat, 1), 0)
        place3, place4, used = slot_places(row, betas)
        for out, grid_level, grid_weight in (
            (own_out, level, weight),
            (other_out, level_other, weight_other),
        ):
            kept = jnp.where(
                jnp.logical_and(used, held(place3, place4, grid_level)), grid_weight, 0.0
            )
            cell3, cell4 = cell_places(cell, grid_level)
            value = surplus_weight(cell3, place3) * surplus_weight(cell4, place4) * kept
            out[...] = value.astype(BF16)
        betas = staircase((level, level_other), (levels[2 * source], levels[2 * source + 1]))
        row = lax.broadcasted_iota(jnp.int32, (slots, 1), 0)
        cell = lax.broadcasted_iota(jnp.int32, (1, flat), 1)
        place3, place4, used = slot_places(row, betas)
        kept = jnp.where(jnp.logical_and(used, held(place3, place4, level)), 1.0, 0.0)
        cell3, cell4 = cell_places(cell, level)
        value = hat_weight(cell3, place3) * hat_weight(cell4, place4) * kept
        back_out[...] = value.astype(BF16)


def setup_tables(flat, chips, place, levels, weights, rates):
    shapes = [jax.ShapeDtypeStruct((flat, flat), BF16)] * 3
    for _ in range(1, chips):
        shapes += [jax.ShapeDtypeStruct((flat, 2 * flat), BF16)] * 2
        shapes += [jax.ShapeDtypeStruct((2 * flat, flat), BF16)]
    return pl.pallas_call(
        lambda *refs: setup_kernel(flat, chips, *refs),
        out_shape=shapes,
        in_specs=[SMEM] * 4,
        out_specs=[VMEM] * len(shapes),
        compiler_params=ROOM,
        name="tables",
    )(place, levels, weights, rates.reshape(-1))


def faces(block, start, count):
    _, own, flat = block.shape
    halo = SECTIONS

    def kernel(block, low, high, rows, sem):
        copy = pltpu.make_async_copy(block.at[pl.ds(start, count)], rows, sem)
        copy.start()
        copy.wait()
        low[...] = rows[:, own - halo :]
        high[...] = rows[:, :halo]

    side = jax.ShapeDtypeStruct((count, halo, flat), F32)
    return pl.pallas_call(
        kernel,
        out_shape=[side, side],
        in_specs=[ANY],
        out_specs=[VMEM] * 2,
        scratch_shapes=[pltpu.VMEM((count, own, flat), F32), pltpu.SemaphoreType.DMA],
        compiler_params=ROOM,
        name="faces",
    )(block)


def outer_faces(block, ends):
    long, own, flat = block.shape
    halo = SECTIONS
    span = long // 4 - halo

    def kernel(block, ends, low, high):
        for out, columns in ((low, slice(own - halo, own)), (high, slice(0, halo))):
            out[:halo] = ends[:halo, columns]
            out[halo : halo + span] = block[:span, columns]
            out[halo + span : halo + 2 * span] = block[long - span :, columns]
            out[halo + 2 * span :] = ends[halo:, columns]

    side = jax.ShapeDtypeStruct((long // 2, halo, flat), F32)
    return pl.pallas_call(
        kernel,
        out_shape=[side, side],
        in_specs=[VMEM] * 2,
        out_specs=[VMEM] * 2,
        compiler_params=ROOM,
        name="outer_faces",
    )(block, ends)


def chunk_plans(long):
    halo = SECTIONS
    quarter = long // 4
    wide = long // 2 + 2 * halo
    piece = quarter + 2 * halo
    return [
        {
            "own": [(None, quarter - halo, 0, wide)],
            "edge": [(0, 0, 0, wide)],
            "start": quarter,
            "rows": wide,
            "pitch": quarter,
        },
        {
            "own": [
                (None, long - quarter - halo, 0, quarter + halo),
                ("ends", halo, quarter + halo, halo),
                ("ends", 0, piece, halo),
                (None, 0, piece + halo, quarter + halo),
            ],
            "edge": [
                (0, wide - 2 * halo, 0, 2 * halo),
                (1, quarter, 2 * halo, quarter),
                (1, 0, piece, quarter),
                (0, 0, piece + quarter, 2 * halo),
            ],
            "start": long - quarter,
            "rows": 2 * piece,
            "pitch": piece,
        },
    ]


def stencil_kernel(plan, order, place, core, levels, rates, reaction, field, *refs):
    count = 2 * len(order) + (2 if plan["own"][1:] else 1) + 1
    held_refs, (keep, give, state, sems) = refs[:count], refs[count:]
    halo = SECTIONS
    own = field.shape[1]
    tall = own + 2 * halo
    flat = field.shape[2]
    first = state.at[0]
    copies = []
    for source, start, target, rows in plan["own"]:
        if source is None:
            copies.append((field.at[pl.ds(start, rows)], first.at[pl.ds(target, rows), pl.ds(0, own)]))
    copies = [
        pltpu.make_async_copy(source, target, sems.at[k]) for k, (source, target) in enumerate(copies)
    ]
    for copy in copies:
        copy.start()
    level = levels[place[0]]
    dif, cou = grid_numbers(rates, level)
    centre_weight = 1.0 - 2.0 * (dif[0] + dif[1] + dif[2] + dif[3])
    centre_weight = centre_weight - (cou[0] + cou[1] + cou[2] + cou[3])
    rate = reaction[0]
    head_ref, tail_ref = held_refs[:2]
    sides = {source: held_refs[2 + 2 * k : 4 + 2 * k] for k, source in enumerate(order)}
    for source, start, target, rows in plan["own"]:
        if source is not None:
            first[target : target + rows, :own] = held_refs[-1][start : start + rows]
    for source, start, target, rows in plan["edge"]:
        low, high = sides[source]
        first[target : target + rows, own : own + halo] = high[start : start + rows]
        first[target : target + rows, own + halo :] = low[start : start + rows]
    for copy in copies:
        copy.wait()

    def block(which, at, depth, step):
        centre = state[which, pl.ds(at, step)]
        above = state[which, pl.ds(at + 1, step), :depth]
        below = state[which, pl.ds(at - 1, step), :depth]
        ahead = jnp.roll(centre, -1, axis=1)[:, :depth]
        behind = jnp.roll(centre, 1, axis=1)[:, :depth]
        centre = centre[:, :depth]
        rounded = centre.reshape(step * depth, flat).astype(BF16)
        inner = dot(rounded, head_ref[...]) + dot(rounded, tail_ref[...])
        value = centre * (centre_weight + rate / (1.0 + centre * centre))
        value = value + dif[0] * above + (dif[0] + cou[0]) * below
        value = value + dif[1] * ahead + (dif[1] + cou[1]) * behind
        return value + inner.reshape(step, depth, flat)

    step = (plan["rows"] - 2) // 2

    def body(i, carry):
        which = jnp.bitwise_and(jnp.right_shift(i, 1), 1)
        at = 1 + step * jnp.bitwise_and(i, 1)
        state[1 - which, pl.ds(at, step)] = block(which, at, tall, step)
        return carry

    lax.fori_loop(0, 2 * (SECTIONS - 1), body, 0)
    last = keep.shape[0] // 2
    for side, out in enumerate((keep, give)):
        base = halo + plan["pitch"] * jnp.bitwise_xor(core[0], side)

        def final(i, carry, base=base, out=out):
            out[pl.ds(i * last, last)] = block((SECTIONS - 1) % 2, base + i * last, own, last)
            return carry

        lax.fori_loop(0, 2, final, 0)


def stencil(plan, place, core, levels, rates, reaction, field, edges, ends, head, tail):
    long, own, flat = field.shape
    halo = SECTIONS
    order = sorted({source for source, *_ in plan["edge"]})
    operands = [head, tail] + [ref for source in order for ref in edges[source]]
    operands += [ends] if plan["own"][1:] else []
    straight = sum(source is None for source, *_ in plan["own"])
    half = jax.ShapeDtypeStruct((long // 4, own, flat), F32)
    return pl.pallas_call(
        lambda *refs: stencil_kernel(plan, order, *refs),
        out_shape=[half, half],
        in_specs=[SMEM] * 5 + [ANY] + [VMEM] * len(operands),
        out_specs=[VMEM, VMEM],
        scratch_shapes=[
            pltpu.VMEM((2, plan["rows"], own + 2 * halo, flat), F32),
            pltpu.SemaphoreType.DMA((straight,)),
        ],
        compiler_params=ROOM,
        name="sections",
    )(place, core, levels, rates.reshape(-1), reaction, field, *operands)


def pack(cap, values, others, tables):
    count, own, flat = values.shape
    parts = len(tables)

    def kernel(mine, other, *refs):
        head, tail = split(mine[...].reshape(count * own, flat))
        other_head, other_tail = split(other[...].reshape(count * own, flat))
        for shift in range(parts):
            own_table = refs[2 * shift][:, :cap]
            other_table = refs[2 * shift + 1][:, :cap]
            refs[2 * parts + shift][...] = (
                dot(head, own_table)
                + dot(tail, own_table)
                + dot(other_head, other_table)
                + dot(other_tail, other_table)
            )

    return pl.pallas_call(
        kernel,
        out_shape=[jax.ShapeDtypeStruct((count * own, cap), F32)] * parts,
        in_specs=[VMEM] * (2 + 2 * parts),
        out_specs=[VMEM] * parts,
        compiler_params=ROOM,
        name="pack",
    )(values, others, *[t for pair in tables for t in pair])


def shares(weight, mine, other, table):
    count, own, flat = mine.shape
    head, tail = split(other.reshape(count * own, flat))
    return weight * mine.reshape(count * own, flat) + dot(head, table) + dot(tail, table)


def received(value, messages, backs):
    for message, back in zip(messages, backs):
        head, tail = split(message)
        value = value + dot(head, back) + dot(tail, back)
    return value


def write_rows(start, sides, core, out, rows, sems):
    copies = []
    for k, side in enumerate(sides):
        at = start + rows.shape[1] * jnp.bitwise_xor(core[0], side)
        at = jnp.where(at >= out.shape[0], at - out.shape[0], at)
        copies.append(pltpu.make_async_copy(rows.at[k], out.at[pl.ds(at, rows.shape[1])], sems.at[k]))
    return copies


def finish(cap, start, core, weight, values, others, partner, near, far, backs, carry, shape):
    count, own, flat = values[0].shape
    parts = len(backs)

    def kernel(core, weight, *refs):
        back_refs = [ref[:cap] for ref in refs[5 + 2 * parts : 5 + 3 * parts]]
        out, rows, sems = refs[-3:]
        copies = write_rows(start, (0, 1), core, out, rows, sems)
        for side in range(2):
            value = shares(weight[0], refs[side][...], refs[2 + side][...], refs[4][...])
            messages = [ref[...] for ref in refs[5 + side * parts : 5 + (side + 1) * parts]]
            rows[side] = received(value, messages, back_refs).reshape(count, own, flat)
            copies[side].start()
        for copy in copies:
            copy.wait()

    operands = [core, weight, *values, *others, partner, *near, *far, *backs]
    specs = [SMEM] * 2 + [VMEM] * (5 + 3 * parts)
    aliases = {}
    if carry is not None:
        aliases = {len(operands): 0}
        operands.append(carry)
        specs.append(ANY)
    return pl.pallas_call(
        kernel,
        out_shape=jax.ShapeDtypeStruct(shape, F32),
        in_specs=specs,
        out_specs=ANY,
        scratch_shapes=[pltpu.VMEM((2, count, own, flat), F32), pltpu.SemaphoreType.DMA((2,))],
        input_output_aliases=aliases,
        compiler_params=ROOM,
        name="finish",
    )(*operands)


def base(weight, values, others, partner):
    def kernel(weight, *refs):
        for side in range(2):
            value = shares(weight[0], refs[side][...], refs[2 + side][...], refs[4][...])
            refs[5 + side][...] = value.reshape(values[0].shape)

    half = jax.ShapeDtypeStruct(values[0].shape, F32)
    return pl.pallas_call(
        kernel,
        out_shape=[half, half],
        in_specs=[SMEM] + [VMEM] * 5,
        out_specs=[VMEM] * 2,
        compiler_params=ROOM,
        name="base",
    )(weight, *values, *others, partner)


def add_messages(cap, start, side, core, current, messages, backs, carry):
    count, own, flat = current.shape
    parts = len(backs)

    def kernel(core, current, *refs):
        out, rows, sems = refs[-3:]
        value = current[...].reshape(count * own, flat)
        value = received(value, [r[...] for r in refs[:parts]], [r[:cap] for r in refs[parts : 2 * parts]])
        rows[0] = value.reshape(count, own, flat)
        copies = write_rows(start, (side,), core, out, rows, sems)
        copies[0].start()
        copies[0].wait()

    return pl.pallas_call(
        kernel,
        out_shape=jax.ShapeDtypeStruct(carry.shape, F32),
        in_specs=[SMEM] + [VMEM] * (1 + 2 * parts) + [ANY],
        out_specs=ANY,
        scratch_shapes=[pltpu.VMEM((1, count, own, flat), F32), pltpu.SemaphoreType.DMA((1,))],
        input_output_aliases={2 + 2 * parts: 0},
        compiler_params=ROOM,
        name="add_messages",
    )(core, current, *messages, *backs, carry)


def slots_needed(third_level, chips):
    levels = third_level.reshape(chips, 2)
    most = jnp.int32(0)
    for shift in range(1, chips):
        shifted = jnp.roll(levels, -shift, axis=0)
        betas = staircase(
            (levels[:, 0], levels[:, 1]), (shifted[:, 0], shifted[:, 1])
        )
        most = jnp.maximum(most, jnp.max(sum(stair_counts(betas))))
    return most


def local(sizes, field, third_level, coefficients, rates, reaction):
    block = field[0]
    long, _, flat = block.shape
    halo = SECTIONS
    chips = sizes["comp"] // 2
    mine = lax.axis_index("comp")
    place = mine.reshape(1).astype(jnp.int32)
    core = jnp.bitwise_and(place, 1)
    weight = lax.dynamic_index_in_dim(coefficients, mine, 0, True).astype(F32)
    swap = [(i, i ^ 1) for i in range(sizes["comp"])]
    forward = {axis: ring(sizes[axis], 1) for axis in ("gx", "gy")}
    backward = {axis: ring(sizes[axis], -1) for axis in ("gx", "gy")}

    shape = block.shape
    plans = chunk_plans(long)
    low_one, high_one = faces(block, plans[0]["start"] - halo, plans[0]["rows"])
    one = (lax.ppermute(low_one, "gy", forward["gy"]), lax.ppermute(high_one, "gy", backward["gy"]))
    first_rows, last_rows = block[:halo], block[long - halo :]
    if sizes["gx"] == 2:
        ends = lax.ppermute(jnp.concatenate([last_rows, first_rows]), "gx", forward["gx"])
    else:
        before = lax.ppermute(last_rows, "gx", forward["gx"])
        after = lax.ppermute(first_rows, "gx", backward["gx"])
        ends = jnp.concatenate([before, after])
    branch = lax.div(slots_needed(third_level, chips) - 1, jnp.int32(LANES))
    tables = setup_tables(flat, chips, place, third_level, coefficients, rates)
    head, tail, partner = tables[:3]
    pairs = [(tables[3 * r], tables[3 * r + 1]) for r in range(1, chips)]
    backs = [tables[3 * r + 2] for r in range(1, chips)]
    low_two, high_two = outer_faces(block, ends)
    low_two = lax.ppermute(low_two, "gy", forward["gy"])
    high_two = lax.ppermute(high_two, "gy", backward["gy"])
    edges = [one, (low_two, high_two)]

    shifts = [
        [(2 * h + c, 2 * ((h + r) % chips) + c) for h in range(chips) for c in range(2)]
        for r in range(1, chips)
    ]
    scalars = (core, third_level, rates, reaction, block)

    def evolve(k, place, edges, ends):
        values = stencil(plans[k], place, *scalars, edges, ends, head, tail)
        return values, lax.ppermute(values[1], "comp", swap)

    def send(cap, values, other):
        sent = pack(cap, values[0], other, pairs)
        near = []
        for message, shift in zip(sent, shifts):
            near.append(lax.ppermute(message, "comp", shift))
        return sent[0], near, (other, lax.ppermute(values[0], "comp", swap))

    ready = lax.optimization_barrier((place, branch, partner))[0]
    values_0, other_0 = evolve(0, ready, edges, None)

    def tail_of(cap):
        def run(values_0, other_0, edges, ends):
            sent, near_0, others_0 = send(cap, values_0, other_0)
            ready = lax.optimization_barrier((place, sent))[0]
            values_1, other_1 = evolve(1, ready, edges, ends)
            _, near_1, others_1 = send(cap, values_1, other_1)

            def back(near):
                far = []
                for message in near:
                    far.append(lax.ppermute(message, "comp", swap))
                return far

            halves = base(weight, values_1, others_1, partner)
            far_0 = back(near_0)
            result = finish(
                cap, plans[0]["start"], core, weight, values_0, others_0, partner,
                near_0, far_0, backs, None, shape,
            )
            far_1 = back(near_1)
            for side, messages in enumerate((near_1, far_1)):
                result = add_messages(
                    cap, plans[1]["start"], side, core, halves[side], messages, backs, result
                )
            return result

        return run

    caps = list(range(LANES, 2 * flat + 1, LANES))
    return lax.switch(
        branch, [tail_of(cap) for cap in caps], values_0, other_0, edges, ends
    )[None]


def solution(mesh):
    sizes = dict(mesh.shape)
    step = jax.shard_map(
        lambda *args: local(sizes, *args),
        mesh=mesh,
        in_specs=(P("comp", "gx", "gy", None), P(), P(), P(), P()),
        out_specs=P("comp", "gx", "gy", None),
        check_vma=False,
    )

    def run(field, third_level, coefficients, rates, reaction):
        placed = step
        return placed(field, third_level, coefficients, rates, reaction)

    return run
```

time: 109 us -> 109 us (level)
  waiting for transfers between devices: 43.5 us -> 57.1 us
  local copies, waits for them, and re-layouts: 10 us -> 2.47 us
  Pallas kernels: 35.6 us -> 31.7 us
  other arithmetic: 3.27 us -> 0.75 us
    ppermute x12 -> x13, waiting for transfers between devices: 43.5 us -> 57.1 us  [the longest x2 32.6 us: send(): near.append(lax.ppermute(message, 'comp', shift))]
    slice x5 -> x1, local copies, waits for them, and re-layouts: 5.92 us -> 0.01 us  [local(): first_rows, last_rows = (block[:halo], block[long - halo:])]
    pallas_call x6 -> x10, Pallas kernels: 32.9 us -> 29 us  [the longest x2 18.7 us: stencil(): pl.pallas_call(lambda *refs: stencil_kernel(plan, order, *refs), out_shap...]
    concatenate x2 -> x1, other arithmetic: 2.48 us -> 0.01 us  [local(): jnp.concatenate([last_rows, first_rows])]
    ppermute x12 -> x13, starting transfers between devices: 14.2 us -> 14.5 us  [the longest x2 3.17 us: send(): near.append(lax.ppermute(message, 'comp', shift))]
  transfers between devices with their start and end apart: 12 -> 13, of which waited for: 6 -> 10; matrix products, arithmetic and copies ran while one was open for 9% -> 1% of each run, Pallas kernels for 9% -> 8%
where the time goes in v1:
time: 109 us
  waiting for transfers between devices  57.1 us (52%)
  Pallas kernels  31.7 us (29%)
  starting transfers between devices  14.5 us (13%)
  local copies, waits for them, and re-layouts  2.47 us (2%)
  between operations  2.29 us (2%)
    ppermute x2, waiting for transfers between devices, send(): near.append(lax.ppermute(message, 'comp', shift))  32.6 us
    pallas_call x2, Pallas kernels, stencil(): pl.pallas_call(lambda *refs: stencil_kernel(plan, order, *refs), out_shap...  18.7 us
    ppermute x1, waiting for transfers between devices, local(): low_two = lax.ppermute(low_two, 'gy', forward['gy'])  5.97 us
    ppermute x1, waiting for transfers between devices, local(): lax.ppermute(high_one, 'gy', backward['gy'])  4.86 us
    ppermute x1, waiting for transfers between devices, local(): lax.ppermute(jnp.concatenate([last_rows, first_rows]), 'gx', forward['gx'])  4.4 us
    ppermute x1, waiting for transfers between devices, local(): high_two = lax.ppermute(high_two, 'gy', backward['gy'])  3.38 us
    pallas_call x1, Pallas kernels, finish(): pl.pallas_call(kernel, out_shape=jax.ShapeDtypeStruct(shape, F32), in_spe...  3.19 us
    ppermute x2, starting transfers between devices, send(): near.append(lax.ppermute(message, 'comp', shift))  3.17 us
  transfers between devices with their start and end apart: 13, of which 10 were waited for; matrix products, arithmetic and copies ran while one was open for 1% of the time, Pallas kernels for 8%

profile of v1, /device:TPU:0, one launch (start us, length us, event | category | flops | bytes accessed | tf_op | source)
XLA Modules:
  0.0 109.0 jit_solution(18364681071078330574)
XLA Ops:
  0.0 1.5 %faces.1 = (f32[72,4,256]{2,1,0:T(4,128)S(1)}, f32[72,4,256]{2,1,0:T(4,128)S(1)}) custom-call(f32[128,16,256]{2,1,0:T(8,128)} %bitcast.14), custom_call_target="tpu_custom_call" | custom-call | tf_op jit(solution)/shard_map/faces/pallas_call | solution.py:218
  1.5 3.1 %collective-permute-start.28 = (f32[72,4,256]{2,1,0:T(4,128)S(1)}, f32[72,4,256]{2,1,0:T(4,128)S(1)}, u32[]{:S(2)}, u32[]{:S(2)}) collective-permute-start(f32[72,4,256]{2,1,0:T(4,128)S(1)} %get-tuple-element.300), channel_id=1, source_target_pairs={{0,1},{1,2},{2,3},{3,0},{4,5},{5,6},{6,7},{7,4},{8,9},{9,10},{10,1... | collective-permute-start | bytes 884744 | tf_op jit(solution)/shard_map/ppermute | solution.py:529
  4.6 2.1 %collective-permute-start.29 = (f32[72,4,256]{2,1,0:T(4,128)S(1)}, f32[72,4,256]{2,1,0:T(4,128)S(1)}, u32[]{:S(2)}, u32[]{:S(2)}) collective-permute-start(f32[72,4,256]{2,1,0:T(4,128)S(1)} %get-tuple-element.301), channel_id=1, source_target_pairs={{0,3},{1,0},{2,1},{3,2},{4,7},{5,4},{6,5},{7,6},{8,11},{9,8},{10,9... | collective-permute-start | bytes 884744 | tf_op jit(solution)/shard_map/ppermute | solution.py:529
  8.3 2.7 %tables.1 = (bf16[256,256]{1,0:T(8,128)(2,1)S(1)}, bf16[256,256]{1,0:T(8,128)(2,1)S(1)}, bf16[256,256]{1,0:T(8,128)(2,1)}, bf16[256,512]{1,0:T(8,128)(2,1)}, bf1...) custom-call(s32[1]{0:T(128)} %bitcast.6.refs_0_, s32[4]{0:T(128)S(1)} %copy-done.25, s32[4]{0:T(128)S(1)} %copy-done, ...), custom_call_target="tpu_custom_call" | custom-call | tf_op jit(solution)/shard_map/tables/pallas_call | solution.py:196
  11.7 2.8 %collective-permute-done.28.refs_8_ = f32[72,4,256]{2,1,0:T(4,128)S(1)} collective-permute-done((f32[72,4,256]{2,1,0:T(4,128)S(1)}, f32[72,4,256]{2,1,0:T(4,128)S(1)}, u32[]{:S(2)}, u32[]{:S(2)}) %collective-permute-start.28) | collective-permute-done | bytes 294944 | tf_op jit(solution)/shard_map/ppermute | solution.py:529
  14.5 4.9 %collective-permute-done.29.refs_9_ = f32[72,4,256]{2,1,0:T(4,128)S(1)} collective-permute-done((f32[72,4,256]{2,1,0:T(4,128)S(1)}, f32[72,4,256]{2,1,0:T(4,128)S(1)}, u32[]{:S(2)}, u32[]{:S(2)}) %collective-permute-start.29) | collective-permute-done | bytes 294944 | tf_op jit(solution)/shard_map/ppermute | solution.py:529
  20.1 8.9 %sections.9 = (f32[32,16,256]{2,1,0:T(8,128)S(1)}, f32[32,16,256]{2,1,0:T(8,128)}) custom-call(s32[1]{0:T(128)} %bitcast.6.refs_0_, s32[1]{0:T(128)} %and.4.refs_1_, s32[4]{0:T(128)S(1)} %copy-done.25, f32[8]{0:T(128)S(1)} %reshape.170.refs_3_, f32[1]{0:T(128)S(6)} %copy.30.refs_4_, f32[128,16,256]{2,1,0:T(8,128)S(1)} %bitcast.15, ...), custom_call_target="tpu_custom_call" | custom-call | tf_op jit(solution)/shard_map/sections/pallas_call | solution.py:361
  29.2 1.6 %collective-permute-start.31 = (f32[8,16,256]{2,1,0:T(8,128)S(1)}, f32[8,16,256]{2,1,0:T(8,128)S(1)}, u32[]{:S(2)}, u32[]{:S(2)}) collective-permute-start(f32[8,16,256]{2,1,0:T(8,128)S(1)} %pad_maximum_fusion), channel_id=1, source_target_pairs={{0,4},{4,0},{1,5},{5,1},{2,6},{6,2},{3,7},{7,3},{8,12},{12,8},{9,1... | collective-permute-start | bytes 393224 | tf_op jit(solution)/shard_map/ppermute | solution.py:532
  30.7 4.4 %collective-permute-done.31.ends = f32[8,16,256]{2,1,0:T(8,128)S(1)} collective-permute-done((f32[8,16,256]{2,1,0:T(8,128)S(1)}, f32[8,16,256]{2,1,0:T(8,128)S(1)}, u32[]{:S(2)}, u32[]{:S(2)}) %collective-permute-start.31) | collective-permute-done | bytes 131104 | tf_op jit(solution)/shard_map/ppermute | solution.py:532
  35.2 1.2 %collective-permute-start.32 = (f32[64,4,256]{2,1,0:T(4,128)S(1)}, f32[64,4,256]{2,1,0:T(4,128)}, u32[]{:S(2)}, u32[]{:S(2)}) collective-permute-start(f32[64,4,256]{2,1,0:T(4,128)S(1)} %get-tuple-element.306), channel_id=1, source_target_pairs={{0,1},{1,2},{2,3},{3,0},{4,5},{5,6},{6,7},{7,4},{8,9},{9,10},{10,1... | collective-permute-start | bytes 786440 | tf_op jit(solution)/shard_map/ppermute | solution.py:543
  36.4 2.7 %collective-permute-start.33 = (f32[64,4,256]{2,1,0:T(4,128)S(1)}, f32[64,4,256]{2,1,0:T(4,128)}, u32[]{:S(2)}, u32[]{:S(2)}) collective-permute-start(f32[64,4,256]{2,1,0:T(4,128)S(1)} %get-tuple-element.307), channel_id=1, source_target_pairs={{0,3},{1,0},{2,1},{3,2},{4,7},{5,4},{6,5},{7,6},{8,11},{9,8},{10,9... | collective-permute-start | bytes 786440 | tf_op jit(solution)/shard_map/ppermute | solution.py:544
  40.4 6.0 %collective-permute-done.32 = f32[64,4,256]{2,1,0:T(4,128)} collective-permute-done((f32[64,4,256]{2,1,0:T(4,128)S(1)}, f32[64,4,256]{2,1,0:T(4,128)}, u32[]{:S(2)}, u32[]{:S(2)}) %collective-permute-start.32) | collective-permute-done | bytes 262176 | tf_op jit(solution)/shard_map/ppermute | solution.py:543
  46.3 3.4 %collective-permute-done.33 = f32[64,4,256]{2,1,0:T(4,128)} collective-permute-done((f32[64,4,256]{2,1,0:T(4,128)S(1)}, f32[64,4,256]{2,1,0:T(4,128)}, u32[]{:S(2)}, u32[]{:S(2)}) %collective-permute-start.33) | collective-permute-done | bytes 262176 | tf_op jit(solution)/shard_map/ppermute | solution.py:544
  49.7 59.1 %conditional.1 = (f32[1,128,16,256]{3,2,1,0:T(8,128)}) conditional(s32[]{:T(128)} %clamp.3, (f32[32,16,256]{2,1,0:T(8,128)S(1)}, f32[32,16,256]{2,1,0:T(8,128)}, bf16[256,512]{1,0:T(8,128)(2,1)}, bf16[256,512]{1,0:T(8,128)(2,1)}, s32[1]{0:T(128)}, /*index=5*/f32[2,4]{1,0:T(2,128)S(1)}, s32[1]{0:T(128)}, ...), branch_computations={%region_1.2_spmd, %region_2.3_spmd, %region_3.4_spmd, %region_4.5_... | conditional | bytes 30409224 | solution.py:596
  50.5 2.1 %pack.12 = f32[512,384]{1,0:T(8,128)S(1)} custom-call(f32[32,16,256]{2,1,0:T(8,128)} %copy-done.2, f32[32,16,256]{2,1,0:T(8,128)} %get-tuple-element.235.other.refs_2_, bf16[256,512]{1,0:T(8,128)(2,1)} %get-tuple-element.236.refs_0_, bf16[256,512]{1,0:T(8,128)(2,1)} %get-tuple-element.237.refs_1_), custom_call_target="tpu_custom_call" | custom-call | tf_op jit(solution)/shard_map/cond/branch_2_fun/pack/pallas_call | solution.py:392
  52.7 9.7 %sections.7 = (f32[32,16,256]{2,1,0:T(8,128)S(1)}, f32[32,16,256]{2,1,0:T(8,128)S(1)}) custom-call(s32[1]{0:T(128)} %get-tuple-element.238.refs_0_, s32[1]{0:T(128)} %get-tuple-element.231.refs_1_.core, s32[4]{0:T(128)S(1)} %get-tuple-element.239.refs_2_, f32[8]{0:T(128)S(1)} %reshape.163.refs_3_, f32[1]{0:T(128)} %get-tuple-element.241.refs_4_, ...), custom_call_target="tpu_custom_call" | custom-call | tf_op jit(solution)/shard_map/cond/branch_2_fun/sections/pallas_call | solution.py:361
  62.5 1.6 %collective-permute-start.19 = (f32[512,384]{1,0:T(8,128)S(1)}, f32[512,384]{1,0:T(8,128)S(1)}, u32[]{:S(2)}, u32[]{:S(2)}) collective-permute-start(f32[512,384]{1,0:T(8,128)S(1)} %pack.12), channel_id=1, source_target_pairs={{0,16},{8,24},{16,0},{24,8},{1,17},{9,25},{17,1},{25,9},{2,18},{10... | collective-permute-start | bytes 2359304 | tf_op jit(solution)/shard_map/cond/branch_2_fun/ppermute | solution.py:561
  65.1 1.6 %collective-permute-start.16 = (f32[512,384]{1,0:T(8,128)S(1)}, f32[512,384]{1,0:T(8,128)S(1)}, u32[]{:S(2)}, u32[]{:S(2)}) collective-permute-start(f32[512,384]{1,0:T(8,128)S(1)} %pack.13), channel_id=1, source_target_pairs={{0,16},{8,24},{16,0},{24,8},{1,17},{9,25},{17,1},{25,9},{2,18},{10... | collective-permute-start | bytes 2359304 | tf_op jit(solution)/shard_map/cond/branch_2_fun/ppermute | solution.py:561
  66.7 16.3 %collective-permute-done.19.refs_5_ = f32[512,384]{1,0:T(8,128)S(1)} collective-permute-done((f32[512,384]{1,0:T(8,128)S(1)}, f32[512,384]{1,0:T(8,128)S(1)}, u32[]{:S(2)}, u32[]{:S(2)}) %collective-permute-start.19) | collective-permute-done | bytes 786464 | tf_op jit(solution)/shard_map/cond/branch_2_fun/ppermute | solution.py:561
  83.0 16.3 %collective-permute-done.16.refs_0_ = f32[512,384]{1,0:T(8,128)S(1)} collective-permute-done((f32[512,384]{1,0:T(8,128)S(1)}, f32[512,384]{1,0:T(8,128)S(1)}, u32[]{:S(2)}, u32[]{:S(2)}) %collective-permute-start.16) | collective-permute-done | bytes 786464 | tf_op jit(solution)/shard_map/cond/branch_2_fun/ppermute | solution.py:561
  99.8 2.5 %collective-permute-done.15.refs_3_ = f32[32,16,256]{2,1,0:T(8,128)S(1)} collective-permute-done((f32[32,16,256]{2,1,0:T(8,128)S(1)}, f32[32,16,256]{2,1,0:T(8,128)S(1)}, u32[]{:S(2)}, u32[]{:S(2)}) %collective-permute-start.15) | collective-permute-done | bytes 524320 | tf_op jit(solution)/shard_map/cond/branch_2_fun/ppermute | solution.py:562
  103.1 3.2 %finish.6.refs_2_ = f32[128,16,256]{2,1,0:T(8,128)} custom-call(s32[1]{0:T(128)} %get-tuple-element.231.refs_1_.core, f32[1]{0:T(128)} %get-tuple-element.232.weight, f32[32,16,256]{2,1,0:T(8,128)S(1)} %copy-done.3, f32[32,16,256]{2,1,0:T(8,128)} %get-tuple-element.256.refs_1_, f32[32,16,256]{2,1,0:T(8,128)} %get-tuple-element.235.other.refs_2_, ...), custom_call_target="tpu_custom_call" | custom-call | tf_op jit(solution)/shard_map/cond/branch_2_fun/finish/pallas_call | solution.py:447
  106.3 1.2 %add_messages.12.refs_2_ = f32[128,16,256]{2,1,0:T(8,128)} custom-call(s32[1]{0:T(128)} %get-tuple-element.231.refs_1_.core, f32[32,16,256]{2,1,0:T(8,128)S(1)} %get-tuple-element.255.current, f32[512,384]{1,0:T(8,128)S(1)} %collective-permute-done.16.refs_0_, ...), custom_call_target="tpu_custom_call", output_to_operand_aliasing={{}: (4, {})} | custom-call | tf_op jit(solution)/shard_map/cond/branch_2_fun/add_messages/pallas_call | solution.py:489
  107.5 1.2 %add_messages.13 = f32[128,16,256]{2,1,0:T(8,128)} custom-call(s32[1]{0:T(128)} %get-tuple-element.231.refs_1_.core, f32[32,16,256]{2,1,0:T(8,128)S(1)} %get-tuple-element.253.current, f32[512,384]{1,0:T(8,128)S(1)} %collective-permute-done.17.refs_0_, bf16[512,256]{1,0:T(8,128)(2,1)S(1)} %get-tuple-element.254.refs_7_.refs_1_, ...), custom_call_target="tpu_custom_call", output_to_operand_aliasing={{}: (4, {})} | custom-call | tf_op jit(solution)/shard_map/cond/branch_2_fun/add_messages/pallas_call | solution.py:489
  (53 shorter events, 5.7 us)
Async XLA Ops:
  0.0 20.1 %copy-start.1 = (f32[1,128,16,256]{3,2,1,0:T(8,128)S(1)}, f32[1,128,16,256]{3,2,1,0:T(8,128)}, u32[]{:S(2)}) copy-start(f32[1,128,16,256]{3,2,1,0:T(8,128)} %param.9) | copy-start | bytes 6291460
  0.0 6.7 %copy-start.25 = (s32[4]{0:T(128)S(1)}, s32[4]{0:T(128)}, u32[]{:S(2)}) copy-start(s32[4]{0:T(128)} %refs_2_.3) | copy-start | bytes 52
  0.0 8.2 %copy-start.26 = (f32[2,4]{1,0:T(2,128)S(1)}, f32[2,4]{1,0:T(2,128)}, u32[]{:S(2)}) copy-start(f32[2,4]{1,0:T(2,128)} %param.12) | copy-start | bytes 100
  0.0 8.3 %copy-start = (s32[4]{0:T(128)S(1)}, s32[4]{0:T(128)}, u32[]{:S(2)}) copy-start(s32[4]{0:T(128)} %refs_2_.2) | copy-start | bytes 52
  1.5 13.0 %collective-permute-start.28 = (f32[72,4,256]{2,1,0:T(4,128)S(1)}, f32[72,4,256]{2,1,0:T(4,128)S(1)}, u32[]{:S(2)}, u32[]{:S(2)}) collective-permute-start(f32[72,4,256]{2,1,0:T(4,128)S(1)} %get-tuple-element.300), channel_id=1, source_target_pairs={{0,1},{1,2},{2,3},{3,0},{4,5},{5,6},{6,7},{7,4},{8,9},{9,10},{10,1... | collective-permute-start | bytes 884744 | tf_op jit(solution)/shard_map/ppermute | solution.py:529
  4.6 14.8 %collective-permute-start.29 = (f32[72,4,256]{2,1,0:T(4,128)S(1)}, f32[72,4,256]{2,1,0:T(4,128)S(1)}, u32[]{:S(2)}, u32[]{:S(2)}) collective-permute-start(f32[72,4,256]{2,1,0:T(4,128)S(1)} %get-tuple-element.301), channel_id=1, source_target_pairs={{0,3},{1,0},{2,1},{3,2},{4,7},{5,4},{6,5},{7,6},{8,11},{9,8},{10,9... | collective-permute-start | bytes 884744 | tf_op jit(solution)/shard_map/ppermute | solution.py:529
  11.0 25.3 %copy-start.20 = (bf16[256,256]{1,0:T(8,128)(2,1)}, bf16[256,256]{1,0:T(8,128)(2,1)S(1)}, u32[]{:S(2)}) copy-start(bf16[256,256]{1,0:T(8,128)(2,1)S(1)} %get-tuple-element.298.refs_6_) | copy-start | bytes 393220
  11.0 25.3 %copy-start.23 = (bf16[256,256]{1,0:T(8,128)(2,1)}, bf16[256,256]{1,0:T(8,128)(2,1)S(1)}, u32[]{:S(2)}) copy-start(bf16[256,256]{1,0:T(8,128)(2,1)S(1)} %get-tuple-element.299.refs_7_) | copy-start | bytes 393220
  14.5 4.9 %copy-start.18 = (f32[72,4,256]{2,1,0:T(4,128)}, f32[72,4,256]{2,1,0:T(4,128)S(1)}, u32[]{:S(2)}) copy-start(f32[72,4,256]{2,1,0:T(4,128)S(1)} %collective-permute-done.28.refs_8_) | copy-start | bytes 884740
  29.1 20.6 %collective-permute-start.30 = (f32[32,16,256]{2,1,0:T(8,128)}, f32[32,16,256]{2,1,0:T(8,128)}, u32[]{:S(2)}, u32[]{:S(2)}) collective-permute-start(f32[32,16,256]{2,1,0:T(8,128)} %get-tuple-element.303), channel_id=1, source_target_pairs={{0,8},{8,0},{16,24},{24,16},{1,9},{9,1},{17,25},{25,17},{2,10},{10... | collective-permute-start | bytes 1572872 | tf_op jit(solution)/shard_map/ppermute | solution.py:555
  29.2 6.0 %collective-permute-start.31 = (f32[8,16,256]{2,1,0:T(8,128)S(1)}, f32[8,16,256]{2,1,0:T(8,128)S(1)}, u32[]{:S(2)}, u32[]{:S(2)}) collective-permute-start(f32[8,16,256]{2,1,0:T(8,128)S(1)} %pad_maximum_fusion), channel_id=1, source_target_pairs={{0,4},{4,0},{1,5},{5,1},{2,6},{6,2},{3,7},{7,3},{8,12},{12,8},{9,1... | collective-permute-start | bytes 393224 | tf_op jit(solution)/shard_map/ppermute | solution.py:532
  35.2 11.1 %collective-permute-start.32 = (f32[64,4,256]{2,1,0:T(4,128)S(1)}, f32[64,4,256]{2,1,0:T(4,128)}, u32[]{:S(2)}, u32[]{:S(2)}) collective-permute-start(f32[64,4,256]{2,1,0:T(4,128)S(1)} %get-tuple-element.306), channel_id=1, source_target_pairs={{0,1},{1,2},{2,3},{3,0},{4,5},{5,6},{6,7},{7,4},{8,9},{9,10},{10,1... | collective-permute-start | bytes 786440 | tf_op jit(solution)/shard_map/ppermute | solution.py:543
  36.4 13.3 %collective-permute-start.33 = (f32[64,4,256]{2,1,0:T(4,128)S(1)}, f32[64,4,256]{2,1,0:T(4,128)}, u32[]{:S(2)}, u32[]{:S(2)}) collective-permute-start(f32[64,4,256]{2,1,0:T(4,128)S(1)} %get-tuple-element.307), channel_id=1, source_target_pairs={{0,3},{1,0},{2,1},{3,2},{4,7},{5,4},{6,5},{7,6},{8,11},{9,8},{10,9... | collective-permute-start | bytes 786440 | tf_op jit(solution)/shard_map/ppermute | solution.py:544
  52.6 11.8 %copy-start.8 = (bf16[256,512]{1,0:T(8,128)(2,1)S(1)}, bf16[256,512]{1,0:T(8,128)(2,1)}, u32[]{:S(2)}) copy-start(bf16[256,512]{1,0:T(8,128)(2,1)} %get-tuple-element.236.refs_0_) | copy-start | bytes 786436 | tf_op jit(solution)/shard_map/cond
  52.7 11.7 %copy-start.12 = (bf16[256,512]{1,0:T(8,128)(2,1)S(1)}, bf16[256,512]{1,0:T(8,128)(2,1)}, u32[]{:S(2)}) copy-start(bf16[256,512]{1,0:T(8,128)(2,1)} %get-tuple-element.237.refs_1_) | copy-start | bytes 786436 | tf_op jit(solution)/shard_map/cond
  52.7 47.1 %copy-start.3 = (f32[32,16,256]{2,1,0:T(8,128)S(1)}, f32[32,16,256]{2,1,0:T(8,128)}, u32[]{:S(2)}) copy-start(f32[32,16,256]{2,1,0:T(8,128)} %copy-done.2) | copy-start | bytes 1572868 | tf_op jit(solution)/shard_map/cond
  52.7 49.6 %copy-start.16 = (bf16[256,256]{1,0:T(8,128)(2,1)S(1)}, bf16[256,256]{1,0:T(8,128)(2,1)}, u32[]{:S(2)}) copy-start(bf16[256,256]{1,0:T(8,128)(2,1)} %get-tuple-element.252.refs_4_) | copy-start | bytes 393220 | tf_op jit(solution)/shard_map/cond
  62.4 2.0 %collective-permute-start.14 = (f32[32,16,256]{2,1,0:T(8,128)S(1)}, f32[32,16,256]{2,1,0:T(8,128)S(1)}, u32[]{:S(2)}, u32[]{:S(2)}) collective-permute-start(f32[32,16,256]{2,1,0:T(8,128)S(1)} %get-tuple-element.251.refs_1_), channel_id=1, source_target_pairs={{0,8},{8,0},{16,24},{24,16},{1,9},{9,1},{17,25},{25,17},{2,10},{10... | collective-permute-start | bytes 1572872 | tf_op jit(solution)/shard_map/cond/branch_2_fun/ppermute | solution.py:555
  62.5 20.5 %collective-permute-start.19 = (f32[512,384]{1,0:T(8,128)S(1)}, f32[512,384]{1,0:T(8,128)S(1)}, u32[]{:S(2)}, u32[]{:S(2)}) collective-permute-start(f32[512,384]{1,0:T(8,128)S(1)} %pack.12), channel_id=1, source_target_pairs={{0,16},{8,24},{16,0},{24,8},{1,17},{9,25},{17,1},{25,9},{2,18},{10... | collective-permute-start | bytes 2359304 | tf_op jit(solution)/shard_map/cond/branch_2_fun/ppermute | solution.py:561
  65.1 34.2 %collective-permute-start.16 = (f32[512,384]{1,0:T(8,128)S(1)}, f32[512,384]{1,0:T(8,128)S(1)}, u32[]{:S(2)}, u32[]{:S(2)}) collective-permute-start(f32[512,384]{1,0:T(8,128)S(1)} %pack.13), channel_id=1, source_target_pairs={{0,16},{8,24},{16,0},{24,8},{1,17},{9,25},{17,1},{25,9},{2,18},{10... | collective-permute-start | bytes 2359304 | tf_op jit(solution)/shard_map/cond/branch_2_fun/ppermute | solution.py:561
  83.0 20.1 %collective-permute-start.20 = (f32[512,384]{1,0:T(8,128)S(1)}, f32[512,384]{1,0:T(8,128)S(1)}, u32[]{:S(2)}, u32[]{:S(2)}) collective-permute-start(f32[512,384]{1,0:T(8,128)S(1)} %collective-permute-done.19.refs_5_), channel_id=1, source_target_pairs={{0,8},{8,0},{16,24},{24,16},{1,9},{9,1},{17,25},{25,17},{2,10},{10... | collective-permute-start | bytes 2359304 | tf_op jit(solution)/shard_map/cond/branch_2_fun/ppermute | solution.py:577
  99.3 8.2 %collective-permute-start.17 = (f32[512,384]{1,0:T(8,128)S(1)}, f32[512,384]{1,0:T(8,128)S(1)}, u32[]{:S(2)}, u32[]{:S(2)}) collective-permute-start(f32[512,384]{1,0:T(8,128)S(1)} %collective-permute-done.16.refs_0_), channel_id=1, source_target_pairs={{0,8},{8,0},{16,24},{24,16},{1,9},{9,1},{17,25},{25,17},{2,10},{10... | collective-permute-start | bytes 2359304 | tf_op jit(solution)/shard_map/cond/branch_2_fun/ppermute | solution.py:577
  99.3 3.0 %collective-permute-start.15 = (f32[32,16,256]{2,1,0:T(8,128)S(1)}, f32[32,16,256]{2,1,0:T(8,128)S(1)}, u32[]{:S(2)}, u32[]{:S(2)}) collective-permute-start(f32[32,16,256]{2,1,0:T(8,128)S(1)} %get-tuple-element.250.refs_0_.mine), channel_id=1, source_target_pairs={{0,8},{8,0},{16,24},{24,16},{1,9},{9,1},{17,25},{25,17},{2,10},{10... | collective-permute-start | bytes 1572872 | tf_op jit(solution)/shard_map/cond/branch_2_fun/ppermute | solution.py:562
  99.8 3.3 %collective-permute-start.18 = (f32[32,16,256]{2,1,0:T(8,128)S(1)}, f32[32,16,256]{2,1,0:T(8,128)S(1)}, u32[]{:S(2)}, u32[]{:S(2)}) collective-permute-start(f32[32,16,256]{2,1,0:T(8,128)S(1)} %copy-done.3), channel_id=1, source_target_pairs={{0,8},{8,0},{16,24},{24,16},{1,9},{9,1},{17,25},{25,17},{2,10},{10... | collective-permute-start | bytes 1572872 | tf_op jit(solution)/shard_map/cond/branch_2_fun/ppermute | solution.py:562
  (4 other events, 4.9 us)

commit v2 on v1

--- a/solution.py
+++ b/solution.py
@@ -136,28 +136,35 @@
     level_other = levels[other]
     weight = weights[mine].astype(F32)
     weight_other = weights[other].astype(F32)
-    rows = lax.broadcasted_iota(jnp.int32, (flat, flat), 0)
-    columns = lax.broadcasted_iota(jnp.int32, (flat, flat), 1)
     dif, cou = grid_numbers(rates, level)
     width = jnp.left_shift(jnp.int32(1), LEVEL_SUM - level)
-    row4 = jnp.bitwise_and(rows, width - 1)
+    part = 32
+    columns = lax.broadcasted_iota(jnp.int32, (part, flat), 1)
     column4 = jnp.bitwise_and(columns, width - 1)
-    same3 = (rows - row4) == (columns - column4)
-    step = jnp.where(jnp.bitwise_and(columns + width, flat - 1) == rows, dif[2], 0.0)
-    step = step + jnp.where(jnp.bitwise_and(columns - width, flat - 1) == rows, dif[2] + cou[2], 0.0)
-    up4 = jnp.logical_and(same3, jnp.bitwise_and(column4 + 1, width - 1) == row4)
-    down4 = jnp.logical_and(same3, jnp.bitwise_and(column4 - 1, width - 1) == row4)
-    step = step + jnp.where(up4, dif[3], 0.0)
-    step = step + jnp.where(down4, dif[3] + cou[3], 0.0)
-    head, tail = split(step)
-    head_out[...] = head
-    tail_out[...] = tail
-
-    node3, node4 = cell_places(rows, level_other)
     cell3, cell4 = cell_places(columns, level)
-    linear = linear_weight(cell3, node3, level, level_other)
-    linear = linear * linear_weight(cell4, node4, LEVEL_SUM - level, LEVEL_SUM - level_other)
-    partner_out[...] = (linear * weight_other).astype(BF16)
+
+    def square(i, carry):
+        at = pl.multiple_of(i * part, part)
+        rows = at + lax.broadcasted_iota(jnp.int32, (part, flat), 0)
+        row4 = jnp.bitwise_and(rows, width - 1)
+        same3 = (rows - row4) == (columns - column4)
+        step = jnp.where(jnp.bitwise_and(columns + width, flat - 1) == rows, dif[2], 0.0)
+        down3 = jnp.bitwise_and(columns - width, flat - 1) == rows
+        step = step + jnp.where(down3, dif[2] + cou[2], 0.0)
+        up4 = jnp.logical_and(same3, jnp.bitwise_and(column4 + 1, width - 1) == row4)
+        down4 = jnp.logical_and(same3, jnp.bitwise_and(column4 - 1, width - 1) == row4)
+        step = step + jnp.where(up4, dif[3], 0.0)
+        step = step + jnp.where(down4, dif[3] + cou[3], 0.0)
+        head, tail = split(step)
+        head_out[pl.ds(at, part)] = head
+        tail_out[pl.ds(at, part)] = tail
+        node3, node4 = cell_places(rows, level_other)
+        linear = linear_weight(cell3, node3, level, level_other)
+        linear = linear * linear_weight(cell4, node4, LEVEL_SUM - level, LEVEL_SUM - level_other)
+        partner_out[pl.ds(at, part)] = (linear * weight_other).astype(BF16)
+        return carry
+
+    lax.fori_loop(0, flat // part, square, 0)
 
     slots = 2 * flat
     for shift in range(1, chips):
@@ -165,9 +172,7 @@
         target = lax.rem(chip + shift, jnp.int32(chips))
         source = lax.rem(chip + chips - shift, jnp.int32(chips))
         betas = staircase((level, level_other), (levels[2 * target], levels[2 * target + 1]))
-        row = lax.broadcasted_iota(jnp.int32, (1, slots), 1)
-        cell = lax.broadcasted_iota(jnp.int32, (flat, 1), 0)
-        place3, place4, used = slot_places(row, betas)
+        place3, place4, used = slot_places(lax.broadcasted_iota(jnp.int32, (1, slots), 1), betas)
         for out, grid_level, grid_weight in (
             (own_out, level, weight),
             (other_out, level_other, weight_other),
@@ -175,17 +180,30 @@
             kept = jnp.where(
                 jnp.logical_and(used, held(place3, place4, grid_level)), grid_weight, 0.0
             )
-            cell3, cell4 = cell_places(cell, grid_level)
-            value = surplus_weight(cell3, place3) * surplus_weight(cell4, place4) * kept
-            out[...] = value.astype(BF16)
+
+            def message(i, carry, out=out, grid_level=grid_level, kept=kept):
+                at = pl.multiple_of(i * part, part)
+                cell = at + lax.broadcasted_iota(jnp.int32, (part, 1), 0)
+                third, fourth = cell_places(cell, grid_level)
+                value = surplus_weight(third, place3) * surplus_weight(fourth, place4) * kept
+                out[pl.ds(at, part)] = value.astype(BF16)
+                return carry
+
+            lax.fori_loop(0, flat // part, message, 0)
         betas = staircase((level, level_other), (levels[2 * source], levels[2 * source + 1]))
-        row = lax.broadcasted_iota(jnp.int32, (slots, 1), 0)
-        cell = lax.broadcasted_iota(jnp.int32, (1, flat), 1)
-        place3, place4, used = slot_places(row, betas)
-        kept = jnp.where(jnp.logical_and(used, held(place3, place4, level)), 1.0, 0.0)
-        cell3, cell4 = cell_places(cell, level)
-        value = hat_weight(cell3, place3) * hat_weight(cell4, place4) * kept
-        back_out[...] = value.astype(BF16)
+
+        def answer(i, carry, betas=betas, back_out=back_out):
+            at = pl.multiple_of(i * part, part)
+            place3, place4, used = slot_places(
+                at + lax.broadcasted_iota(jnp.int32, (part, 1), 0), betas
+            )
+            kept = jnp.where(jnp.logical_and(used, held(place3, place4, level)), 1.0, 0.0)
+            third, fourth = cell_places(lax.broadcasted_iota(jnp.int32, (1, flat), 1), level)
+            value = hat_weight(third, place3) * hat_weight(fourth, place4) * kept
+            back_out[pl.ds(at, part)] = value.astype(BF16)
+            return carry
+
+        lax.fori_loop(0, slots // part, answer, 0)
 
 
 def setup_tables(flat, chips, place, levels, weights, rates):
@@ -200,7 +218,28 @@
         out_specs=[VMEM] * len(shapes),
         compiler_params=ROOM,
         name="tables",
-    )(place, levels, weights, rates.reshape(-1))
+    )(place, levels, weights, rates)
+
+
+def choose_room(chips, levels):
+    def kernel(levels, out):
+        most = jnp.int32(1)
+        for one in range(chips):
+            for other in range(one + 1, chips):
+                betas = staircase(
+                    (levels[2 * one], levels[2 * one + 1]), (levels[2 * other], levels[2 * other + 1])
+                )
+                most = jnp.maximum(most, sum(stair_counts(betas)))
+        out[0] = jnp.right_shift(most - 1, LANES.bit_length() - 1)
+
+    return pl.pallas_call(
+        kernel,
+        out_shape=jax.ShapeDtypeStruct((1,), jnp.int32),
+        in_specs=[SMEM],
+        out_specs=SMEM,
+        compiler_params=ROOM,
+        name="room",
+    )(levels)[0]
 
 
 def faces(block, start, count):
@@ -226,10 +265,10 @@
     )(block)
 
 
-def outer_faces(block, ends):
+def outer_faces(block, ends, side):
     long, own, flat = block.shape
     halo = SECTIONS
-    span = long // 4 - halo
+    span = side - halo
 
     def kernel(block, ends, low, high):
         for out, columns in ((low, slice(own - halo, own)), (high, slice(0, halo))):
@@ -238,10 +277,10 @@
             out[halo + span : halo + 2 * span] = block[long - span :, columns]
             out[halo + 2 * span :] = ends[halo:, columns]
 
-    side = jax.ShapeDtypeStruct((long // 2, halo, flat), F32)
+    columns = jax.ShapeDtypeStruct((2 * side, halo, flat), F32)
     return pl.pallas_call(
         kernel,
-        out_shape=[side, side],
+        out_shape=[columns, columns],
         in_specs=[VMEM] * 2,
         out_specs=[VMEM] * 2,
         compiler_params=ROOM,
@@ -249,34 +288,40 @@
     )(block, ends)
 
 
-def chunk_plans(long):
+def chunk_plans(long, cap, flat):
     halo = SECTIONS
-    quarter = long // 4
-    wide = long // 2 + 2 * halo
-    piece = quarter + 2 * halo
+    share = 8 if cap <= flat else 7 if 2 * cap <= 3 * flat else 6
+    first = share * (long // 16)
+    side = (long - first) // 2
+    wide = first + 2 * halo
+    piece = side + 2 * halo
     return [
         {
-            "own": [(None, quarter - halo, 0, wide)],
+            "start": side,
+            "half": first // 2,
+            "own": [(None, side - halo, 0, wide)],
             "edge": [(0, 0, 0, wide)],
-            "start": quarter,
-            "rows": wide,
-            "pitch": quarter,
+            "pieces": 1,
+            "piece": wide,
+            "pitch": first // 2,
         },
         {
+            "start": long - side,
+            "half": side,
             "own": [
-                (None, long - quarter - halo, 0, quarter + halo),
-                ("ends", halo, quarter + halo, halo),
+                (None, long - side - halo, 0, side + halo),
+                ("ends", halo, side + halo, halo),
                 ("ends", 0, piece, halo),
-                (None, 0, piece + halo, quarter + halo),
+                (None, 0, piece + halo, side + halo),
             ],
             "edge": [
                 (0, wide - 2 * halo, 0, 2 * halo),
-                (1, quarter, 2 * halo, quarter),
-                (1, 0, piece, quarter),
-                (0, 0, piece + quarter, 2 * halo),
+                (1, side, 2 * halo, side),
+                (1, 0, piece, side),
+                (0, 0, piece + side, 2 * halo),
             ],
-            "start": long - quarter,
-            "rows": 2 * piece,
+            "pieces": 2,
+            "piece": piece,
             "pitch": piece,
         },
     ]
@@ -330,15 +375,18 @@
         value = value + dif[1] * ahead + (dif[1] + cou[1]) * behind
         return value + inner.reshape(step, depth, flat)
 
-    step = (plan["rows"] - 2) // 2
+    step = (plan["piece"] - 2) // 2
+    shift = plan["pieces"]
 
     def body(i, carry):
-        which = jnp.bitwise_and(jnp.right_shift(i, 1), 1)
+        which = jnp.bitwise_and(jnp.right_shift(i, shift), 1)
         at = 1 + step * jnp.bitwise_and(i, 1)
+        if plan["pieces"] == 2:
+            at = at + plan["piece"] * jnp.bitwise_and(jnp.right_shift(i, 1), 1)
         state[1 - which, pl.ds(at, step)] = block(which, at, tall, step)
         return carry
 
-    lax.fori_loop(0, 2 * (SECTIONS - 1), body, 0)
+    lax.fori_loop(0, 2 * plan["pieces"] * (SECTIONS - 1), body, 0)
     last = keep.shape[0] // 2
     for side, out in enumerate((keep, give)):
         base = halo + plan["pitch"] * jnp.bitwise_xor(core[0], side)
@@ -351,25 +399,25 @@
 
 
 def stencil(plan, place, core, levels, rates, reaction, field, edges, ends, head, tail):
-    long, own, flat = field.shape
+    _, own, flat = field.shape
     halo = SECTIONS
     order = sorted({source for source, *_ in plan["edge"]})
     operands = [head, tail] + [ref for source in order for ref in edges[source]]
     operands += [ends] if plan["own"][1:] else []
     straight = sum(source is None for source, *_ in plan["own"])
-    half = jax.ShapeDtypeStruct((long // 4, own, flat), F32)
+    half = jax.ShapeDtypeStruct((plan["half"], own, flat), F32)
     return pl.pallas_call(
         lambda *refs: stencil_kernel(plan, order, *refs),
         out_shape=[half, half],
         in_specs=[SMEM] * 5 + [ANY] + [VMEM] * len(operands),
         out_specs=[VMEM, VMEM],
         scratch_shapes=[
-            pltpu.VMEM((2, plan["rows"], own + 2 * halo, flat), F32),
+            pltpu.VMEM((2, plan["pieces"] * plan["piece"], own + 2 * halo, flat), F32),
             pltpu.SemaphoreType.DMA((straight,)),
         ],
         compiler_params=ROOM,
         name="sections",
-    )(place, core, levels, rates.reshape(-1), reaction, field, *operands)
+    )(place, core, levels, rates, reaction, field, *operands)
 
 
 def pack(cap, values, others, tables):
@@ -421,24 +469,25 @@
     return copies
 
 
-def finish(cap, start, core, weight, values, others, partner, near, far, backs, carry, shape):
+def finish(cap, start, core, place, weights, values, others, partner, near, far, backs, carry, shape):
     count, own, flat = values[0].shape
     parts = len(backs)
 
-    def kernel(core, weight, *refs):
+    def kernel(core, place, weights, *refs):
+        weight = weights[place[0]].astype(F32)
         back_refs = [ref[:cap] for ref in refs[5 + 2 * parts : 5 + 3 * parts]]
         out, rows, sems = refs[-3:]
         copies = write_rows(start, (0, 1), core, out, rows, sems)
         for side in range(2):
-            value = shares(weight[0], refs[side][...], refs[2 + side][...], refs[4][...])
+            value = shares(weight, refs[side][...], refs[2 + side][...], refs[4][...])
             messages = [ref[...] for ref in refs[5 + side * parts : 5 + (side + 1) * parts]]
             rows[side] = received(value, messages, back_refs).reshape(count, own, flat)
             copies[side].start()
         for copy in copies:
             copy.wait()
 
-    operands = [core, weight, *values, *others, partner, *near, *far, *backs]
-    specs = [SMEM] * 2 + [VMEM] * (5 + 3 * parts)
+    operands = [core, place, weights, *values, *others, partner, *near, *far, *backs]
+    specs = [SMEM] * 3 + [VMEM] * (5 + 3 * parts)
     aliases = {}
     if carry is not None:
         aliases = {len(operands): 0}
@@ -456,21 +505,22 @@
     )(*operands)
 
 
-def base(weight, values, others, partner):
-    def kernel(weight, *refs):
+def base(place, weights, values, others, partner):
+    def kernel(place, weights, *refs):
+        weight = weights[place[0]].astype(F32)
         for side in range(2):
-            value = shares(weight[0], refs[side][...], refs[2 + side][...], refs[4][...])
+            value = shares(weight, refs[side][...], refs[2 + side][...], refs[4][...])
             refs[5 + side][...] = value.reshape(values[0].shape)
 
     half = jax.ShapeDtypeStruct(values[0].shape, F32)
     return pl.pallas_call(
         kernel,
         out_shape=[half, half],
-        in_specs=[SMEM] + [VMEM] * 5,
+        in_specs=[SMEM] * 2 + [VMEM] * 5,
         out_specs=[VMEM] * 2,
         compiler_params=ROOM,
         name="base",
-    )(weight, *values, *others, partner)
+    )(place, weights, *values, *others, partner)
 
 
 def add_messages(cap, start, side, core, current, messages, backs, carry):
@@ -498,35 +548,43 @@
     )(core, current, *messages, *backs, carry)
 
 
-def slots_needed(third_level, chips):
-    levels = third_level.reshape(chips, 2)
-    most = jnp.int32(0)
-    for shift in range(1, chips):
-        shifted = jnp.roll(levels, -shift, axis=0)
-        betas = staircase(
-            (levels[:, 0], levels[:, 1]), (shifted[:, 0], shifted[:, 1])
-        )
-        most = jnp.maximum(most, jnp.max(sum(stair_counts(betas))))
-    return most
-
-
 def local(sizes, field, third_level, coefficients, rates, reaction):
-    block = field[0]
-    long, _, flat = block.shape
+    chips = sizes["comp"] // 2
+    flat = field.shape[-1]
+    rates = rates.reshape(-1)
+    place = lax.axis_index("comp").reshape(1).astype(jnp.int32)
+
+    def branch(cap):
+        return lambda *args: run(sizes, cap, *args)
+
+    caps = list(range(LANES, 2 * flat + 1, LANES))
+    return lax.switch(
+        choose_room(chips, third_level),
+        [branch(cap) for cap in caps],
+        field[0], place, third_level, coefficients, rates, reaction,
+    )[None]
+
+
+def run(sizes, cap, block, place, third_level, coefficients, rates, reaction):
+    shape = block.shape
+    long, _, flat = shape
     halo = SECTIONS
     chips = sizes["comp"] // 2
-    mine = lax.axis_index("comp")
-    place = mine.reshape(1).astype(jnp.int32)
     core = jnp.bitwise_and(place, 1)
-    weight = lax.dynamic_index_in_dim(coefficients, mine, 0, True).astype(F32)
     swap = [(i, i ^ 1) for i in range(sizes["comp"])]
     forward = {axis: ring(sizes[axis], 1) for axis in ("gx", "gy")}
     backward = {axis: ring(sizes[axis], -1) for axis in ("gx", "gy")}
-
-    shape = block.shape
-    plans = chunk_plans(long)
-    low_one, high_one = faces(block, plans[0]["start"] - halo, plans[0]["rows"])
-    one = (lax.ppermute(low_one, "gy", forward["gy"]), lax.ppermute(high_one, "gy", backward["gy"]))
+    shifts = [
+        [(2 * h + c, 2 * ((h + r) % chips) + c) for h in range(chips) for c in range(2)]
+        for r in range(1, chips)
+    ]
+    plans = chunk_plans(long, cap, flat)
+
+    low_one, high_one = faces(block, plans[0]["start"] - halo, plans[0]["piece"])
+    one = (
+        lax.ppermute(low_one, "gy", forward["gy"]),
+        lax.ppermute(high_one, "gy", backward["gy"]),
+    )
     first_rows, last_rows = block[:halo], block[long - halo :]
     if sizes["gx"] == 2:
         ends = lax.ppermute(jnp.concatenate([last_rows, first_rows]), "gx", forward["gx"])
@@ -534,68 +592,51 @@
         before = lax.ppermute(last_rows, "gx", forward["gx"])
         after = lax.ppermute(first_rows, "gx", backward["gx"])
         ends = jnp.concatenate([before, after])
-    branch = lax.div(slots_needed(third_level, chips) - 1, jnp.int32(LANES))
     tables = setup_tables(flat, chips, place, third_level, coefficients, rates)
     head, tail, partner = tables[:3]
     pairs = [(tables[3 * r], tables[3 * r + 1]) for r in range(1, chips)]
     backs = [tables[3 * r + 2] for r in range(1, chips)]
-    low_two, high_two = outer_faces(block, ends)
+    low_two, high_two = outer_faces(block, ends, plans[1]["half"])
     low_two = lax.ppermute(low_two, "gy", forward["gy"])
     high_two = lax.ppermute(high_two, "gy", backward["gy"])
     edges = [one, (low_two, high_two)]
-
-    shifts = [
-        [(2 * h + c, 2 * ((h + r) % chips) + c) for h in range(chips) for c in range(2)]
-        for r in range(1, chips)
-    ]
     scalars = (core, third_level, rates, reaction, block)
 
-    def evolve(k, place, edges, ends):
+    def evolve(k, place):
         values = stencil(plans[k], place, *scalars, edges, ends, head, tail)
         return values, lax.ppermute(values[1], "comp", swap)
 
-    def send(cap, values, other):
+    def send(values, other):
         sent = pack(cap, values[0], other, pairs)
         near = []
         for message, shift in zip(sent, shifts):
             near.append(lax.ppermute(message, "comp", shift))
         return sent[0], near, (other, lax.ppermute(values[0], "comp", swap))
 
-    ready = lax.optimization_barrier((place, branch, partner))[0]
-    values_0, other_0 = evolve(0, ready, edges, None)
-
-    def tail_of(cap):
-        def run(values_0, other_0, edges, ends):
-            sent, near_0, others_0 = send(cap, values_0, other_0)
-            ready = lax.optimization_barrier((place, sent))[0]
-            values_1, other_1 = evolve(1, ready, edges, ends)
-            _, near_1, others_1 = send(cap, values_1, other_1)
-
-            def back(near):
-                far = []
-                for message in near:
-                    far.append(lax.ppermute(message, "comp", swap))
-                return far
-
-            halves = base(weight, values_1, others_1, partner)
-            far_0 = back(near_0)
-            result = finish(
-                cap, plans[0]["start"], core, weight, values_0, others_0, partner,
-                near_0, far_0, backs, None, shape,
-            )
-            far_1 = back(near_1)
-            for side, messages in enumerate((near_1, far_1)):
-                result = add_messages(
-                    cap, plans[1]["start"], side, core, halves[side], messages, backs, result
-                )
-            return result
-
-        return run
-
-    caps = list(range(LANES, 2 * flat + 1, LANES))
-    return lax.switch(
-        branch, [tail_of(cap) for cap in caps], values_0, other_0, edges, ends
-    )[None]
+    def back(near):
+        far = []
+        for message in near:
+            far.append(lax.ppermute(message, "comp", swap))
+        return far
+
+    ready = lax.optimization_barrier((place, partner))[0]
+    values_0, other_0 = evolve(0, ready)
+    sent, near_0, others_0 = send(values_0, other_0)
+    ready = lax.optimization_barrier((place, sent))[0]
+    values_1, other_1 = evolve(1, ready)
+    _, near_1, others_1 = send(values_1, other_1)
+    halves = base(place, coefficients, values_1, others_1, partner)
+    far_0 = back(near_0)
+    result = finish(
+        cap, plans[0]["start"], core, place, coefficients, values_0, others_0, partner,
+        near_0, far_0, backs, None, shape,
+    )
+    far_1 = back(near_1)
+    for side, messages in enumerate((near_1, far_1)):
+        result = add_messages(
+            cap, plans[1]["start"], side, core, halves[side], messages, backs, result
+        )
+    return result
 
 
 def solution(mesh):
@@ -608,8 +649,8 @@
         check_vma=False,
     )
 
-    def run(field, third_level, coefficients, rates, reaction):
+    def whole(field, third_level, coefficients, rates, reaction):
         placed = step
         return placed(field, third_level, coefficients, rates, reaction)
 
-    return run
+    return whole

time: 109 us -> 109 us (level)
  waiting for transfers between devices: 57.1 us -> 62.6 us
  local copies, waits for them, and re-layouts: 2.47 us -> 0.12 us
  between operations: 2.29 us -> 0.88 us
  starting transfers between devices: 14.5 us -> 13.4 us
    ppermute x5, waiting for transfers between devices: 21.4 us -> 23.7 us  [the longest x1 7.2 us: run(): low_two = lax.ppermute(low_two, 'gy', forward['gy'])]
    ppermute x2, waiting for transfers between devices: 32.6 us -> 34.4 us  [send(): near.append(lax.ppermute(message, 'comp', shift))]
    pallas_call x2 -> x3, Pallas kernels: 0.48 us -> 2.3 us  [the longest x1 1.24 us: choose_room(): pl.pallas_call(kernel, out_shape=jax.ShapeDtypeStruct((1,), jnp.int32), i...]
    ppermute x2, waiting for transfers between devices: 0.32 us -> 1.99 us  [evolve(): return (values, lax.ppermute(values[1], 'comp', swap))]
    pallas_call x2, Pallas kernels: 2.81 us -> 1.42 us  [pack(): pl.pallas_call(kernel, out_shape=[jax.ShapeDtypeStruct((count * own, cap)...]
    pallas_call x2, Pallas kernels: 18.7 us -> 17.6 us  [stencil(): pl.pallas_call(lambda *refs: stencil_kernel(plan, order, *refs), out_shap...]
  transfers between devices with their start and end apart: 13 -> 13, of which waited for: 10 -> 9; matrix products, arithmetic and copies ran while one was open for 1% -> 0% of each run, Pallas kernels for 8% -> 8%
where the time goes in v2:
time: 109 us; the launch traced here: 108 us
  waiting for transfers between devices  62.6 us (57%)
  Pallas kernels  30.8 us (28%)
  starting transfers between devices  13.4 us (12%)
    ppermute x2, waiting for transfers between devices, send(): near.append(lax.ppermute(message, 'comp', shift))  34.4 us
    pallas_call x2, Pallas kernels, stencil(): pl.pallas_call(lambda *refs: stencil_kernel(plan, order, *refs), out_shap...  17.6 us
    ppermute x1, waiting for transfers between devices, run(): low_two = lax.ppermute(low_two, 'gy', forward['gy'])  7.2 us
    ppermute x1, waiting for transfers between devices, run(): lax.ppermute(jnp.concatenate([last_rows, first_rows]), 'gx', forward['gx'])  4.41 us
    ppermute x1, waiting for transfers between devices, run(): lax.ppermute(high_one, 'gy', backward['gy'])  4.16 us
    ppermute x1, waiting for transfers between devices, run(): high_two = lax.ppermute(high_two, 'gy', backward['gy'])  4.03 us
    ppermute x1, waiting for transfers between devices, run(): lax.ppermute(low_one, 'gy', forward['gy'])  3.89 us
    pallas_call x1, Pallas kernels, setup_tables(): pl.pallas_call(lambda *refs: setup_kernel(flat, chips, *refs), out_shape=...  3.12 us
  transfers between devices with their start and end apart: 13, of which 9 were waited for; matrix products, arithmetic and copies ran while one was open for 0% of the time, Pallas kernels for 8%

profile of v2, /device:TPU:0, one launch (start us, length us, event | category | flops | bytes accessed | tf_op | source)
XLA Modules:
  0.0 108.4 jit_solution(12396176707316237084)
XLA Ops:
  0.0 1.2 %room.1 = s32[1]{0:T(128)} custom-call(s32[4]{0:T(128)} %levels.1), custom_call_target="tpu_custom_call" | custom-call | tf_op jit(solution)/shard_map/room/pallas_call | solution.py:235
  1.9 106.3 %conditional.1 = (f32[1,128,16,256]{3,2,1,0:T(8,128)}) conditional(s32[]{:T(128)} %bitcast.20, (s32[]{:T(128)}, f32[2,4]{1,0:T(2,128)}, s32[4]{0:T(128)}, s32[4]{0:T(128)}, f32[1,128,16,256]{3,2,1,0:T(8,128)}, /*index=5*/f32[1]{0:T(128)}) %tuple.29, (s32[]{:T(128)}, f32[2,4]{1,0:T(2,128)}, s32[4]{0:T(128)}, ...), branch_computations={%region_0.0_spmd, %region_1.0_spmd, %region_2.0_spmd, %region_3.0_... | conditional | flops 32769 | bytes 39060428 | solution.py:561
  2.2 1.4 %faces.6 = (f32[64,4,256]{2,1,0:T(4,128)S(1)}, f32[64,4,256]{2,1,0:T(4,128)S(1)}) custom-call(f32[128,16,256]{2,1,0:T(8,128)} %bitcast.37), custom_call_target="tpu_custom_call" | custom-call | tf_op jit(solution)/shard_map/cond/branch_2_fun/faces/pallas_call | solution.py:257
  3.6 3.1 %collective-permute-start.26 = (f32[64,4,256]{2,1,0:T(4,128)S(1)}, f32[64,4,256]{2,1,0:T(4,128)S(1)}, u32[]{:S(2)}, u32[]{:S(2)}) collective-permute-start(f32[64,4,256]{2,1,0:T(4,128)S(1)} %get-tuple-element.129), channel_id=1, source_target_pairs={{0,1},{1,2},{2,3},{3,0},{4,5},{5,6},{6,7},{7,4},{8,9},{9,10},{10,1... | collective-permute-start | bytes 786440 | tf_op jit(solution)/shard_map/cond/branch_2_fun/ppermute | solution.py:585
  6.7 2.1 %collective-permute-start.27 = (f32[64,4,256]{2,1,0:T(4,128)S(1)}, f32[64,4,256]{2,1,0:T(4,128)S(1)}, u32[]{:S(2)}, u32[]{:S(2)}) collective-permute-start(f32[64,4,256]{2,1,0:T(4,128)S(1)} %get-tuple-element.130), channel_id=1, source_target_pairs={{0,3},{1,0},{2,1},{3,2},{4,7},{5,4},{6,5},{7,6},{8,11},{9,8},{10,9... | collective-permute-start | bytes 786440 | tf_op jit(solution)/shard_map/cond/branch_2_fun/ppermute | solution.py:586
  8.9 3.1 %tables.6 = (bf16[256,256]{1,0:T(8,128)(2,1)S(1)}, bf16[256,256]{1,0:T(8,128)(2,1)S(1)}, bf16[256,256]{1,0:T(8,128)(2,1)S(1)}, bf16[256,512]{1,0:T(8,128)(2,1)S(...) custom-call(s32[1]{0:T(128)} %bitcast.10.refs_0_.place, s32[4]{0:T(128)S(1)} %copy-done.10, ...), custom_call_target="tpu_custom_call" | custom-call | tf_op jit(solution)/shard_map/cond/branch_2_fun/tables/pallas_call | solution.py:214
  12.1 3.9 %collective-permute-done.26.refs_8_ = f32[64,4,256]{2,1,0:T(4,128)S(1)} collective-permute-done((f32[64,4,256]{2,1,0:T(4,128)S(1)}, f32[64,4,256]{2,1,0:T(4,128)S(1)}, u32[]{:S(2)}, u32[]{:S(2)}) %collective-permute-start.26) | collective-permute-done | bytes 262176 | tf_op jit(solution)/shard_map/cond/branch_2_fun/ppermute | solution.py:585
  15.9 4.2 %collective-permute-done.27.refs_9_ = f32[64,4,256]{2,1,0:T(4,128)S(1)} collective-permute-done((f32[64,4,256]{2,1,0:T(4,128)S(1)}, f32[64,4,256]{2,1,0:T(4,128)S(1)}, u32[]{:S(2)}, u32[]{:S(2)}) %collective-permute-start.27) | collective-permute-done | bytes 262176 | tf_op jit(solution)/shard_map/cond/branch_2_fun/ppermute | solution.py:586
  20.1 7.6 %sections.12 = (f32[28,16,256]{2,1,0:T(8,128)S(1)}, f32[28,16,256]{2,1,0:T(8,128)S(1)}) custom-call(s32[1]{0:T(128)} %bitcast.10.refs_0_.place, s32[1]{0:T(128)S(6)} %and.11.refs_1_.core, s32[4]{0:T(128)S(1)} %copy-done.10, f32[8]{0:T(128)S(1)} %reshape.34.refs_3_, f32[1]{0:T(128)} %get-tuple-element.198.refs_4_, f32[128,16,256]{2,1,0:T(8,128)S(1)} %bitcast.38, ...), custom_call_target="tpu_custom_call" | custom-call | tf_op jit(solution)/shard_map/cond/branch_2_fun/sections/pallas_call | solution.py:409
  27.8 1.6 %collective-permute-start.29 = (f32[8,16,256]{2,1,0:T(8,128)S(1)}, f32[8,16,256]{2,1,0:T(8,128)S(1)}, u32[]{:S(2)}, u32[]{:S(2)}) collective-permute-start(f32[8,16,256]{2,1,0:T(8,128)S(1)} %pad_maximum_fusion.2), channel_id=1, source_target_pairs={{0,4},{4,0},{1,5},{5,1},{2,6},{6,2},{3,7},{7,3},{8,12},{12,8},{9,1... | collective-permute-start | bytes 393224 | tf_op jit(solution)/shard_map/cond/branch_2_fun/ppermute | solution.py:590
  29.3 4.4 %collective-permute-done.29.ends.refs_12_ = f32[8,16,256]{2,1,0:T(8,128)S(1)} collective-permute-done((f32[8,16,256]{2,1,0:T(8,128)S(1)}, f32[8,16,256]{2,1,0:T(8,128)S(1)}, u32[]{:S(2)}, u32[]{:S(2)}) %collective-permute-start.29) | collective-permute-done | bytes 131104 | tf_op jit(solution)/shard_map/cond/branch_2_fun/ppermute | solution.py:590
  33.8 1.2 %collective-permute-start.30 = (f32[72,4,256]{2,1,0:T(4,128)S(1)}, f32[72,4,256]{2,1,0:T(4,128)S(1)}, u32[]{:S(2)}, u32[]{:S(2)}) collective-permute-start(f32[72,4,256]{2,1,0:T(4,128)S(1)} %get-tuple-element.136), channel_id=1, source_target_pairs={{0,1},{1,2},{2,3},{3,0},{4,5},{5,6},{6,7},{7,4},{8,9},{9,10},{10,1... | collective-permute-start | bytes 884744 | tf_op jit(solution)/shard_map/cond/branch_2_fun/ppermute | solution.py:600
  34.9 2.7 %collective-permute-start.31 = (f32[72,4,256]{2,1,0:T(4,128)S(1)}, f32[72,4,256]{2,1,0:T(4,128)S(1)}, u32[]{:S(2)}, u32[]{:S(2)}) collective-permute-start(f32[72,4,256]{2,1,0:T(4,128)S(1)} %get-tuple-element.137), channel_id=1, source_target_pairs={{0,3},{1,0},{2,1},{3,2},{4,7},{5,4},{6,5},{7,6},{8,11},{9,8},{10,9... | collective-permute-start | bytes 884744 | tf_op jit(solution)/shard_map/cond/branch_2_fun/ppermute | solution.py:601
  38.3 7.2 %collective-permute-done.30.refs_10_ = f32[72,4,256]{2,1,0:T(4,128)S(1)} collective-permute-done((f32[72,4,256]{2,1,0:T(4,128)S(1)}, f32[72,4,256]{2,1,0:T(4,128)S(1)}, u32[]{:S(2)}, u32[]{:S(2)}) %collective-permute-start.30) | collective-permute-done | bytes 294944 | tf_op jit(solution)/shard_map/cond/branch_2_fun/ppermute | solution.py:600
  45.5 4.0 %collective-permute-done.31.refs_11_ = f32[72,4,256]{2,1,0:T(4,128)S(1)} collective-permute-done((f32[72,4,256]{2,1,0:T(4,128)S(1)}, f32[72,4,256]{2,1,0:T(4,128)S(1)}, u32[]{:S(2)}, u32[]{:S(2)}) %collective-permute-start.31) | collective-permute-done | bytes 294944 | tf_op jit(solution)/shard_map/cond/branch_2_fun/ppermute | solution.py:601
  49.5 10.0 %sections.13 = (f32[36,16,256]{2,1,0:T(8,128)S(1)}, f32[36,16,256]{2,1,0:T(8,128)S(1)}) custom-call(s32[1]{0:T(128)} %bitcast.10.refs_0_.place, s32[1]{0:T(128)S(6)} %and.11.refs_1_.core, s32[4]{0:T(128)S(1)} %copy-done.10, f32[8]{0:T(128)S(1)} %reshape.34.refs_3_, f32[1]{0:T(128)} %get-tuple-element.198.refs_4_, f32[128,16,256]{2,1,0:T(8,128)S(1)} %bitcast.40, ...), custom_call_target="tpu_custom_call" | custom-call | tf_op jit(solution)/shard_map/cond/branch_2_fun/sections/pallas_call | solution.py:409
  59.6 2.0 %collective-permute-done.32.refs_2_.other = f32[36,16,256]{2,1,0:T(8,128)S(1)} collective-permute-done((f32[36,16,256]{2,1,0:T(8,128)S(1)}, f32[36,16,256]{2,1,0:T(8,128)S(1)}, u32[]{:S(2)}, u32[]{:S(2)}) %collective-permute-start.32) | collective-permute-done | bytes 589856 | tf_op jit(solution)/shard_map/cond/branch_2_fun/ppermute | solution.py:607
  62.4 1.6 %collective-permute-start.34 = (f32[576,384]{1,0:T(8,128)S(1)}, f32[576,384]{1,0:T(8,128)S(1)}, u32[]{:S(2)}, u32[]{:S(2)}) collective-permute-start(f32[576,384]{1,0:T(8,128)S(1)} %pack.13), channel_id=1, source_target_pairs={{0,16},{8,24},{16,0},{24,8},{1,17},{9,25},{17,1},{25,9},{2,18},{10... | collective-permute-start | bytes 2654216 | tf_op jit(solution)/shard_map/cond/branch_2_fun/ppermute | solution.py:613
  64.5 20.5 %collective-permute-done.34.refs_0_ = f32[576,384]{1,0:T(8,128)S(1)} collective-permute-done((f32[576,384]{1,0:T(8,128)S(1)}, f32[576,384]{1,0:T(8,128)S(1)}, u32[]{:S(2)}, u32[]{:S(2)}) %collective-permute-start.34) | collective-permute-done | bytes 884768 | tf_op jit(solution)/shard_map/cond/branch_2_fun/ppermute | solution.py:613
  85.0 13.9 %collective-permute-done.37.refs_5_ = f32[448,384]{1,0:T(8,128)S(1)} collective-permute-done((f32[448,384]{1,0:T(8,128)S(1)}, f32[448,384]{1,0:T(8,128)S(1)}, u32[]{:S(2)}, u32[]{:S(2)}) %collective-permute-start.37) | collective-permute-done | bytes 688160 | tf_op jit(solution)/shard_map/cond/branch_2_fun/ppermute | solution.py:613
  99.4 2.5 %collective-permute-done.33.refs_3_ = f32[36,16,256]{2,1,0:T(8,128)S(1)} collective-permute-done((f32[36,16,256]{2,1,0:T(8,128)S(1)}, f32[36,16,256]{2,1,0:T(8,128)S(1)}, u32[]{:S(2)}, u32[]{:S(2)}) %collective-permute-start.33) | collective-permute-done | bytes 589856 | tf_op jit(solution)/shard_map/cond/branch_2_fun/ppermute | solution.py:614
  102.9 2.4 %finish.6.refs_2_ = f32[128,16,256]{2,1,0:T(8,128)} custom-call(s32[1]{0:T(128)S(6)} %and.11.refs_1_.core, s32[1]{0:T(128)} %bitcast.10.refs_0_.place, s32[4]{0:T(128)S(1)} %copy-done.6, f32[28,16,256]{2,1,0:T(8,128)S(1)} %get-tuple-element.131.mine.refs_0_, f32[28,16,256]{2,1,0:T(8,128)S(1)} %get-tuple-element.132.refs_1_, ...), custom_call_target="tpu_custom_call" | custom-call | tf_op jit(solution)/shard_map/cond/branch_2_fun/finish/pallas_call | solution.py:496
  105.3 1.3 %add_messages.12.refs_2_ = f32[128,16,256]{2,1,0:T(8,128)} custom-call(s32[1]{0:T(128)S(6)} %and.11.refs_1_.core, f32[36,16,256]{2,1,0:T(8,128)S(1)} %get-tuple-element.142.current, f32[576,384]{1,0:T(8,128)S(1)} %collective-permute-done.34.refs_0_, bf16[512,256]{1,0:T(8,128)(2,1)S(1)} %get-tuple-element.141.refs_7_.refs_1_, ...), custom_call_target="tpu_custom_call", output_to_operand_aliasing={{}: (4, {})} | custom-call | tf_op jit(solution)/shard_map/cond/branch_2_fun/add_messages/pallas_call | solution.py:539
  106.6 1.3 %add_messages.13 = f32[128,16,256]{2,1,0:T(8,128)} custom-call(s32[1]{0:T(128)S(6)} %and.11.refs_1_.core, f32[36,16,256]{2,1,0:T(8,128)S(1)} %get-tuple-element.140.current, f32[576,384]{1,0:T(8,128)S(1)} %collective-permute-done.35.refs_0_, bf16[512,256]{1,0:T(8,128)(2,1)S(1)} %get-tuple-element.141.refs_7_.refs_1_, ...), custom_call_target="tpu_custom_call", output_to_operand_aliasing={{}: (4, {})} | custom-call | tf_op jit(solution)/shard_map/cond/branch_2_fun/add_messages/pallas_call | solution.py:539
  (26 shorter events, 3.8 us)
Async XLA Ops:
  2.1 6.7 %copy-start.14 = (f32[2,4]{1,0:T(2,128)S(1)}, f32[2,4]{1,0:T(2,128)}, u32[]{:S(2)}) copy-start(f32[2,4]{1,0:T(2,128)} %get-tuple-element.186) | copy-start | bytes 100 | tf_op jit(solution)/shard_map/cond
  2.2 6.7 %copy-start.6 = (s32[4]{0:T(128)S(1)}, s32[4]{0:T(128)}, u32[]{:S(2)}) copy-start(s32[4]{0:T(128)} %get-tuple-element.190.refs_2_.weights) | copy-start | bytes 52 | tf_op jit(solution)/shard_map/cond
  2.2 6.7 %copy-start.10 = (s32[4]{0:T(128)S(1)}, s32[4]{0:T(128)}, u32[]{:S(2)}) copy-start(s32[4]{0:T(128)} %get-tuple-element.121.refs_1_.refs_2_) | copy-start | bytes 52 | tf_op jit(solution)/shard_map/cond
  2.2 9.9 %copy-start.2 = (f32[1,128,16,256]{3,2,1,0:T(8,128)S(1)}, f32[1,128,16,256]{3,2,1,0:T(8,128)}, u32[]{:S(2)}) copy-start(f32[1,128,16,256]{3,2,1,0:T(8,128)} %get-tuple-element.194) | copy-start | bytes 6291460 | tf_op jit(solution)/shard_map/cond
  3.6 12.3 %collective-permute-start.26 = (f32[64,4,256]{2,1,0:T(4,128)S(1)}, f32[64,4,256]{2,1,0:T(4,128)S(1)}, u32[]{:S(2)}, u32[]{:S(2)}) collective-permute-start(f32[64,4,256]{2,1,0:T(4,128)S(1)} %get-tuple-element.129), channel_id=1, source_target_pairs={{0,1},{1,2},{2,3},{3,0},{4,5},{5,6},{6,7},{7,4},{8,9},{9,10},{10,1... | collective-permute-start | bytes 786440 | tf_op jit(solution)/shard_map/cond/branch_2_fun/ppermute | solution.py:585
  6.7 13.4 %collective-permute-start.27 = (f32[64,4,256]{2,1,0:T(4,128)S(1)}, f32[64,4,256]{2,1,0:T(4,128)S(1)}, u32[]{:S(2)}, u32[]{:S(2)}) collective-permute-start(f32[64,4,256]{2,1,0:T(4,128)S(1)} %get-tuple-element.130), channel_id=1, source_target_pairs={{0,3},{1,0},{2,1},{3,2},{4,7},{5,4},{6,5},{7,6},{8,11},{9,8},{10,9... | collective-permute-start | bytes 786440 | tf_op jit(solution)/shard_map/cond/branch_2_fun/ppermute | solution.py:586
  27.7 10.0 %collective-permute-start.28 = (f32[28,16,256]{2,1,0:T(8,128)S(1)}, f32[28,16,256]{2,1,0:T(8,128)S(1)}, u32[]{:S(2)}, u32[]{:S(2)}) collective-permute-start(f32[28,16,256]{2,1,0:T(8,128)S(1)} %get-tuple-element.132.refs_1_), channel_id=1, source_target_pairs={{0,8},{8,0},{16,24},{24,16},{1,9},{9,1},{17,25},{25,17},{2,10},{10... | collective-permute-start | bytes 1376264 | tf_op jit(solution)/shard_map/cond/branch_2_fun/ppermute | solution.py:607
  27.8 6.0 %collective-permute-start.29 = (f32[8,16,256]{2,1,0:T(8,128)S(1)}, f32[8,16,256]{2,1,0:T(8,128)S(1)}, u32[]{:S(2)}, u32[]{:S(2)}) collective-permute-start(f32[8,16,256]{2,1,0:T(8,128)S(1)} %pad_maximum_fusion.2), channel_id=1, source_target_pairs={{0,4},{4,0},{1,5},{5,1},{2,6},{6,2},{3,7},{7,3},{8,12},{12,8},{9,1... | collective-permute-start | bytes 393224 | tf_op jit(solution)/shard_map/cond/branch_2_fun/ppermute | solution.py:590
  33.8 11.7 %collective-permute-start.30 = (f32[72,4,256]{2,1,0:T(4,128)S(1)}, f32[72,4,256]{2,1,0:T(4,128)S(1)}, u32[]{:S(2)}, u32[]{:S(2)}) collective-permute-start(f32[72,4,256]{2,1,0:T(4,128)S(1)} %get-tuple-element.136), channel_id=1, source_target_pairs={{0,1},{1,2},{2,3},{3,0},{4,5},{5,6},{6,7},{7,4},{8,9},{9,10},{10,1... | collective-permute-start | bytes 884744 | tf_op jit(solution)/shard_map/cond/branch_2_fun/ppermute | solution.py:600
  34.9 14.6 %collective-permute-start.31 = (f32[72,4,256]{2,1,0:T(4,128)S(1)}, f32[72,4,256]{2,1,0:T(4,128)S(1)}, u32[]{:S(2)}, u32[]{:S(2)}) collective-permute-start(f32[72,4,256]{2,1,0:T(4,128)S(1)} %get-tuple-element.137), channel_id=1, source_target_pairs={{0,3},{1,0},{2,1},{3,2},{4,7},{5,4},{6,5},{7,6},{8,11},{9,8},{10,9... | collective-permute-start | bytes 884744 | tf_op jit(solution)/shard_map/cond/branch_2_fun/ppermute | solution.py:601
  59.5 2.1 %collective-permute-start.32 = (f32[36,16,256]{2,1,0:T(8,128)S(1)}, f32[36,16,256]{2,1,0:T(8,128)S(1)}, u32[]{:S(2)}, u32[]{:S(2)}) collective-permute-start(f32[36,16,256]{2,1,0:T(8,128)S(1)} %get-tuple-element.139.refs_1_), channel_id=1, source_target_pairs={{0,8},{8,0},{16,24},{24,16},{1,9},{9,1},{17,25},{25,17},{2,10},{10... | collective-permute-start | bytes 1769480 | tf_op jit(solution)/shard_map/cond/branch_2_fun/ppermute | solution.py:607
  62.4 22.6 %collective-permute-start.34 = (f32[576,384]{1,0:T(8,128)S(1)}, f32[576,384]{1,0:T(8,128)S(1)}, u32[]{:S(2)}, u32[]{:S(2)}) collective-permute-start(f32[576,384]{1,0:T(8,128)S(1)} %pack.13), channel_id=1, source_target_pairs={{0,16},{8,24},{16,0},{24,8},{1,17},{9,25},{17,1},{25,9},{2,18},{10... | collective-permute-start | bytes 2654216 | tf_op jit(solution)/shard_map/cond/branch_2_fun/ppermute | solution.py:613
  64.0 34.9 %collective-permute-start.37 = (f32[448,384]{1,0:T(8,128)S(1)}, f32[448,384]{1,0:T(8,128)S(1)}, u32[]{:S(2)}, u32[]{:S(2)}) collective-permute-start(f32[448,384]{1,0:T(8,128)S(1)} %pack.12), channel_id=1, source_target_pairs={{0,16},{8,24},{16,0},{24,8},{1,17},{9,25},{17,1},{25,9},{2,18},{10... | collective-permute-start | bytes 2064392 | tf_op jit(solution)/shard_map/cond/branch_2_fun/ppermute | solution.py:613
  85.0 21.6 %collective-permute-start.35 = (f32[576,384]{1,0:T(8,128)S(1)}, f32[576,384]{1,0:T(8,128)S(1)}, u32[]{:S(2)}, u32[]{:S(2)}) collective-permute-start(f32[576,384]{1,0:T(8,128)S(1)} %collective-permute-done.34.refs_0_), channel_id=1, source_target_pairs={{0,8},{8,0},{16,24},{24,16},{1,9},{9,1},{17,25},{25,17},{2,10},{10... | collective-permute-start | bytes 2654216 | tf_op jit(solution)/shard_map/cond/branch_2_fun/ppermute | solution.py:619
  98.9 4.0 %collective-permute-start.38 = (f32[448,384]{1,0:T(8,128)S(1)}, f32[448,384]{1,0:T(8,128)S(1)}, u32[]{:S(2)}, u32[]{:S(2)}) collective-permute-start(f32[448,384]{1,0:T(8,128)S(1)} %collective-permute-done.37.refs_5_), channel_id=1, source_target_pairs={{0,8},{8,0},{16,24},{24,16},{1,9},{9,1},{17,25},{25,17},{2,10},{10... | collective-permute-start | bytes 2064392 | tf_op jit(solution)/shard_map/cond/branch_2_fun/ppermute | solution.py:619
  98.9 3.0 %collective-permute-start.33 = (f32[36,16,256]{2,1,0:T(8,128)S(1)}, f32[36,16,256]{2,1,0:T(8,128)S(1)}, u32[]{:S(2)}, u32[]{:S(2)}) collective-permute-start(f32[36,16,256]{2,1,0:T(8,128)S(1)} %get-tuple-element.138.refs_0_.mine), channel_id=1, source_target_pairs={{0,8},{8,0},{16,24},{24,16},{1,9},{9,1},{17,25},{25,17},{2,10},{10... | collective-permute-start | bytes 1769480 | tf_op jit(solution)/shard_map/cond/branch_2_fun/ppermute | solution.py:614
  99.4 3.5 %collective-permute-start.36 = (f32[28,16,256]{2,1,0:T(8,128)S(1)}, f32[28,16,256]{2,1,0:T(8,128)S(1)}, u32[]{:S(2)}, u32[]{:S(2)}) collective-permute-start(f32[28,16,256]{2,1,0:T(8,128)S(1)} %get-tuple-element.131.mine.refs_0_), channel_id=1, source_target_pairs={{0,8},{8,0},{16,24},{24,16},{1,9},{9,1},{17,25},{25,17},{2,10},{10... | collective-permute-start | bytes 1376264 | tf_op jit(solution)/shard_map/cond/branch_2_fun/ppermute | solution.py:614

commit v3 on v2

--- a/solution.py
+++ b/solution.py
@@ -290,7 +290,7 @@
 
 def chunk_plans(long, cap, flat):
     halo = SECTIONS
-    share = 8 if cap <= flat else 7 if 2 * cap <= 3 * flat else 6
+    share = 7 if 2 * cap <= 3 * flat else 6
     first = share * (long // 16)
     side = (long - first) // 2
     wide = first + 2 * halo
@@ -329,21 +329,12 @@
 
 def stencil_kernel(plan, order, place, core, levels, rates, reaction, field, *refs):
     count = 2 * len(order) + (2 if plan["own"][1:] else 1) + 1
-    held_refs, (keep, give, state, sems) = refs[:count], refs[count:]
+    held_refs, (keep, give, state) = refs[:count], refs[count:]
     halo = SECTIONS
     own = field.shape[1]
     tall = own + 2 * halo
     flat = field.shape[2]
     first = state.at[0]
-    copies = []
-    for source, start, target, rows in plan["own"]:
-        if source is None:
-            copies.append((field.at[pl.ds(start, rows)], first.at[pl.ds(target, rows), pl.ds(0, own)]))
-    copies = [
-        pltpu.make_async_copy(source, target, sems.at[k]) for k, (source, target) in enumerate(copies)
-    ]
-    for copy in copies:
-        copy.start()
     level = levels[place[0]]
     dif, cou = grid_numbers(rates, level)
     centre_weight = 1.0 - 2.0 * (dif[0] + dif[1] + dif[2] + dif[3])
@@ -352,14 +343,12 @@
     head_ref, tail_ref = held_refs[:2]
     sides = {source: held_refs[2 + 2 * k : 4 + 2 * k] for k, source in enumerate(order)}
     for source, start, target, rows in plan["own"]:
-        if source is not None:
-            first[target : target + rows, :own] = held_refs[-1][start : start + rows]
+        origin = field if source is None else held_refs[-1]
+        first[target : target + rows, :own] = origin[start : start + rows]
     for source, start, target, rows in plan["edge"]:
         low, high = sides[source]
         first[target : target + rows, own : own + halo] = high[start : start + rows]
         first[target : target + rows, own + halo :] = low[start : start + rows]
-    for copy in copies:
-        copy.wait()
 
     def block(which, at, depth, step):
         centre = state[which, pl.ds(at, step)]
@@ -404,16 +393,14 @@
     order = sorted({source for source, *_ in plan["edge"]})
     operands = [head, tail] + [ref for source in order for ref in edges[source]]
     operands += [ends] if plan["own"][1:] else []
-    straight = sum(source is None for source, *_ in plan["own"])
     half = jax.ShapeDtypeStruct((plan["half"], own, flat), F32)
     return pl.pallas_call(
         lambda *refs: stencil_kernel(plan, order, *refs),
         out_shape=[half, half],
-        in_specs=[SMEM] * 5 + [ANY] + [VMEM] * len(operands),
+        in_specs=[SMEM] * 5 + [VMEM] * (1 + len(operands)),
         out_specs=[VMEM, VMEM],
         scratch_shapes=[
-            pltpu.VMEM((2, plan["pieces"] * plan["piece"], own + 2 * halo, flat), F32),
-            pltpu.SemaphoreType.DMA((straight,)),
+            pltpu.VMEM((2, plan["pieces"] * plan["piece"], own + 2 * halo, flat), F32)
         ],
         compiler_params=ROOM,
         name="sections",

time: 109 us -> 109 us (level)
  no operation moved by 1% of the time
where the time goes in v3:
time: 109 us; the launch traced here: 108 us
  waiting for transfers between devices  62.6 us (57%)
  Pallas kernels  30.7 us (28%)
  starting transfers between devices  13.4 us (12%)
    ppermute x2, waiting for transfers between devices, send(): near.append(lax.ppermute(message, 'comp', shift))  34.4 us
    pallas_call x2, Pallas kernels, stencil(): pl.pallas_call(lambda *refs: stencil_kernel(plan, order, *refs), out_shap...  17.5 us
    ppermute x1, waiting for transfers between devices, run(): low_two = lax.ppermute(low_two, 'gy', forward['gy'])  7.21 us
    ppermute x1, waiting for transfers between devices, run(): lax.ppermute(jnp.concatenate([last_rows, first_rows]), 'gx', forward['gx'])  4.4 us
    ppermute x1, waiting for transfers between devices, run(): lax.ppermute(high_one, 'gy', backward['gy'])  4.16 us
    ppermute x1, waiting for transfers between devices, run(): high_two = lax.ppermute(high_two, 'gy', backward['gy'])  4.03 us
    ppermute x1, waiting for transfers between devices, run(): lax.ppermute(low_one, 'gy', forward['gy'])  3.89 us
    pallas_call x1, Pallas kernels, setup_tables(): pl.pallas_call(lambda *refs: setup_kernel(flat, chips, *refs), out_shape=...  3.12 us
  transfers between devices with their start and end apart: 13, of which 9 were waited for; matrix products, arithmetic and copies ran while one was open for 0% of the time, Pallas kernels for 8%

profile of v3, /device:TPU:0, one launch (start us, length us, event | category | flops | bytes accessed | tf_op | source)
XLA Modules:
  0.0 108.3 jit_solution(16745725597925363607)
XLA Ops:
  0.0 1.2 %room.1 = s32[1]{0:T(128)} custom-call(s32[4]{0:T(128)} %levels.1), custom_call_target="tpu_custom_call" | custom-call | tf_op jit(solution)/shard_map/room/pallas_call | solution.py:235
  1.9 106.2 %conditional.1 = (f32[1,128,16,256]{3,2,1,0:T(8,128)}) conditional(s32[]{:T(128)} %bitcast.20, (s32[]{:T(128)}, f32[2,4]{1,0:T(2,128)}, s32[4]{0:T(128)}, s32[4]{0:T(128)}, f32[1,128,16,256]{3,2,1,0:T(8,128)}, /*index=5*/f32[1]{0:T(128)}) %tuple.29, (s32[]{:T(128)}, f32[2,4]{1,0:T(2,128)}, s32[4]{0:T(128)}, ...), branch_computations={%region_0.0_spmd, %region_1.0_spmd, %region_2.0_spmd, %region_3.0_... | conditional | flops 32769 | bytes 39060428 | solution.py:548
  2.2 1.4 %faces.6 = (f32[64,4,256]{2,1,0:T(4,128)S(1)}, f32[64,4,256]{2,1,0:T(4,128)S(1)}) custom-call(f32[128,16,256]{2,1,0:T(8,128)} %bitcast.37), custom_call_target="tpu_custom_call" | custom-call | tf_op jit(solution)/shard_map/cond/branch_2_fun/faces/pallas_call | solution.py:257
  3.6 3.1 %collective-permute-start.26 = (f32[64,4,256]{2,1,0:T(4,128)S(1)}, f32[64,4,256]{2,1,0:T(4,128)S(1)}, u32[]{:S(2)}, u32[]{:S(2)}) collective-permute-start(f32[64,4,256]{2,1,0:T(4,128)S(1)} %get-tuple-element.129), channel_id=1, source_target_pairs={{0,1},{1,2},{2,3},{3,0},{4,5},{5,6},{6,7},{7,4},{8,9},{9,10},{10,1... | collective-permute-start | bytes 786440 | tf_op jit(solution)/shard_map/cond/branch_2_fun/ppermute | solution.py:572
  6.7 2.1 %collective-permute-start.27 = (f32[64,4,256]{2,1,0:T(4,128)S(1)}, f32[64,4,256]{2,1,0:T(4,128)S(1)}, u32[]{:S(2)}, u32[]{:S(2)}) collective-permute-start(f32[64,4,256]{2,1,0:T(4,128)S(1)} %get-tuple-element.130), channel_id=1, source_target_pairs={{0,3},{1,0},{2,1},{3,2},{4,7},{5,4},{6,5},{7,6},{8,11},{9,8},{10,9... | collective-permute-start | bytes 786440 | tf_op jit(solution)/shard_map/cond/branch_2_fun/ppermute | solution.py:573
  8.9 3.1 %tables.6 = (bf16[256,256]{1,0:T(8,128)(2,1)S(1)}, bf16[256,256]{1,0:T(8,128)(2,1)S(1)}, bf16[256,256]{1,0:T(8,128)(2,1)S(1)}, bf16[256,512]{1,0:T(8,128)(2,1)S(...) custom-call(s32[1]{0:T(128)} %bitcast.10.refs_0_.place, s32[4]{0:T(128)S(1)} %copy-done.10, ...), custom_call_target="tpu_custom_call" | custom-call | tf_op jit(solution)/shard_map/cond/branch_2_fun/tables/pallas_call | solution.py:214
  12.1 3.9 %collective-permute-done.26.refs_8_ = f32[64,4,256]{2,1,0:T(4,128)S(1)} collective-permute-done((f32[64,4,256]{2,1,0:T(4,128)S(1)}, f32[64,4,256]{2,1,0:T(4,128)S(1)}, u32[]{:S(2)}, u32[]{:S(2)}) %collective-permute-start.26) | collective-permute-done | bytes 262176 | tf_op jit(solution)/shard_map/cond/branch_2_fun/ppermute | solution.py:572
  15.9 4.2 %collective-permute-done.27.refs_9_ = f32[64,4,256]{2,1,0:T(4,128)S(1)} collective-permute-done((f32[64,4,256]{2,1,0:T(4,128)S(1)}, f32[64,4,256]{2,1,0:T(4,128)S(1)}, u32[]{:S(2)}, u32[]{:S(2)}) %collective-permute-start.27) | collective-permute-done | bytes 262176 | tf_op jit(solution)/shard_map/cond/branch_2_fun/ppermute | solution.py:573
  20.1 7.5 %sections.12 = (f32[28,16,256]{2,1,0:T(8,128)S(1)}, f32[28,16,256]{2,1,0:T(8,128)S(1)}) custom-call(s32[1]{0:T(128)} %bitcast.10.refs_0_.place, s32[1]{0:T(128)S(6)} %and.11.refs_1_.core, s32[4]{0:T(128)S(1)} %copy-done.10, f32[8]{0:T(128)S(1)} %reshape.34.refs_3_, f32[1]{0:T(128)} %get-tuple-element.198.refs_4_, f32[128,16,256]{2,1,0:T(8,128)S(1)} %bitcast.38, ...), custom_call_target="tpu_custom_call" | custom-call | tf_op jit(solution)/shard_map/cond/branch_2_fun/sections/pallas_call | solution.py:397
  27.7 1.6 %collective-permute-start.29 = (f32[8,16,256]{2,1,0:T(8,128)S(1)}, f32[8,16,256]{2,1,0:T(8,128)S(1)}, u32[]{:S(2)}, u32[]{:S(2)}) collective-permute-start(f32[8,16,256]{2,1,0:T(8,128)S(1)} %pad_maximum_fusion.2), channel_id=1, source_target_pairs={{0,4},{4,0},{1,5},{5,1},{2,6},{6,2},{3,7},{7,3},{8,12},{12,8},{9,1... | collective-permute-start | bytes 393224 | tf_op jit(solution)/shard_map/cond/branch_2_fun/ppermute | solution.py:577
  29.2 4.4 %collective-permute-done.29.ends.refs_12_ = f32[8,16,256]{2,1,0:T(8,128)S(1)} collective-permute-done((f32[8,16,256]{2,1,0:T(8,128)S(1)}, f32[8,16,256]{2,1,0:T(8,128)S(1)}, u32[]{:S(2)}, u32[]{:S(2)}) %collective-permute-start.29) | collective-permute-done | bytes 131104 | tf_op jit(solution)/shard_map/cond/branch_2_fun/ppermute | solution.py:577
  33.7 1.2 %collective-permute-start.30 = (f32[72,4,256]{2,1,0:T(4,128)S(1)}, f32[72,4,256]{2,1,0:T(4,128)S(1)}, u32[]{:S(2)}, u32[]{:S(2)}) collective-permute-start(f32[72,4,256]{2,1,0:T(4,128)S(1)} %get-tuple-element.136), channel_id=1, source_target_pairs={{0,1},{1,2},{2,3},{3,0},{4,5},{5,6},{6,7},{7,4},{8,9},{9,10},{10,1... | collective-permute-start | bytes 884744 | tf_op jit(solution)/shard_map/cond/branch_2_fun/ppermute | solution.py:587
  34.9 2.7 %collective-permute-start.31 = (f32[72,4,256]{2,1,0:T(4,128)S(1)}, f32[72,4,256]{2,1,0:T(4,128)S(1)}, u32[]{:S(2)}, u32[]{:S(2)}) collective-permute-start(f32[72,4,256]{2,1,0:T(4,128)S(1)} %get-tuple-element.137), channel_id=1, source_target_pairs={{0,3},{1,0},{2,1},{3,2},{4,7},{5,4},{6,5},{7,6},{8,11},{9,8},{10,9... | collective-permute-start | bytes 884744 | tf_op jit(solution)/shard_map/cond/branch_2_fun/ppermute | solution.py:588
  38.2 7.2 %collective-permute-done.30.refs_10_ = f32[72,4,256]{2,1,0:T(4,128)S(1)} collective-permute-done((f32[72,4,256]{2,1,0:T(4,128)S(1)}, f32[72,4,256]{2,1,0:T(4,128)S(1)}, u32[]{:S(2)}, u32[]{:S(2)}) %collective-permute-start.30) | collective-permute-done | bytes 294944 | tf_op jit(solution)/shard_map/cond/branch_2_fun/ppermute | solution.py:587
  45.4 4.0 %collective-permute-done.31.refs_11_ = f32[72,4,256]{2,1,0:T(4,128)S(1)} collective-permute-done((f32[72,4,256]{2,1,0:T(4,128)S(1)}, f32[72,4,256]{2,1,0:T(4,128)S(1)}, u32[]{:S(2)}, u32[]{:S(2)}) %collective-permute-start.31) | collective-permute-done | bytes 294944 | tf_op jit(solution)/shard_map/cond/branch_2_fun/ppermute | solution.py:588
  49.5 10.0 %sections.13 = (f32[36,16,256]{2,1,0:T(8,128)S(1)}, f32[36,16,256]{2,1,0:T(8,128)S(1)}) custom-call(s32[1]{0:T(128)} %bitcast.10.refs_0_.place, s32[1]{0:T(128)S(6)} %and.11.refs_1_.core, s32[4]{0:T(128)S(1)} %copy-done.10, f32[8]{0:T(128)S(1)} %reshape.34.refs_3_, f32[1]{0:T(128)} %get-tuple-element.198.refs_4_, f32[128,16,256]{2,1,0:T(8,128)S(1)} %bitcast.40, ...), custom_call_target="tpu_custom_call" | custom-call | tf_op jit(solution)/shard_map/cond/branch_2_fun/sections/pallas_call | solution.py:397
  59.5 2.0 %collective-permute-done.32.refs_2_.other = f32[36,16,256]{2,1,0:T(8,128)S(1)} collective-permute-done((f32[36,16,256]{2,1,0:T(8,128)S(1)}, f32[36,16,256]{2,1,0:T(8,128)S(1)}, u32[]{:S(2)}, u32[]{:S(2)}) %collective-permute-start.32) | collective-permute-done | bytes 589856 | tf_op jit(solution)/shard_map/cond/branch_2_fun/ppermute | solution.py:594
  62.3 1.6 %collective-permute-start.34 = (f32[576,384]{1,0:T(8,128)S(1)}, f32[576,384]{1,0:T(8,128)S(1)}, u32[]{:S(2)}, u32[]{:S(2)}) collective-permute-start(f32[576,384]{1,0:T(8,128)S(1)} %pack.13), channel_id=1, source_target_pairs={{0,16},{8,24},{16,0},{24,8},{1,17},{9,25},{17,1},{25,9},{2,18},{10... | collective-permute-start | bytes 2654216 | tf_op jit(solution)/shard_map/cond/branch_2_fun/ppermute | solution.py:600
  64.4 20.5 %collective-permute-done.34.refs_0_ = f32[576,384]{1,0:T(8,128)S(1)} collective-permute-done((f32[576,384]{1,0:T(8,128)S(1)}, f32[576,384]{1,0:T(8,128)S(1)}, u32[]{:S(2)}, u32[]{:S(2)}) %collective-permute-start.34) | collective-permute-done | bytes 884768 | tf_op jit(solution)/shard_map/cond/branch_2_fun/ppermute | solution.py:600
  84.9 13.9 %collective-permute-done.37.refs_5_ = f32[448,384]{1,0:T(8,128)S(1)} collective-permute-done((f32[448,384]{1,0:T(8,128)S(1)}, f32[448,384]{1,0:T(8,128)S(1)}, u32[]{:S(2)}, u32[]{:S(2)}) %collective-permute-start.37) | collective-permute-done | bytes 688160 | tf_op jit(solution)/shard_map/cond/branch_2_fun/ppermute | solution.py:600
  99.3 2.5 %collective-permute-done.33.refs_3_ = f32[36,16,256]{2,1,0:T(8,128)S(1)} collective-permute-done((f32[36,16,256]{2,1,0:T(8,128)S(1)}, f32[36,16,256]{2,1,0:T(8,128)S(1)}, u32[]{:S(2)}, u32[]{:S(2)}) %collective-permute-start.33) | collective-permute-done | bytes 589856 | tf_op jit(solution)/shard_map/cond/branch_2_fun/ppermute | solution.py:601
  102.8 2.4 %finish.6.refs_2_ = f32[128,16,256]{2,1,0:T(8,128)} custom-call(s32[1]{0:T(128)S(6)} %and.11.refs_1_.core, s32[1]{0:T(128)} %bitcast.10.refs_0_.place, s32[4]{0:T(128)S(1)} %copy-done.6, f32[28,16,256]{2,1,0:T(8,128)S(1)} %get-tuple-element.131.mine.refs_0_, f32[28,16,256]{2,1,0:T(8,128)S(1)} %get-tuple-element.132.refs_1_, ...), custom_call_target="tpu_custom_call" | custom-call | tf_op jit(solution)/shard_map/cond/branch_2_fun/finish/pallas_call | solution.py:483
  105.2 1.3 %add_messages.12.refs_2_ = f32[128,16,256]{2,1,0:T(8,128)} custom-call(s32[1]{0:T(128)S(6)} %and.11.refs_1_.core, f32[36,16,256]{2,1,0:T(8,128)S(1)} %get-tuple-element.142.current, f32[576,384]{1,0:T(8,128)S(1)} %collective-permute-done.34.refs_0_, bf16[512,256]{1,0:T(8,128)(2,1)S(1)} %get-tuple-element.141.refs_7_.refs_1_, ...), custom_call_target="tpu_custom_call", output_to_operand_aliasing={{}: (4, {})} | custom-call | tf_op jit(solution)/shard_map/cond/branch_2_fun/add_messages/pallas_call | solution.py:526
  106.5 1.3 %add_messages.13 = f32[128,16,256]{2,1,0:T(8,128)} custom-call(s32[1]{0:T(128)S(6)} %and.11.refs_1_.core, f32[36,16,256]{2,1,0:T(8,128)S(1)} %get-tuple-element.140.current, f32[576,384]{1,0:T(8,128)S(1)} %collective-permute-done.35.refs_0_, bf16[512,256]{1,0:T(8,128)(2,1)S(1)} %get-tuple-element.141.refs_7_.refs_1_, ...), custom_call_target="tpu_custom_call", output_to_operand_aliasing={{}: (4, {})} | custom-call | tf_op jit(solution)/shard_map/cond/branch_2_fun/add_messages/pallas_call | solution.py:526
  (26 shorter events, 3.8 us)
Async XLA Ops:
  2.1 6.7 %copy-start.14 = (f32[2,4]{1,0:T(2,128)S(1)}, f32[2,4]{1,0:T(2,128)}, u32[]{:S(2)}) copy-start(f32[2,4]{1,0:T(2,128)} %get-tuple-element.186) | copy-start | bytes 100 | tf_op jit(solution)/shard_map/cond
  2.2 6.7 %copy-start.6 = (s32[4]{0:T(128)S(1)}, s32[4]{0:T(128)}, u32[]{:S(2)}) copy-start(s32[4]{0:T(128)} %get-tuple-element.190.refs_2_.weights) | copy-start | bytes 52 | tf_op jit(solution)/shard_map/cond
  2.2 6.7 %copy-start.10 = (s32[4]{0:T(128)S(1)}, s32[4]{0:T(128)}, u32[]{:S(2)}) copy-start(s32[4]{0:T(128)} %get-tuple-element.121.refs_1_.refs_2_) | copy-start | bytes 52 | tf_op jit(solution)/shard_map/cond
  2.2 9.9 %copy-start.2 = (f32[1,128,16,256]{3,2,1,0:T(8,128)S(1)}, f32[1,128,16,256]{3,2,1,0:T(8,128)}, u32[]{:S(2)}) copy-start(f32[1,128,16,256]{3,2,1,0:T(8,128)} %get-tuple-element.194) | copy-start | bytes 6291460 | tf_op jit(solution)/shard_map/cond
  3.6 12.3 %collective-permute-start.26 = (f32[64,4,256]{2,1,0:T(4,128)S(1)}, f32[64,4,256]{2,1,0:T(4,128)S(1)}, u32[]{:S(2)}, u32[]{:S(2)}) collective-permute-start(f32[64,4,256]{2,1,0:T(4,128)S(1)} %get-tuple-element.129), channel_id=1, source_target_pairs={{0,1},{1,2},{2,3},{3,0},{4,5},{5,6},{6,7},{7,4},{8,9},{9,10},{10,1... | collective-permute-start | bytes 786440 | tf_op jit(solution)/shard_map/cond/branch_2_fun/ppermute | solution.py:572
  6.7 13.4 %collective-permute-start.27 = (f32[64,4,256]{2,1,0:T(4,128)S(1)}, f32[64,4,256]{2,1,0:T(4,128)S(1)}, u32[]{:S(2)}, u32[]{:S(2)}) collective-permute-start(f32[64,4,256]{2,1,0:T(4,128)S(1)} %get-tuple-element.130), channel_id=1, source_target_pairs={{0,3},{1,0},{2,1},{3,2},{4,7},{5,4},{6,5},{7,6},{8,11},{9,8},{10,9... | collective-permute-start | bytes 786440 | tf_op jit(solution)/shard_map/cond/branch_2_fun/ppermute | solution.py:573
  27.6 10.0 %collective-permute-start.28 = (f32[28,16,256]{2,1,0:T(8,128)S(1)}, f32[28,16,256]{2,1,0:T(8,128)S(1)}, u32[]{:S(2)}, u32[]{:S(2)}) collective-permute-start(f32[28,16,256]{2,1,0:T(8,128)S(1)} %get-tuple-element.132.refs_1_), channel_id=1, source_target_pairs={{0,8},{8,0},{16,24},{24,16},{1,9},{9,1},{17,25},{25,17},{2,10},{10... | collective-permute-start | bytes 1376264 | tf_op jit(solution)/shard_map/cond/branch_2_fun/ppermute | solution.py:594
  27.7 6.0 %collective-permute-start.29 = (f32[8,16,256]{2,1,0:T(8,128)S(1)}, f32[8,16,256]{2,1,0:T(8,128)S(1)}, u32[]{:S(2)}, u32[]{:S(2)}) collective-permute-start(f32[8,16,256]{2,1,0:T(8,128)S(1)} %pad_maximum_fusion.2), channel_id=1, source_target_pairs={{0,4},{4,0},{1,5},{5,1},{2,6},{6,2},{3,7},{7,3},{8,12},{12,8},{9,1... | collective-permute-start | bytes 393224 | tf_op jit(solution)/shard_map/cond/branch_2_fun/ppermute | solution.py:577
  33.7 11.7 %collective-permute-start.30 = (f32[72,4,256]{2,1,0:T(4,128)S(1)}, f32[72,4,256]{2,1,0:T(4,128)S(1)}, u32[]{:S(2)}, u32[]{:S(2)}) collective-permute-start(f32[72,4,256]{2,1,0:T(4,128)S(1)} %get-tuple-element.136), channel_id=1, source_target_pairs={{0,1},{1,2},{2,3},{3,0},{4,5},{5,6},{6,7},{7,4},{8,9},{9,10},{10,1... | collective-permute-start | bytes 884744 | tf_op jit(solution)/shard_map/cond/branch_2_fun/ppermute | solution.py:587
  34.9 14.6 %collective-permute-start.31 = (f32[72,4,256]{2,1,0:T(4,128)S(1)}, f32[72,4,256]{2,1,0:T(4,128)S(1)}, u32[]{:S(2)}, u32[]{:S(2)}) collective-permute-start(f32[72,4,256]{2,1,0:T(4,128)S(1)} %get-tuple-element.137), channel_id=1, source_target_pairs={{0,3},{1,0},{2,1},{3,2},{4,7},{5,4},{6,5},{7,6},{8,11},{9,8},{10,9... | collective-permute-start | bytes 884744 | tf_op jit(solution)/shard_map/cond/branch_2_fun/ppermute | solution.py:588
  59.4 2.1 %collective-permute-start.32 = (f32[36,16,256]{2,1,0:T(8,128)S(1)}, f32[36,16,256]{2,1,0:T(8,128)S(1)}, u32[]{:S(2)}, u32[]{:S(2)}) collective-permute-start(f32[36,16,256]{2,1,0:T(8,128)S(1)} %get-tuple-element.139.refs_1_), channel_id=1, source_target_pairs={{0,8},{8,0},{16,24},{24,16},{1,9},{9,1},{17,25},{25,17},{2,10},{10... | collective-permute-start | bytes 1769480 | tf_op jit(solution)/shard_map/cond/branch_2_fun/ppermute | solution.py:594
  62.3 22.6 %collective-permute-start.34 = (f32[576,384]{1,0:T(8,128)S(1)}, f32[576,384]{1,0:T(8,128)S(1)}, u32[]{:S(2)}, u32[]{:S(2)}) collective-permute-start(f32[576,384]{1,0:T(8,128)S(1)} %pack.13), channel_id=1, source_target_pairs={{0,16},{8,24},{16,0},{24,8},{1,17},{9,25},{17,1},{25,9},{2,18},{10... | collective-permute-start | bytes 2654216 | tf_op jit(solution)/shard_map/cond/branch_2_fun/ppermute | solution.py:600
  63.9 34.9 %collective-permute-start.37 = (f32[448,384]{1,0:T(8,128)S(1)}, f32[448,384]{1,0:T(8,128)S(1)}, u32[]{:S(2)}, u32[]{:S(2)}) collective-permute-start(f32[448,384]{1,0:T(8,128)S(1)} %pack.12), channel_id=1, source_target_pairs={{0,16},{8,24},{16,0},{24,8},{1,17},{9,25},{17,1},{25,9},{2,18},{10... | collective-permute-start | bytes 2064392 | tf_op jit(solution)/shard_map/cond/branch_2_fun/ppermute | solution.py:600
  84.9 21.6 %collective-permute-start.35 = (f32[576,384]{1,0:T(8,128)S(1)}, f32[576,384]{1,0:T(8,128)S(1)}, u32[]{:S(2)}, u32[]{:S(2)}) collective-permute-start(f32[576,384]{1,0:T(8,128)S(1)} %collective-permute-done.34.refs_0_), channel_id=1, source_target_pairs={{0,8},{8,0},{16,24},{24,16},{1,9},{9,1},{17,25},{25,17},{2,10},{10... | collective-permute-start | bytes 2654216 | tf_op jit(solution)/shard_map/cond/branch_2_fun/ppermute | solution.py:606
  98.8 4.0 %collective-permute-start.38 = (f32[448,384]{1,0:T(8,128)S(1)}, f32[448,384]{1,0:T(8,128)S(1)}, u32[]{:S(2)}, u32[]{:S(2)}) collective-permute-start(f32[448,384]{1,0:T(8,128)S(1)} %collective-permute-done.37.refs_5_), channel_id=1, source_target_pairs={{0,8},{8,0},{16,24},{24,16},{1,9},{9,1},{17,25},{25,17},{2,10},{10... | collective-permute-start | bytes 2064392 | tf_op jit(solution)/shard_map/cond/branch_2_fun/ppermute | solution.py:606
  98.8 3.0 %collective-permute-start.33 = (f32[36,16,256]{2,1,0:T(8,128)S(1)}, f32[36,16,256]{2,1,0:T(8,128)S(1)}, u32[]{:S(2)}, u32[]{:S(2)}) collective-permute-start(f32[36,16,256]{2,1,0:T(8,128)S(1)} %get-tuple-element.138.refs_0_.mine), channel_id=1, source_target_pairs={{0,8},{8,0},{16,24},{24,16},{1,9},{9,1},{17,25},{25,17},{2,10},{10... | collective-permute-start | bytes 1769480 | tf_op jit(solution)/shard_map/cond/branch_2_fun/ppermute | solution.py:601
  99.3 3.5 %collective-permute-start.36 = (f32[28,16,256]{2,1,0:T(8,128)S(1)}, f32[28,16,256]{2,1,0:T(8,128)S(1)}, u32[]{:S(2)}, u32[]{:S(2)}) collective-permute-start(f32[28,16,256]{2,1,0:T(8,128)S(1)} %get-tuple-element.131.mine.refs_0_), channel_id=1, source_target_pairs={{0,8},{8,0},{16,24},{24,16},{1,9},{9,1},{17,25},{25,17},{2,10},{10... | collective-permute-start | bytes 1376264 | tf_op jit(solution)/shard_map/cond/branch_2_fun/ppermute | solution.py:601

commit v4 on v3

--- a/solution.py
+++ b/solution.py
@@ -290,8 +290,8 @@
 
 def chunk_plans(long, cap, flat):
     halo = SECTIONS
-    share = 7 if 2 * cap <= 3 * flat else 6
-    first = share * (long // 16)
+    share = 13 if 2 * cap <= flat else 14 if 2 * cap <= 3 * flat else 12
+    first = share * (long // 32)
     side = (long - first) // 2
     wide = first + 2 * halo
     piece = side + 2 * halo
@@ -364,18 +364,16 @@
         value = value + dif[1] * ahead + (dif[1] + cou[1]) * behind
         return value + inner.reshape(step, depth, flat)
 
-    step = (plan["piece"] - 2) // 2
-    shift = plan["pieces"]
+    step = (plan["piece"] - 2) * plan["pieces"] // 2
+    apart = plan["piece"] if plan["pieces"] == 2 else step
 
     def body(i, carry):
-        which = jnp.bitwise_and(jnp.right_shift(i, shift), 1)
-        at = 1 + step * jnp.bitwise_and(i, 1)
-        if plan["pieces"] == 2:
-            at = at + plan["piece"] * jnp.bitwise_and(jnp.right_shift(i, 1), 1)
+        which = jnp.bitwise_and(jnp.right_shift(i, 1), 1)
+        at = 1 + apart * jnp.bitwise_and(i, 1)
         state[1 - which, pl.ds(at, step)] = block(which, at, tall, step)
         return carry
 
-    lax.fori_loop(0, 2 * plan["pieces"] * (SECTIONS - 1), body, 0)
+    lax.fori_loop(0, 2 * (SECTIONS - 1), body, 0)
     last = keep.shape[0] // 2
     for side, out in enumerate((keep, give)):
         base = halo + plan["pitch"] * jnp.bitwise_xor(core[0], side)

time: 109 us -> 108 us (level)
  no operation moved by 1% of the time
where the time goes in v4:
time: 108 us
  waiting for transfers between devices  62.6 us (58%)
  Pallas kernels  30.2 us (28%)
  starting transfers between devices  13.4 us (12%)
    ppermute x2, waiting for transfers between devices, send(): near.append(lax.ppermute(message, 'comp', shift))  34.4 us
    pallas_call x2, Pallas kernels, stencil(): pl.pallas_call(lambda *refs: stencil_kernel(plan, order, *refs), out_shap...  17 us
    ppermute x1, waiting for transfers between devices, run(): low_two = lax.ppermute(low_two, 'gy', forward['gy'])  7.21 us
    ppermute x1, waiting for transfers between devices, run(): lax.ppermute(jnp.concatenate([last_rows, first_rows]), 'gx', forward['gx'])  4.4 us
    ppermute x1, waiting for transfers between devices, run(): lax.ppermute(high_one, 'gy', backward['gy'])  4.16 us
    ppermute x1, waiting for transfers between devices, run(): high_two = lax.ppermute(high_two, 'gy', backward['gy'])  4.03 us
    ppermute x1, waiting for transfers between devices, run(): lax.ppermute(low_one, 'gy', forward['gy'])  3.89 us
    pallas_call x1, Pallas kernels, setup_tables(): pl.pallas_call(lambda *refs: setup_kernel(flat, chips, *refs), out_shape=...  3.12 us
  transfers between devices with their start and end apart: 13, of which 9 were waited for; matrix products, arithmetic and copies ran while one was open for 0% of the time, Pallas kernels for 8%

profile of v4, /device:TPU:0, one launch (start us, length us, event | category | flops | bytes accessed | tf_op | source)
XLA Modules:
  0.0 107.8 jit_solution(17118223788406964089)
XLA Ops:
  0.0 1.2 %room.1 = s32[1]{0:T(128)} custom-call(s32[4]{0:T(128)} %levels.1), custom_call_target="tpu_custom_call" | custom-call | tf_op jit(solution)/shard_map/room/pallas_call | solution.py:235
  1.9 105.7 %conditional.1 = (f32[1,128,16,256]{3,2,1,0:T(8,128)}) conditional(s32[]{:T(128)} %bitcast.20, (s32[]{:T(128)}, f32[2,4]{1,0:T(2,128)}, s32[4]{0:T(128)}, s32[4]{0:T(128)}, f32[1,128,16,256]{3,2,1,0:T(8,128)}, /*index=5*/f32[1]{0:T(128)}) %tuple.29, (s32[]{:T(128)}, f32[2,4]{1,0:T(2,128)}, s32[4]{0:T(128)}, ...), branch_computations={%region_0.0_spmd, %region_1.0_spmd, %region_2.0_spmd, %region_3.0_... | conditional | flops 32769 | bytes 39060428 | solution.py:546
  2.2 1.4 %faces.6 = (f32[64,4,256]{2,1,0:T(4,128)S(1)}, f32[64,4,256]{2,1,0:T(4,128)S(1)}) custom-call(f32[128,16,256]{2,1,0:T(8,128)} %bitcast.37), custom_call_target="tpu_custom_call" | custom-call | tf_op jit(solution)/shard_map/cond/branch_2_fun/faces/pallas_call | solution.py:257
  3.6 3.1 %collective-permute-start.26 = (f32[64,4,256]{2,1,0:T(4,128)S(1)}, f32[64,4,256]{2,1,0:T(4,128)S(1)}, u32[]{:S(2)}, u32[]{:S(2)}) collective-permute-start(f32[64,4,256]{2,1,0:T(4,128)S(1)} %get-tuple-element.129), channel_id=1, source_target_pairs={{0,1},{1,2},{2,3},{3,0},{4,5},{5,6},{6,7},{7,4},{8,9},{9,10},{10,1... | collective-permute-start | bytes 786440 | tf_op jit(solution)/shard_map/cond/branch_2_fun/ppermute | solution.py:570
  6.7 2.1 %collective-permute-start.27 = (f32[64,4,256]{2,1,0:T(4,128)S(1)}, f32[64,4,256]{2,1,0:T(4,128)S(1)}, u32[]{:S(2)}, u32[]{:S(2)}) collective-permute-start(f32[64,4,256]{2,1,0:T(4,128)S(1)} %get-tuple-element.130), channel_id=1, source_target_pairs={{0,3},{1,0},{2,1},{3,2},{4,7},{5,4},{6,5},{7,6},{8,11},{9,8},{10,9... | collective-permute-start | bytes 786440 | tf_op jit(solution)/shard_map/cond/branch_2_fun/ppermute | solution.py:571
  8.9 3.1 %tables.6 = (bf16[256,256]{1,0:T(8,128)(2,1)S(1)}, bf16[256,256]{1,0:T(8,128)(2,1)S(1)}, bf16[256,256]{1,0:T(8,128)(2,1)S(1)}, bf16[256,512]{1,0:T(8,128)(2,1)S(...) custom-call(s32[1]{0:T(128)} %bitcast.10.refs_0_.place, s32[4]{0:T(128)S(1)} %copy-done.10, ...), custom_call_target="tpu_custom_call" | custom-call | tf_op jit(solution)/shard_map/cond/branch_2_fun/tables/pallas_call | solution.py:214
  12.1 3.9 %collective-permute-done.26.refs_8_ = f32[64,4,256]{2,1,0:T(4,128)S(1)} collective-permute-done((f32[64,4,256]{2,1,0:T(4,128)S(1)}, f32[64,4,256]{2,1,0:T(4,128)S(1)}, u32[]{:S(2)}, u32[]{:S(2)}) %collective-permute-start.26) | collective-permute-done | bytes 262176 | tf_op jit(solution)/shard_map/cond/branch_2_fun/ppermute | solution.py:570
  15.9 4.2 %collective-permute-done.27.refs_9_ = f32[64,4,256]{2,1,0:T(4,128)S(1)} collective-permute-done((f32[64,4,256]{2,1,0:T(4,128)S(1)}, f32[64,4,256]{2,1,0:T(4,128)S(1)}, u32[]{:S(2)}, u32[]{:S(2)}) %collective-permute-start.27) | collective-permute-done | bytes 262176 | tf_op jit(solution)/shard_map/cond/branch_2_fun/ppermute | solution.py:571
  20.1 7.5 %sections.12 = (f32[28,16,256]{2,1,0:T(8,128)S(1)}, f32[28,16,256]{2,1,0:T(8,128)S(1)}) custom-call(s32[1]{0:T(128)} %bitcast.10.refs_0_.place, s32[1]{0:T(128)S(6)} %and.11.refs_1_.core, s32[4]{0:T(128)S(1)} %copy-done.10, f32[8]{0:T(128)S(1)} %reshape.34.refs_3_, f32[1]{0:T(128)} %get-tuple-element.198.refs_4_, f32[128,16,256]{2,1,0:T(8,128)S(1)} %bitcast.38, ...), custom_call_target="tpu_custom_call" | custom-call | tf_op jit(solution)/shard_map/cond/branch_2_fun/sections/pallas_call | solution.py:395
  27.7 1.6 %collective-permute-start.29 = (f32[8,16,256]{2,1,0:T(8,128)S(1)}, f32[8,16,256]{2,1,0:T(8,128)S(1)}, u32[]{:S(2)}, u32[]{:S(2)}) collective-permute-start(f32[8,16,256]{2,1,0:T(8,128)S(1)} %pad_maximum_fusion.2), channel_id=1, source_target_pairs={{0,4},{4,0},{1,5},{5,1},{2,6},{6,2},{3,7},{7,3},{8,12},{12,8},{9,1... | collective-permute-start | bytes 393224 | tf_op jit(solution)/shard_map/cond/branch_2_fun/ppermute | solution.py:575
  29.2 4.4 %collective-permute-done.29.ends.refs_12_ = f32[8,16,256]{2,1,0:T(8,128)S(1)} collective-permute-done((f32[8,16,256]{2,1,0:T(8,128)S(1)}, f32[8,16,256]{2,1,0:T(8,128)S(1)}, u32[]{:S(2)}, u32[]{:S(2)}) %collective-permute-start.29) | collective-permute-done | bytes 131104 | tf_op jit(solution)/shard_map/cond/branch_2_fun/ppermute | solution.py:575
  33.7 1.2 %collective-permute-start.30 = (f32[72,4,256]{2,1,0:T(4,128)S(1)}, f32[72,4,256]{2,1,0:T(4,128)S(1)}, u32[]{:S(2)}, u32[]{:S(2)}) collective-permute-start(f32[72,4,256]{2,1,0:T(4,128)S(1)} %get-tuple-element.136), channel_id=1, source_target_pairs={{0,1},{1,2},{2,3},{3,0},{4,5},{5,6},{6,7},{7,4},{8,9},{9,10},{10,1... | collective-permute-start | bytes 884744 | tf_op jit(solution)/shard_map/cond/branch_2_fun/ppermute | solution.py:585
  34.9 2.7 %collective-permute-start.31 = (f32[72,4,256]{2,1,0:T(4,128)S(1)}, f32[72,4,256]{2,1,0:T(4,128)S(1)}, u32[]{:S(2)}, u32[]{:S(2)}) collective-permute-start(f32[72,4,256]{2,1,0:T(4,128)S(1)} %get-tuple-element.137), channel_id=1, source_target_pairs={{0,3},{1,0},{2,1},{3,2},{4,7},{5,4},{6,5},{7,6},{8,11},{9,8},{10,9... | collective-permute-start | bytes 884744 | tf_op jit(solution)/shard_map/cond/branch_2_fun/ppermute | solution.py:586
  38.2 7.2 %collective-permute-done.30.refs_10_ = f32[72,4,256]{2,1,0:T(4,128)S(1)} collective-permute-done((f32[72,4,256]{2,1,0:T(4,128)S(1)}, f32[72,4,256]{2,1,0:T(4,128)S(1)}, u32[]{:S(2)}, u32[]{:S(2)}) %collective-permute-start.30) | collective-permute-done | bytes 294944 | tf_op jit(solution)/shard_map/cond/branch_2_fun/ppermute | solution.py:585
  45.4 4.0 %collective-permute-done.31.refs_11_ = f32[72,4,256]{2,1,0:T(4,128)S(1)} collective-permute-done((f32[72,4,256]{2,1,0:T(4,128)S(1)}, f32[72,4,256]{2,1,0:T(4,128)S(1)}, u32[]{:S(2)}, u32[]{:S(2)}) %collective-permute-start.31) | collective-permute-done | bytes 294944 | tf_op jit(solution)/shard_map/cond/branch_2_fun/ppermute | solution.py:586
  49.5 9.5 %sections.13 = (f32[36,16,256]{2,1,0:T(8,128)S(1)}, f32[36,16,256]{2,1,0:T(8,128)S(1)}) custom-call(s32[1]{0:T(128)} %bitcast.10.refs_0_.place, s32[1]{0:T(128)S(6)} %and.11.refs_1_.core, s32[4]{0:T(128)S(1)} %copy-done.10, f32[8]{0:T(128)S(1)} %reshape.34.refs_3_, f32[1]{0:T(128)} %get-tuple-element.198.refs_4_, f32[128,16,256]{2,1,0:T(8,128)S(1)} %bitcast.40, ...), custom_call_target="tpu_custom_call" | custom-call | tf_op jit(solution)/shard_map/cond/branch_2_fun/sections/pallas_call | solution.py:395
  59.0 2.0 %collective-permute-done.32.refs_2_.other = f32[36,16,256]{2,1,0:T(8,128)S(1)} collective-permute-done((f32[36,16,256]{2,1,0:T(8,128)S(1)}, f32[36,16,256]{2,1,0:T(8,128)S(1)}, u32[]{:S(2)}, u32[]{:S(2)}) %collective-permute-start.32) | collective-permute-done | bytes 589856 | tf_op jit(solution)/shard_map/cond/branch_2_fun/ppermute | solution.py:592
  61.8 1.6 %collective-permute-start.34 = (f32[576,384]{1,0:T(8,128)S(1)}, f32[576,384]{1,0:T(8,128)S(1)}, u32[]{:S(2)}, u32[]{:S(2)}) collective-permute-start(f32[576,384]{1,0:T(8,128)S(1)} %pack.13), channel_id=1, source_target_pairs={{0,16},{8,24},{16,0},{24,8},{1,17},{9,25},{17,1},{25,9},{2,18},{10... | collective-permute-start | bytes 2654216 | tf_op jit(solution)/shard_map/cond/branch_2_fun/ppermute | solution.py:598
  63.9 20.5 %collective-permute-done.34.refs_0_ = f32[576,384]{1,0:T(8,128)S(1)} collective-permute-done((f32[576,384]{1,0:T(8,128)S(1)}, f32[576,384]{1,0:T(8,128)S(1)}, u32[]{:S(2)}, u32[]{:S(2)}) %collective-permute-start.34) | collective-permute-done | bytes 884768 | tf_op jit(solution)/shard_map/cond/branch_2_fun/ppermute | solution.py:598
  84.4 13.9 %collective-permute-done.37.refs_5_ = f32[448,384]{1,0:T(8,128)S(1)} collective-permute-done((f32[448,384]{1,0:T(8,128)S(1)}, f32[448,384]{1,0:T(8,128)S(1)}, u32[]{:S(2)}, u32[]{:S(2)}) %collective-permute-start.37) | collective-permute-done | bytes 688160 | tf_op jit(solution)/shard_map/cond/branch_2_fun/ppermute | solution.py:598
  98.8 2.5 %collective-permute-done.33.refs_3_ = f32[36,16,256]{2,1,0:T(8,128)S(1)} collective-permute-done((f32[36,16,256]{2,1,0:T(8,128)S(1)}, f32[36,16,256]{2,1,0:T(8,128)S(1)}, u32[]{:S(2)}, u32[]{:S(2)}) %collective-permute-start.33) | collective-permute-done | bytes 589856 | tf_op jit(solution)/shard_map/cond/branch_2_fun/ppermute | solution.py:599
  102.3 2.4 %finish.6.refs_2_ = f32[128,16,256]{2,1,0:T(8,128)} custom-call(s32[1]{0:T(128)S(6)} %and.11.refs_1_.core, s32[1]{0:T(128)} %bitcast.10.refs_0_.place, s32[4]{0:T(128)S(1)} %copy-done.6, f32[28,16,256]{2,1,0:T(8,128)S(1)} %get-tuple-element.131.mine.refs_0_, f32[28,16,256]{2,1,0:T(8,128)S(1)} %get-tuple-element.132.refs_1_, ...), custom_call_target="tpu_custom_call" | custom-call | tf_op jit(solution)/shard_map/cond/branch_2_fun/finish/pallas_call | solution.py:481
  104.7 1.3 %add_messages.12.refs_2_ = f32[128,16,256]{2,1,0:T(8,128)} custom-call(s32[1]{0:T(128)S(6)} %and.11.refs_1_.core, f32[36,16,256]{2,1,0:T(8,128)S(1)} %get-tuple-element.142.current, f32[576,384]{1,0:T(8,128)S(1)} %collective-permute-done.34.refs_0_, bf16[512,256]{1,0:T(8,128)(2,1)S(1)} %get-tuple-element.141.refs_7_.refs_1_, ...), custom_call_target="tpu_custom_call", output_to_operand_aliasing={{}: (4, {})} | custom-call | tf_op jit(solution)/shard_map/cond/branch_2_fun/add_messages/pallas_call | solution.py:524
  106.0 1.3 %add_messages.13 = f32[128,16,256]{2,1,0:T(8,128)} custom-call(s32[1]{0:T(128)S(6)} %and.11.refs_1_.core, f32[36,16,256]{2,1,0:T(8,128)S(1)} %get-tuple-element.140.current, f32[576,384]{1,0:T(8,128)S(1)} %collective-permute-done.35.refs_0_, bf16[512,256]{1,0:T(8,128)(2,1)S(1)} %get-tuple-element.141.refs_7_.refs_1_, ...), custom_call_target="tpu_custom_call", output_to_operand_aliasing={{}: (4, {})} | custom-call | tf_op jit(solution)/shard_map/cond/branch_2_fun/add_messages/pallas_call | solution.py:524
  (26 shorter events, 3.8 us)
Async XLA Ops:
  2.1 6.7 %copy-start.14 = (f32[2,4]{1,0:T(2,128)S(1)}, f32[2,4]{1,0:T(2,128)}, u32[]{:S(2)}) copy-start(f32[2,4]{1,0:T(2,128)} %get-tuple-element.186) | copy-start | bytes 100 | tf_op jit(solution)/shard_map/cond
  2.2 6.7 %copy-start.6 = (s32[4]{0:T(128)S(1)}, s32[4]{0:T(128)}, u32[]{:S(2)}) copy-start(s32[4]{0:T(128)} %get-tuple-element.190.refs_2_.weights) | copy-start | bytes 52 | tf_op jit(solution)/shard_map/cond
  2.2 6.7 %copy-start.10 = (s32[4]{0:T(128)S(1)}, s32[4]{0:T(128)}, u32[]{:S(2)}) copy-start(s32[4]{0:T(128)} %get-tuple-element.121.refs_1_.refs_2_) | copy-start | bytes 52 | tf_op jit(solution)/shard_map/cond
  2.2 9.9 %copy-start.2 = (f32[1,128,16,256]{3,2,1,0:T(8,128)S(1)}, f32[1,128,16,256]{3,2,1,0:T(8,128)}, u32[]{:S(2)}) copy-start(f32[1,128,16,256]{3,2,1,0:T(8,128)} %get-tuple-element.194) | copy-start | bytes 6291460 | tf_op jit(solution)/shard_map/cond
  3.6 12.3 %collective-permute-start.26 = (f32[64,4,256]{2,1,0:T(4,128)S(1)}, f32[64,4,256]{2,1,0:T(4,128)S(1)}, u32[]{:S(2)}, u32[]{:S(2)}) collective-permute-start(f32[64,4,256]{2,1,0:T(4,128)S(1)} %get-tuple-element.129), channel_id=1, source_target_pairs={{0,1},{1,2},{2,3},{3,0},{4,5},{5,6},{6,7},{7,4},{8,9},{9,10},{10,1... | collective-permute-start | bytes 786440 | tf_op jit(solution)/shard_map/cond/branch_2_fun/ppermute | solution.py:570
  6.7 13.4 %collective-permute-start.27 = (f32[64,4,256]{2,1,0:T(4,128)S(1)}, f32[64,4,256]{2,1,0:T(4,128)S(1)}, u32[]{:S(2)}, u32[]{:S(2)}) collective-permute-start(f32[64,4,256]{2,1,0:T(4,128)S(1)} %get-tuple-element.130), channel_id=1, source_target_pairs={{0,3},{1,0},{2,1},{3,2},{4,7},{5,4},{6,5},{7,6},{8,11},{9,8},{10,9... | collective-permute-start | bytes 786440 | tf_op jit(solution)/shard_map/cond/branch_2_fun/ppermute | solution.py:571
  27.6 10.0 %collective-permute-start.28 = (f32[28,16,256]{2,1,0:T(8,128)S(1)}, f32[28,16,256]{2,1,0:T(8,128)S(1)}, u32[]{:S(2)}, u32[]{:S(2)}) collective-permute-start(f32[28,16,256]{2,1,0:T(8,128)S(1)} %get-tuple-element.132.refs_1_), channel_id=1, source_target_pairs={{0,8},{8,0},{16,24},{24,16},{1,9},{9,1},{17,25},{25,17},{2,10},{10... | collective-permute-start | bytes 1376264 | tf_op jit(solution)/shard_map/cond/branch_2_fun/ppermute | solution.py:592
  27.7 6.0 %collective-permute-start.29 = (f32[8,16,256]{2,1,0:T(8,128)S(1)}, f32[8,16,256]{2,1,0:T(8,128)S(1)}, u32[]{:S(2)}, u32[]{:S(2)}) collective-permute-start(f32[8,16,256]{2,1,0:T(8,128)S(1)} %pad_maximum_fusion.2), channel_id=1, source_target_pairs={{0,4},{4,0},{1,5},{5,1},{2,6},{6,2},{3,7},{7,3},{8,12},{12,8},{9,1... | collective-permute-start | bytes 393224 | tf_op jit(solution)/shard_map/cond/branch_2_fun/ppermute | solution.py:575
  33.7 11.7 %collective-permute-start.30 = (f32[72,4,256]{2,1,0:T(4,128)S(1)}, f32[72,4,256]{2,1,0:T(4,128)S(1)}, u32[]{:S(2)}, u32[]{:S(2)}) collective-permute-start(f32[72,4,256]{2,1,0:T(4,128)S(1)} %get-tuple-element.136), channel_id=1, source_target_pairs={{0,1},{1,2},{2,3},{3,0},{4,5},{5,6},{6,7},{7,4},{8,9},{9,10},{10,1... | collective-permute-start | bytes 884744 | tf_op jit(solution)/shard_map/cond/branch_2_fun/ppermute | solution.py:585
  34.9 14.6 %collective-permute-start.31 = (f32[72,4,256]{2,1,0:T(4,128)S(1)}, f32[72,4,256]{2,1,0:T(4,128)S(1)}, u32[]{:S(2)}, u32[]{:S(2)}) collective-permute-start(f32[72,4,256]{2,1,0:T(4,128)S(1)} %get-tuple-element.137), channel_id=1, source_target_pairs={{0,3},{1,0},{2,1},{3,2},{4,7},{5,4},{6,5},{7,6},{8,11},{9,8},{10,9... | collective-permute-start | bytes 884744 | tf_op jit(solution)/shard_map/cond/branch_2_fun/ppermute | solution.py:586
  59.0 2.1 %collective-permute-start.32 = (f32[36,16,256]{2,1,0:T(8,128)S(1)}, f32[36,16,256]{2,1,0:T(8,128)S(1)}, u32[]{:S(2)}, u32[]{:S(2)}) collective-permute-start(f32[36,16,256]{2,1,0:T(8,128)S(1)} %get-tuple-element.139.refs_1_), channel_id=1, source_target_pairs={{0,8},{8,0},{16,24},{24,16},{1,9},{9,1},{17,25},{25,17},{2,10},{10... | collective-permute-start | bytes 1769480 | tf_op jit(solution)/shard_map/cond/branch_2_fun/ppermute | solution.py:592
  61.8 22.6 %collective-permute-start.34 = (f32[576,384]{1,0:T(8,128)S(1)}, f32[576,384]{1,0:T(8,128)S(1)}, u32[]{:S(2)}, u32[]{:S(2)}) collective-permute-start(f32[576,384]{1,0:T(8,128)S(1)} %pack.13), channel_id=1, source_target_pairs={{0,16},{8,24},{16,0},{24,8},{1,17},{9,25},{17,1},{25,9},{2,18},{10... | collective-permute-start | bytes 2654216 | tf_op jit(solution)/shard_map/cond/branch_2_fun/ppermute | solution.py:598
  63.4 34.9 %collective-permute-start.37 = (f32[448,384]{1,0:T(8,128)S(1)}, f32[448,384]{1,0:T(8,128)S(1)}, u32[]{:S(2)}, u32[]{:S(2)}) collective-permute-start(f32[448,384]{1,0:T(8,128)S(1)} %pack.12), channel_id=1, source_target_pairs={{0,16},{8,24},{16,0},{24,8},{1,17},{9,25},{17,1},{25,9},{2,18},{10... | collective-permute-start | bytes 2064392 | tf_op jit(solution)/shard_map/cond/branch_2_fun/ppermute | solution.py:598
  84.4 21.6 %collective-permute-start.35 = (f32[576,384]{1,0:T(8,128)S(1)}, f32[576,384]{1,0:T(8,128)S(1)}, u32[]{:S(2)}, u32[]{:S(2)}) collective-permute-start(f32[576,384]{1,0:T(8,128)S(1)} %collective-permute-done.34.refs_0_), channel_id=1, source_target_pairs={{0,8},{8,0},{16,24},{24,16},{1,9},{9,1},{17,25},{25,17},{2,10},{10... | collective-permute-start | bytes 2654216 | tf_op jit(solution)/shard_map/cond/branch_2_fun/ppermute | solution.py:604
  98.3 4.0 %collective-permute-start.38 = (f32[448,384]{1,0:T(8,128)S(1)}, f32[448,384]{1,0:T(8,128)S(1)}, u32[]{:S(2)}, u32[]{:S(2)}) collective-permute-start(f32[448,384]{1,0:T(8,128)S(1)} %collective-permute-done.37.refs_5_), channel_id=1, source_target_pairs={{0,8},{8,0},{16,24},{24,16},{1,9},{9,1},{17,25},{25,17},{2,10},{10... | collective-permute-start | bytes 2064392 | tf_op jit(solution)/shard_map/cond/branch_2_fun/ppermute | solution.py:604
  98.3 3.0 %collective-permute-start.33 = (f32[36,16,256]{2,1,0:T(8,128)S(1)}, f32[36,16,256]{2,1,0:T(8,128)S(1)}, u32[]{:S(2)}, u32[]{:S(2)}) collective-permute-start(f32[36,16,256]{2,1,0:T(8,128)S(1)} %get-tuple-element.138.refs_0_.mine), channel_id=1, source_target_pairs={{0,8},{8,0},{16,24},{24,16},{1,9},{9,1},{17,25},{25,17},{2,10},{10... | collective-permute-start | bytes 1769480 | tf_op jit(solution)/shard_map/cond/branch_2_fun/ppermute | solution.py:599
  98.8 3.5 %collective-permute-start.36 = (f32[28,16,256]{2,1,0:T(8,128)S(1)}, f32[28,16,256]{2,1,0:T(8,128)S(1)}, u32[]{:S(2)}, u32[]{:S(2)}) collective-permute-start(f32[28,16,256]{2,1,0:T(8,128)S(1)} %get-tuple-element.131.mine.refs_0_), channel_id=1, source_target_pairs={{0,8},{8,0},{16,24},{24,16},{1,9},{9,1},{17,25},{25,17},{2,10},{10... | collective-permute-start | bytes 1376264 | tf_op jit(solution)/shard_map/cond/branch_2_fun/ppermute | solution.py:599
